TPU v7x, 32 devices: a whole 2x2x4 slice. The times are simulated.
32 devices in a mesh: gx: 4 (over z), gy: 8 (over y, x, core).
Axes of the slice: x: 2, y: 2, z: 4, core: 2. Of those that a mesh axis runs over, the one named last changes fastest.
Arguments:
- forcing: float32 [16, 128, 512], P(None, 'gy', 'gx'), may hold values from -6 to 6
- pressure_in: float32 [16, 128, 512], P(None, 'gy', 'gx'), may hold values from -6 to 6
- x_coupling: float32 [16, 128, 512], P(None, 'gy', 'gx'), may hold values from 0.5 to 2000
- y_coupling: float32 [16, 128, 512], P(None, 'gy', 'gx'), may hold values from 0.5 to 2000
- z_coupling: float32 [16, 128, 512], P(None, 'gy', 'gx'), may hold values from 0.05 to 0.5
- damping: float32 [16, 128, 512], P(None, 'gy', 'gx'), may hold values from 0.2 to 2
Outputs:
- pressure: float32 [16, 128, 512], P(None, 'gy', 'gx')
- coarse_residual: float32 [8, 64, 256], P(None, 'gy', 'gx')
- coarse_correction: float32 [8, 64, 256], P(None, 'gy')
All inputs are finite; a program needn't handle non-finite values.
Results may differ from a plain program's by a relative error of at most 0.0001.
Values sent between devices are 32-bit elements; how exact they have to be, the bound alone decides.
A program may use at most 128 MiB of HBM per device.

v0:
```python
import functools

import jax
import jax.numpy as jnp
from jax import lax
from jax.experimental import pallas as pl
from jax.experimental.pallas import tpu as pltpu
from jax.sharding import PartitionSpec as P

COARSE = 3
RELAX = 0.8
CH = 16
CH2 = 4
MESH = pl.DeviceIdType.MESH


def up(v, s, fill):
    return jnp.concatenate([jnp.full_like(v[:s], fill), v[:-s]], axis=0)


def down(v, s, fill):
    return jnp.concatenate([v[s:], jnp.full_like(v[:s], fill)], axis=0)


def strides_of(length):
    out, s = [], 1
    while s < length:
        out.append(s)
        s *= 2
    return out


class Comm:
    def __init__(self, send_sems):
        self.sems, self.used, self.pending = send_sems, 0, []

    def send(self, src, dst, recv, dev, cond=None):
        copy = pltpu.make_async_remote_copy(
            src_ref=src, dst_ref=dst, send_sem=self.sems.at[self.used], recv_sem=recv,
            device_id=dev, device_id_type=MESH,
        )
        self.used += 1
        self.pending.append((copy, cond))
        if cond is None:
            copy.start()
        else:
            pl.when(cond)(copy.start)

    def finish(self):
        for copy, cond in self.pending:
            if cond is None:
                copy.wait_send()
            else:
                pl.when(cond)(copy.wait_send)


def await_recv(src, dst, sems, recv, dev, cond=None):
    copy = pltpu.make_async_remote_copy(
        src_ref=src, dst_ref=dst, send_sem=sems.at[0], recv_sem=recv, device_id=dev, device_id_type=MESH
    )
    if cond is None:
        copy.wait_recv()
    else:
        pl.when(cond)(copy.wait_recv)


def interface_factor(n, me, ls, le, rs, re, own, tau, sig, bet, tau2, sig2, dlt, kk):
    beta = jnp.zeros_like(ls[0])
    for d in range(n):
        bet[d] = beta
        w = 1.0 / (1.0 - ls[d] * beta)
        t = le[d] * w
        tau[d] = t
        s = t * beta
        sig[d] = s
        beta = re[d] + s * rs[d]
    delta = jnp.zeros_like(ls[0])
    for d in reversed(range(n)):
        dlt[d] = delta
        w = 1.0 / (1.0 - re[d] * delta)
        t = rs[d] * w
        tau2[d] = t
        s = t * delta
        sig2[d] = s
        delta = ls[d] + s * le[d]
    ls_m, le_m, rs_m, re_m = own
    beta, delta = bet[me], dlt[me]
    a, b = 1.0 - beta * ls_m, 1.0 - delta * re_m
    o1, o2 = beta * rs_m, delta * le_m
    inv = 1.0 / (a * b - o1 * o2)
    kk[0], kk[1], kk[2], kk[3] = b * inv, o1 * inv, a * inv, o2 * inv
    kk[4], kk[5] = beta, delta


def interface_solve(n, me, h_left, h_right, gs, ge, tau, tau2, kk):
    alpha = jnp.zeros_like(gs)
    for d in range(n - 1):
        alpha = jnp.where(d < me, h_left(d) + tau[d] * alpha, alpha)
    gamma = jnp.zeros_like(gs)
    for d in reversed(range(1, n)):
        gamma = jnp.where(d > me, h_right(d) + tau2[d] * gamma, gamma)
    p = alpha + kk[4] * gs
    q = gamma + kk[5] * ge
    return kk[0] * p + kk[1] * q, kk[2] * q + kk[3] * p


def kernel(nx, ny, f_hbm, p_hbm, x_hbm, y_hbm, z_hbm, d_hbm, op_ref, or_ref, oc_ref,
           xl_s, xc_s, yl_s, yc_s, zl_s, zt_s, fo_s, p_s, ri_s, g_s, q_s, zds_s,
           lx_s, rx_s, wx_s, ly_s, ry_s, wy_s,
           sx0, sy0, hx, hyd, hyu, xb, sxb, ycb, syc, yb, shy,
           xtau, xsig, xbet, xtau2, xsig2, xdlt, xkk,
           ytau, ysig, ybet, ytau2, ysig2, ydlt, ykk,
           pair_s, cown, cbuf, rown, rbuf, fown, fbuf, flip,
           ssem, s0, sx, syco, sy, sc, sr, sf, ins, sin):
    Y, Z, X = xc_s.shape
    CY, CZ = Y // 2, Z // 2
    gx, gy = lax.axis_index("gx"), lax.axis_index("gy")
    has_w, has_e = gx > 0, gx < nx - 1
    has_n, has_s = gy > 0, gy < ny - 1
    west, east = jnp.maximum(gx - 1, 0), jnp.minimum(gx + 1, nx - 1)
    north, south = jnp.maximum(gy - 1, 0), jnp.minimum(gy + 1, ny - 1)
    x_peers = [lax.rem(gx + o, nx) for o in range(1, nx)]
    y_peers = [lax.rem(gy + o, ny) for o in range(1, ny)]

    loads = []
    for m, ref in enumerate((x_hbm, y_hbm, p_hbm, z_hbm, d_hbm, f_hbm)):
        loads.append(pltpu.make_async_copy(ref, ins.at[m], sin.at[m]))
        loads[m].start()
    x_ref, y_ref, p_ref, z_ref, d_ref, f_ref = [ins.at[m] for m in range(6)]

    barrier = pltpu.get_barrier_semaphore()

    def greet(dev):
        pl.semaphore_signal(barrier, inc=1, device_id=dev, device_id_type=MESH)

    for i in x_peers:
        greet((i, gy))
    for j in y_peers:
        greet((gx, j))

    corners = [
        (jnp.logical_and(h, v), (i, j)) for h, i in ((has_w, west), (has_e, east)) for v, j in ((has_n, north), (has_s, south))
    ]
    for cond, dev in corners:
        pl.when(cond)(functools.partial(greet, dev))

    lane = lax.broadcasted_iota(jnp.int32, (Z, X), 1)
    level = lax.broadcasted_iota(jnp.int32, (Z, X), 0)
    lane3 = lax.broadcasted_iota(jnp.int32, (1, 1, X), 2)

    def rows(ref, j):
        return ref[pl.ds(j, Z, stride=Y), :]

    packed = jnp.zeros((Z, X), jnp.float32)
    for m in range(3):
        loads[m].wait()
    for j in range(Y):
        v = rows(x_ref, j)
        xc_s[j] = v
        packed = jnp.where(lane == j, v[:, X - 1:], packed)
        yc_s[j] = rows(y_ref, j)
        p_s[j] = rows(p_ref, j)
    for m in range(3, 6):
        loads[m].wait()
    for j in range(Y):
        zv = jnp.where(level < Z - 1, rows(z_ref, j), 0.0)
        zt_s[j] = zv
        zl_s[j] = pltpu.roll(zv, 1, 0)
        fo_s[j] = rows(f_ref, j)
    sx0[...] = packed
    sy0[0] = yc_s[Y - 1]
    sy0[1] = p_s[Y - 1]
    sy0[2] = p_s[0]

    @pl.when(jnp.logical_not(has_w))
    def _():
        hx[...] = jnp.zeros_like(hx)
        cbuf[0] = jnp.zeros_like(cbuf[0])
        rbuf[0] = jnp.zeros_like(rbuf[0])

    @pl.when(jnp.logical_not(has_e))
    def _():
        cbuf[2] = jnp.zeros_like(cbuf[2])
        rbuf[2] = jnp.zeros_like(rbuf[2])

    @pl.when(jnp.logical_not(has_n))
    def _():
        hyd[...] = jnp.zeros_like(hyd)
        for d in range(3):
            cbuf[d, :, 0:3] = jnp.zeros_like(cbuf[d, :, 0:3])
            rbuf[d, 0:2] = jnp.zeros_like(rbuf[d, 0:2])

    @pl.when(jnp.logical_not(has_s))
    def _():
        hyu[...] = jnp.zeros_like(hyu)
        for d in range(3):
            cbuf[d, :, 3 + CY:] = jnp.zeros_like(cbuf[d, :, 3 + CY:])
            rbuf[d, 2 + CY:] = jnp.zeros_like(rbuf[d, 2 + CY:])

    n_corners = sum(cond.astype(jnp.int32) for cond, _ in corners)
    pl.semaphore_wait(barrier, (nx - 1) + (ny - 1) + n_corners)

    comm = Comm(ssem)
    comm.send(sx0, hx, s0.at[0], (east, gy), has_e)
    comm.send(sy0.at[0:2], hyd, s0.at[1], (gx, south), has_s)
    comm.send(sy0.at[2:3], hyu, s0.at[2], (gx, north), has_n)

    half = X // 2
    off = half // 2
    ii = lax.broadcasted_iota(jnp.int32, (X, X), 0)
    mm = lax.broadcasted_iota(jnp.int32, (X, X), 1)

    def selection(step, start):
        target = lax.rem((ii + (step + 2)) // 2 - 1 + start + X, X)
        return jnp.where(mm == target, 0.125, 0.0)

    def pairs(field):
        v = field.reshape(CY, 2, Z, X)
        pair_s[...] = (v[:, 0] + v[:, 1]).reshape(CY * Z, X)
        return pair_s[pl.ds(0, CY * CZ, stride=2), :] + pair_s[pl.ds(1, CY * CZ, stride=2), :]

    def mxu(a, b):
        return jnp.dot(a, b, precision=lax.Precision.HIGHEST, preferred_element_type=jnp.float32)

    here, there = selection(0, off), selection(0, half + off)
    sel2 = jnp.concatenate([here, there], axis=0)
    zfull = jnp.stack([rows(z_ref, j) for j in range(Y)])
    damp = jnp.stack([rows(d_ref, j) for j in range(Y)])
    for m, (u, v) in enumerate(((xc_s[...], yc_s[...]), (zfull, damp))):
        both_pairs = jnp.concatenate([pairs(u), pairs(v)], axis=1)
        cown[m] = mxu(both_pairs, sel2).reshape(CY, CZ, X)

    await_recv(sx0, hx, ssem, s0.at[0], (east, gy), has_w)
    await_recv(sy0.at[0:2], hyd, ssem, s0.at[1], (gx, south), has_n)
    await_recv(sy0.at[2:3], hyu, ssem, s0.at[2], (gx, north), has_s)

    xc, yc = xc_s[...], yc_s[...]
    border = jnp.stack([jnp.broadcast_to(hx[:, j:j + 1], (Z, X)) for j in range(Y)])
    xl = jnp.where(lane3 == 0, border, pltpu.roll(xc, 1, 2))
    xl_s[...] = xl
    yl = jnp.concatenate([hyd[0:1], yc[:-1]], axis=0)
    yl_s[...] = yl
    zd = zl_s[...] + zt_s[...] + damp
    xs, ys = xl + xc, yl + yc
    ri = 1.0 / (xs + ys + zd)
    ri_s[...] = ri

    a, c, e = yl * ri, yc * ri, (xs + zd) * ri
    for n, s in enumerate(strides_of(Y)):
        a2, c2 = a * up(a, s, 1.0), c * down(c, s, 1.0)
        e2 = e + a * up(e, s, 0.0) + c * down(e, s, 0.0)
        inv = 1.0 / (a2 + c2 + e2)
        wy_s[n, 0], wy_s[n, 1], wy_s[n, 2] = inv, a * inv, c * inv
        a, c, e = a2 * inv, c2 * inv, e2 * inv
    ly_s[...], ry_s[...] = a, c
    syc[0], syc[1], syc[2], syc[3] = a[0], a[Y - 1], c[0], c[Y - 1]
    ycb[gy] = syc[...]
    for j in y_peers:
        comm.send(syc, ycb.at[gy], syco.at[gy], (gx, j))

    def y_local(r):
        for n, s in enumerate(strides_of(Y)):
            r = wy_s[n, 0] * r + wy_s[n, 1] * up(r, s, 0.0) + wy_s[n, 2] * down(r, s, 0.0)
        return r

    def z_terms(v):
        return zl_s[...] * pltpu.roll(v, 1, 1) + zt_s[...] * pltpu.roll(v, Z - 1, 1)

    def x_source(v, above, below):
        lower = jnp.concatenate([above[None], v[:-1]], axis=0)
        upper = jnp.concatenate([v[1:], below[None]], axis=0)
        return (fo_s[...] + yl_s[...] * lower + yc_s[...] * upper + z_terms(v)) * ri_s[...]

    def pack_edges(into, at, v, start):
        for j in range(v.shape[0]):
            into = jnp.where(lane == start + at + j, v[j][:, 0:1], into)
            into = jnp.where(lane == start + at + Y + j, v[j][:, X - 1:], into)
        return into

    ones = jnp.ones((1, 1, X), jnp.float32)
    packed = jnp.zeros((Z, X), jnp.float32)
    zds_s[...] = (yl + yc + zd) * ri
    g_s[...] = x_source(p_s[...], hyd[1], hyu[0])
    for lo in range(0, Y, CH):
        part = slice(lo, lo + CH)
        a, c = xl_s[part] * ri_s[part], xc_s[part] * ri_s[part]
        e, r = zds_s[part], g_s[part]
        for n, s in enumerate(strides_of(X)):
            low, high = lane3 >= s, lane3 < X - s
            a_in, c_in = jnp.where(low, a, 0.0), jnp.where(high, c, 0.0)
            a2 = a * jnp.where(low, pltpu.roll(a, s, 2), ones)
            c2 = c * jnp.where(high, pltpu.roll(c, X - s, 2), ones)
            e2 = e + a_in * pltpu.roll(e, s, 2) + c_in * pltpu.roll(e, X - s, 2)
            inv = 1.0 / (a2 + c2 + e2)
            wa, wc = a_in * inv, c_in * inv
            wx_s[n, 0, part], wx_s[n, 1, part], wx_s[n, 2, part] = inv, wa, wc
            r = inv * r + wa * pltpu.roll(r, s, 2) + wc * pltpu.roll(r, X - s, 2)
            a, c, e = a2 * inv, c2 * inv, e2 * inv
        g_s[part], lx_s[part], rx_s[part] = r, a, c
        for q, v in enumerate((r, a, c)):
            packed = pack_edges(packed, lo, v, 2 * q * Y)

    def x_exchange(m, packed):
        sxb[m] = packed
        xb[m, gx] = packed
        for i in x_peers:
            comm.send(sxb.at[m], xb.at[m, gx], sx.at[m, gx], (i, gy))

    x_exchange(0, packed)

    def halo_exchange(src, dst, sems, top, lead, starting):
        def part(ref, lo, n):
            return ref.at[(slice(None),) * lead + (pl.ds(lo, n),)]

        def rows_of(slot):
            return dst.at[slot]

        for slot, i, ok, back in ((0, west, has_w, 2), (1, gx, None, 1), (2, east, has_e, 0)):
            both_ok = (lambda c: c) if ok is None else (lambda c, ok=ok: jnp.logical_and(c, ok))
            if starting:
                if ok is not None:
                    comm.send(src, part(rows_of(back), top, CY), sems.at[0, back], (i, gy), ok)
                comm.send(part(src, CY - top, top), part(rows_of(back), 0, top), sems.at[1, back], (i, south), both_ok(has_s))
                comm.send(part(src, 0, 2), part(rows_of(back), top + CY, 2), sems.at[2, back], (i, north), both_ok(has_n))
            else:
                if ok is not None:
                    await_recv(src, part(rows_of(slot), top, CY), ssem, sems.at[0, slot], (i, gy), ok)
                await_recv(part(src, CY - top, top), part(rows_of(slot), 0, top), ssem, sems.at[1, slot], (i, south), both_ok(has_n))
                await_recv(part(src, 0, 2), part(rows_of(slot), top + CY, 2), ssem, sems.at[2, slot], (i, north), both_ok(has_s))

    for m in range(2):
        cbuf[1, m, 3:3 + CY] = cown[m]
    halo_exchange(cown, cbuf, sc, 3, 1, True)

    for j in y_peers:
        await_recv(syc, ycb.at[j], ssem, syco.at[j], (gx, j))
    interface_factor(
        ny, gy, *[[ycb[d, m] for d in range(ny)] for m in range(4)], [syc[m] for m in range(4)],
        ytau, ysig, ybet, ytau2, ysig2, ydlt, ykk,
    )

    def slot(v, m):
        return v if m == 0 else pltpu.roll(v, X - m * Y, 1)

    def x_collect(m):
        for i in x_peers:
            await_recv(sxb.at[m], xb.at[m, i], ssem, sx.at[m, i], (i, gy))
        if m == 0:
            coefs = [[slot(xb[0, d], 2 + q) for d in range(nx)] for q in range(4)]
            own = [slot(sxb[0], 2 + q) for q in range(4)]
            interface_factor(nx, gx, *coefs, own, xtau, xsig, xbet, xtau2, xsig2, xdlt, xkk)
        gs = [xb[m, d] for d in range(nx)]
        ge = [slot(v, 1) for v in gs]
        return interface_solve(
            nx, gx, lambda d: ge[d] + xsig[d] * gs[d], lambda d: gs[d] + xsig2[d] * ge[d],
            sxb[m], slot(sxb[m], 1), xtau, xtau2, xkk,
        )

    def spread(v):
        return jnp.stack([jnp.broadcast_to(v[:, j:j + 1], (Z, X)) for j in range(Y)])

    def y_half(m):
        left, right = x_collect(m)
        left, right = spread(left), spread(right)
        v = g_s[...] + lx_s[...] * left + rx_s[...] * right
        q_s[...] = v
        before = jnp.where(lane3 == 0, left, pltpu.roll(v, 1, 2))
        after = jnp.where(lane3 == X - 1, right, pltpu.roll(v, X - 1, 2))
        r = (fo_s[...] + xl_s[...] * before + xc_s[...] * after + z_terms(v)) * ri_s[...]
        r = y_local(r)
        g_s[...] = r
        gs, ge = r[0], r[Y - 1]
        shy[m, 0] = ge + ysig[gy] * gs
        shy[m, 1] = gs + ysig2[gy] * ge
        yb[m, gy] = shy[m, 0]
        for j in y_peers:
            side = jnp.where(j > gy, 0, 1)
            comm.send(shy.at[m, side], yb.at[m, gy], sy.at[m, gy], (gx, j))
        for j in y_peers:
            await_recv(shy.at[m, 0], yb.at[m, j], ssem, sy.at[m, j], (gx, j))
        above, below = interface_solve(
            ny, gy, lambda d: yb[m, d], lambda d: yb[m, d], g_s[0], g_s[Y - 1], ytau, ytau2, ykk
        )
        return g_s[...] + ly_s[...] * above[None] + ry_s[...] * below[None], above, below

    v, above, below = y_half(0)
    g_s[...] = x_source(v, above, below)
    packed = jnp.zeros((Z, X), jnp.float32)
    for lo in range(0, Y, CH2):
        part = slice(lo, lo + CH2)
        r = g_s[part]
        for n, s in enumerate(strides_of(X)):
            r = wx_s[n, 0, part] * r + wx_s[n, 1, part] * pltpu.roll(r, s, 2) + wx_s[n, 2, part] * pltpu.roll(r, X - s, 2)
        g_s[part] = r
        packed = pack_edges(packed, lo, r, 0)
    x_exchange(1, packed)
    v, above, below = y_half(1)

    change = v - q_s[...]
    stacked = jnp.concatenate(
        [pairs(xc_s[...] * change), pairs(xl_s[...] * change), pairs(z_terms(change))], axis=1
    )
    sel3 = jnp.concatenate([selection(1, off), selection(-1, off), here], axis=0)
    partial = mxu(stacked, sel3).reshape(CY, CZ, X)
    rown[...] = partial
    rbuf[1, 2:2 + CY] = partial
    halo_exchange(rown, rbuf, sr, 2, 0, True)
    for j in range(Y):
        op_ref[pl.ds(j, Z, stride=Y), :] = v[j]

    halo_exchange(cown, cbuf, sc, 3, 1, False)

    centre = jnp.logical_and(lane3 >= off, lane3 < off + half)
    wide = lane3

    def planes(m):
        w, o, e = cbuf[0, m], cbuf[1, m], cbuf[2, m]
        near = jnp.where(centre, o, pltpu.roll(jnp.where(lane3 >= half, w, e), half, 2))
        far = jnp.where(centre, pltpu.roll(o, half, 2), jnp.where(lane3 < half, w, e))
        return near, far

    cx, cy = planes(0)
    cz, cd = planes(1)
    czl = lax.broadcasted_iota(jnp.int32, (1, CZ, 1), 1)
    H = CY + 4
    row = lax.broadcasted_iota(jnp.int32, (H, 1, 1), 0)
    inside = jnp.logical_and(
        jnp.logical_or(row >= 2, has_n), jnp.logical_or(row < 2 + CY, has_s)
    )
    inside = jnp.logical_and(
        inside,
        jnp.logical_and(jnp.logical_or(lane3 >= off, has_w), jnp.logical_or(lane3 < off + half, has_e)),
    )
    cyl, cy = cy[:H], cy[1:]
    cx, cz, cd = cx[1:], cz[1:], cd[1:]
    cd = jnp.where(inside, cd, 1.0)
    ct = jnp.where(czl < CZ - 1, cz, 0.0)
    cl = pltpu.roll(ct, 1, 1)
    cxl = pltpu.roll(cx, 1, 2)
    diag = cxl + cx + cyl + cy + cl + ct + cd
    scale = RELAX / diag

    halo_exchange(rown, rbuf, sr, 2, 0, False)
    w, e = pltpu.roll(rbuf[0], half, 2), pltpu.roll(rbuf[2], half, 2)
    res = (
        rbuf[1]
        + jnp.where(jnp.logical_and(lane3 >= off - 2, lane3 <= off), w, 0.0)
        + jnp.where(jnp.logical_and(lane3 >= off + half - 1, lane3 <= off + half + 1), e, 0.0)
    )
    res = jnp.where(inside, res, 0.0)
    cor = scale * res
    for repeat in range(COARSE - 1):
        lo, n = 1 + repeat, H - 2 - 2 * repeat
        cut = slice(lo, lo + n)
        mid, above, below = cor[1:-1], cor[:-2], cor[2:]
        applied = (
            diag[cut] * mid
            - cxl[cut] * pltpu.roll(mid, 1, 2)
            - cx[cut] * pltpu.roll(mid, X - 1, 2)
            - cyl[cut] * above
            - cy[cut] * below
            - cl[cut] * pltpu.roll(mid, 1, 1)
            - ct[cut] * pltpu.roll(mid, CZ - 1, 1)
        )
        cor = jnp.where(inside[cut], mid + scale[cut] * (res[cut] - applied), 0.0)
    hj = CY // 2
    mine = jnp.where(lane3 < half, pltpu.roll(cor[:hj], X - off, 2), pltpu.roll(cor[hj:], off, 2))
    fown[...] = mine
    fbuf[gx] = mine
    for i in x_peers:
        comm.send(fown, fbuf.at[gx], sf.at[gx], (i, gy))
    own = pltpu.roll(res[2:2 + CY], X - off, 2)
    for j in range(CY):
        flip[pl.ds(j, CZ, stride=CY), :] = own[j]
    or_ref[...] = flip[0:CZ * CY, :half]
    for i in x_peers:
        await_recv(fown, fbuf.at[i], ssem, sf.at[i], (i, gy))
    for t in range(nx // 2):
        u, v = fbuf[2 * t], fbuf[2 * t + 1]
        top = jnp.where(lane3 < half, u, pltpu.roll(v, half, 2))
        low = jnp.where(lane3 < half, pltpu.roll(u, half, 2), v)
        base = (t + 1) * CZ * CY
        for j in range(CY):
            flip[pl.ds(base + j, CZ, stride=CY), :] = top[j] if j < hj else low[j - hj]
        oc_ref[:, t * X:(t + 1) * X] = flip[base:base + CZ * CY, :]
    comm.finish()


def put(*refs):
    sems = refs[6]
    give = [pltpu.make_async_copy(refs[m], refs[3 + m], sems.at[m]) for m in range(3)]
    for copy in give:
        copy.start()
    for copy in give:
        copy.wait()


def body(nx, ny, *args):
    Z, Y, X = args[0].shape
    CZ, CY = Z // 2, Y // 2
    flat = [v.reshape(Z * Y, X) for v in args]
    f32 = jnp.float32

    def vm(*shape):
        return pltpu.VMEM(shape, f32)

    block = (Y, Z, X)
    nsx, nsy = len(strides_of(X)), len(strides_of(Y))
    tables_x = [vm(nx, Z, X) for _ in range(6)] + [vm(6, Z, X)]
    tables_y = [vm(ny, Z, X) for _ in range(6)] + [vm(6, Z, X)]
    sends = 3 + (ny - 1) * 3 + (nx - 1) * 3 + 8 * 2
    dma = pltpu.SemaphoreType.DMA
    scratch = (
        [vm(*block) for _ in range(12)]
        + [vm(*block), vm(*block), vm(nsx, 3, *block), vm(*block), vm(*block), vm(nsy, 3, *block)]
        + [vm(Z, X), vm(3, Z, X), vm(Z, X), vm(2, Z, X), vm(1, Z, X)]
        + [vm(2, nx, Z, X), vm(2, Z, X), vm(ny, 4, Z, X), vm(4, Z, X), vm(2, ny, Z, X), vm(2, 2, Z, X)]
        + tables_x + tables_y
        + [vm(CY * Z, X), vm(2, CY, CZ, X), vm(3, 2, CY + 5, CZ, X), vm(CY, CZ, X), vm(3, CY + 4, CZ, X),
           vm(CY // 2, CZ, X), vm(nx, CY // 2, CZ, X), vm((nx // 2 + 1) * CZ * CY, X)]
        + [dma((sends,)), dma((3,)), dma((2, nx)), dma((ny,)), dma((2, ny)), dma((3, 3)), dma((3, 3)), dma((nx,))]
        + [vm(6, Z * Y, X), dma((6,))]
    )
    p, r, c = pl.pallas_call(
        functools.partial(kernel, nx, ny),
        out_shape=(
            vm(Z * Y, X),
            vm(CZ * CY, X // 2),
            vm(CZ * CY, nx * X // 2),
        ),
        in_specs=[pl.BlockSpec(memory_space=pltpu.HBM)] * 6,
        out_specs=[pl.BlockSpec(memory_space=pltpu.VMEM)] * 3,
        scratch_shapes=scratch,
        compiler_params=pltpu.CompilerParams(
            collective_id=0, has_side_effects=True, vmem_limit_bytes=60000000
        ),
    )(*flat)
    p, r, c = pl.pallas_call(
        put,
        out_shape=tuple(jax.ShapeDtypeStruct(v.shape, f32) for v in (p, r, c)),
        in_specs=[pl.BlockSpec(memory_space=pltpu.VMEM)] * 3,
        out_specs=[pl.BlockSpec(memory_space=pltpu.HBM)] * 3,
        scratch_shapes=[dma((3,))],
    )(*[pltpu.with_memory_space_constraint(v, pltpu.VMEM) for v in (p, r, c)])
    return p.reshape(Z, Y, X), r.reshape(CZ, CY, X // 2), c.reshape(CZ, CY, nx * X // 2)


def solution(mesh):
    nx, ny = mesh.shape["gx"], mesh.shape["gy"]
    split = P(None, "gy", "gx")
    return jax.shard_map(
        functools.partial(body, nx, ny),
        mesh=mesh,
        in_specs=(split,) * 6,
        out_specs=(split, split, P(None, "gy", None)),
        check_vma=False,
    )
```

profile of v0, /device:TPU:0, one launch (start us, length us, event | category | flops | bytes accessed | tf_op | source)
XLA Modules:
  0.0 35.7 jit_solution(13714774745119394796)
XLA Ops:
  0.6 34.4 %shard_map.85 = (f32[256,128]{1,0:T(8,128)S(1)}, f32[64,64]{1,0:T(8,128)S(1)}, f32[64,256]{1,0:T(8,128)S(1)}) custom-call(f32[256,128]{1,0:T(8,128)} %bitcast.9, f32[256,128]{1,0:T(8,128)} %bitcast.10, f32[256,128]{1,0:T(8,128)} %bitcast.11, f32[256,128]{1,0:T(8,128)} %bitcast.12, f32[256,128]{1,0:T(8,128)} %bitcast.13, f32[256,128]{1,0:T(8,128)} %bitcast.14), custom_call_target="tpu_custom_call" | custom-call | tf_op jit(solution)/shard_map/pallas_call | solution.py:524
  35.0 0.7 %shard_map.86 = (f32[256,128]{1,0:T(8,128)}, f32[64,64]{1,0:T(8,128)}, f32[64,256]{1,0:T(8,128)}) custom-call(f32[256,128]{1,0:T(8,128)S(1)} %get-tuple-element.9.refs_0_, f32[64,64]{1,0:T(8,128)S(1)} %get-tuple-element.10.refs_1_, f32[64,256]{1,0:T(8,128)S(1)} %get-tuple-element.11.refs_2_), custom_call_target="tpu_custom_call" | custom-call | tf_op jit(solution)/shard_map/pallas_call | solution.py:538
where the time goes:
time: 35.9 us; the launch traced here: 35.7 us
  Pallas kernels  35.1 us (98%)
  between operations  0.64 us (2%)
    pallas_call x1, Pallas kernels, body(): pl.pallas_call(functools.partial(kernel, nx, ny), out_shape=(vm(Z * Y, X)...  34.4 us

commit v1 on v0

v1 whole, which is shorter than its diff:
```python
import functools

import jax
import jax.numpy as jnp
from jax import lax
from jax.experimental import pallas as pl
from jax.experimental.pallas import tpu as pltpu
from jax.sharding import PartitionSpec as P

COARSE = 3
RELAX = 0.8
CH = 4
LE, LS, RE, RS, GS, GE, XC = range(7)
SLOTS = 8
MESH = pl.DeviceIdType.MESH


def strides_of(length):
    out, s = [], 1
    while s < length:
        out.append(s)
        s *= 2
    return out


class Comm:
    def __init__(self, send_sems):
        self.sems, self.used, self.pending = send_sems, 0, []

    def send(self, src, dst, recv, dev, cond=None):
        copy = pltpu.make_async_remote_copy(
            src_ref=src, dst_ref=dst, send_sem=self.sems.at[self.used], recv_sem=recv,
            device_id=dev, device_id_type=MESH,
        )
        self.used += 1
        self.pending.append((copy, cond))
        if cond is None:
            copy.start()
        else:
            pl.when(cond)(copy.start)

    def finish(self):
        for copy, cond in self.pending:
            if cond is None:
                copy.wait_send()
            else:
                pl.when(cond)(copy.wait_send)


def await_recv(src, dst, sems, recv, dev, cond=None):
    copy = pltpu.make_async_remote_copy(
        src_ref=src, dst_ref=dst, send_sem=sems.at[0], recv_sem=recv, device_id=dev, device_id_type=MESH
    )
    if cond is None:
        copy.wait_recv()
    else:
        pl.when(cond)(copy.wait_recv)


def farthest_first(me, n):
    out = []
    for k in range(n - 1):
        down = jnp.where(n - 1 - k > me, n - 1 - k, n - 2 - k)
        up = jnp.where(k < me, k, k + 1)
        out.append(jnp.where(2 * me < n, down, up))
    return out


def flipped(me, n):
    if n & (n - 1):
        return [lax.rem(me + o, n) for o in range(1, n)]
    out = []
    for mask in range(n - 1, 0, -1):
        peer, bit = 0, 1
        while bit < n:
            value = lax.rem(me // bit, 2)
            peer = peer + bit * (1 - value if mask & bit else value)
            bit *= 2
        out.append(peer)
    return out


def interface_factor(n, me, ls, le, rs, re, own, tau, sig, bet, tau2, sig2, dlt, kk):
    beta = jnp.zeros_like(ls[0])
    for d in range(n):
        bet[d] = beta
        w = 1.0 / (1.0 - ls[d] * beta)
        t = le[d] * w
        tau[d] = t
        s = t * beta
        sig[d] = s
        beta = re[d] + s * rs[d]
    delta = jnp.zeros_like(ls[0])
    for d in reversed(range(n)):
        dlt[d] = delta
        w = 1.0 / (1.0 - re[d] * delta)
        t = rs[d] * w
        tau2[d] = t
        s = t * delta
        sig2[d] = s
        delta = ls[d] + s * le[d]
    ls_m, le_m, rs_m, re_m = own
    beta, delta = bet[me], dlt[me]
    a, b = 1.0 - beta * ls_m, 1.0 - delta * re_m
    o1, o2 = beta * rs_m, delta * le_m
    inv = 1.0 / (a * b - o1 * o2)
    kk[0], kk[1], kk[2], kk[3] = b * inv, o1 * inv, a * inv, o2 * inv
    kk[4], kk[5] = beta, delta


def interface_solve(n, me, h_left, h_right, gs, ge, tau, tau2, kk):
    alpha = jnp.zeros_like(gs)
    for d in range(n - 1):
        alpha = jnp.where(d < me, h_left(d) + tau[d] * alpha, alpha)
    gamma = jnp.zeros_like(gs)
    for d in reversed(range(1, n)):
        gamma = jnp.where(d > me, h_right(d) + tau2[d] * gamma, gamma)
    p = alpha + kk[4] * gs
    q = gamma + kk[5] * ge
    return kk[0] * p + kk[1] * q, kk[2] * q + kk[3] * p


def chain_factor(n, me, ls, le, rs, re, xc, own, rho, tau, sig, bet, tau2, sig2, scl, dlt, kk):
    one, zero = jnp.ones_like(ls[0]), jnp.zeros_like(ls[0])
    beta = zero
    for d in range(n):
        r = zero if d == 0 else xc[d - 1]
        b = one if d == 0 else 1.0 - r * (1.0 - beta)
        rho[d], bet[d] = r, b
        w = 1.0 / (1.0 - ls[d] * b)
        t = le[d] * w
        tau[d] = t * r
        s = t * b
        sig[d] = s
        beta = re[d] + s * rs[d]
    delta = zero
    for d in reversed(range(n)):
        dlt[d] = delta
        t = rs[d] / (1.0 - re[d] * delta)
        s = t * delta
        q = ls[d] + s * le[d]
        if d > 0:
            v = 1.0 / (1.0 - q + q * xc[d - 1])
            scl[d], tau2[d], sig2[d] = v, v * t, v * s
            delta = v * q * xc[d - 1]
        else:
            scl[d], tau2[d], sig2[d] = zero, zero, zero
    ls_m, le_m, rs_m, re_m = own
    beta, delta = bet[me], dlt[me]
    a, b = 1.0 - beta * ls_m, 1.0 - delta * re_m
    o1, o2 = beta * rs_m, delta * le_m
    inv = 1.0 / (a * b - o1 * o2)
    kk[0], kk[1], kk[2], kk[3] = b * inv, o1 * inv, a * inv, o2 * inv


def kernel(nx, ny, f_hbm, p_hbm, x_hbm, y_hbm, z_hbm, d_hbm, op_ref, or_ref, oc_ref,
           xl_s, xc_s, yl_s, yc_s, zl_s, zt_s, zd_s, fo_s, p_s, r_s, g_s, q_s,
           lx_s, rx_s, ix_s, wx_s, ly_s, ry_s, iy_s, wy_s,
           sx0, sy0, hx, hyd, hyu, xb, sxb, xb1, sx1, ycb, syc, yb, shy,
           xown, xrho, xtau, xsig, xbet, xtau2, xsig2, xscl, xdlt, xkk,
           ytau, ysig, ybet, ytau2, ysig2, ydlt, ykk, ysc,
           pair_s, cown, cbuf, rown, nbuf, ebuf, sedge, fown, fbuf, flip,
           ssem, s0, sx, syco, sy, sc, sr, sf, ins, sin):
    Y, Z, X = xc_s.shape
    CY, CZ = Y // 2, Z // 2
    f32 = jnp.float32
    gx, gy = lax.axis_index("gx"), lax.axis_index("gy")
    has_w, has_e = gx > 0, gx < nx - 1
    has_n, has_s = gy > 0, gy < ny - 1
    west, east = jnp.maximum(gx - 1, 0), jnp.minimum(gx + 1, nx - 1)
    north, south = jnp.maximum(gy - 1, 0), jnp.minimum(gy + 1, ny - 1)
    x_peers = farthest_first(gx, nx)
    y_peers = flipped(gy, ny)

    loads = []
    for m, ref in enumerate((x_hbm, y_hbm, p_hbm, z_hbm, d_hbm, f_hbm)):
        loads.append(pltpu.make_async_copy(ref, ins.at[m], sin.at[m]))
        loads[m].start()
    x_ref, y_ref, p_ref, z_ref, d_ref, f_ref = [ins.at[m] for m in range(6)]

    barrier = pltpu.get_barrier_semaphore()

    def greet(dev):
        pl.semaphore_signal(barrier, inc=1, device_id=dev, device_id_type=MESH)

    for i in x_peers:
        greet((i, gy))
    for j in y_peers:
        greet((gx, j))

    corners = [
        (jnp.logical_and(h, v), (i, j)) for h, i in ((has_w, west), (has_e, east)) for v, j in ((has_n, north), (has_s, south))
    ]
    for cond, dev in corners:
        pl.when(cond)(functools.partial(greet, dev))

    lane = lax.broadcasted_iota(jnp.int32, (Z, X), 1)
    level = lax.broadcasted_iota(jnp.int32, (Z, X), 0)
    lane3 = lax.broadcasted_iota(jnp.int32, (1, 1, X), 2)
    item, group = lane % SLOTS, lane // SLOTS

    def rows(ref, j):
        return ref[pl.ds(j, Z, stride=Y), :]

    for m in range(3):
        loads[m].wait()
    packed = jnp.zeros((Z, X), f32)
    for j in range(Y):
        v = rows(x_ref, j)
        xc_s[j] = v
        packed = jnp.where(lane == SLOTS * j + XC, v[:, X - 1:], packed)
    sx0[...] = packed
    sy0[0] = rows(y_ref, Y - 1)
    sy0[1] = rows(p_ref, Y - 1)
    sy0[2] = rows(p_ref, 0)

    n_corners = sum(cond.astype(jnp.int32) for cond, _ in corners)
    pl.semaphore_wait(barrier, (nx - 1) + (ny - 1) + n_corners)

    comm = Comm(ssem)
    comm.send(sy0.at[0:2], hyd, s0.at[1], (gx, south), has_s)
    comm.send(sy0.at[2:3], hyu, s0.at[2], (gx, north), has_n)
    comm.send(sx0, hx, s0.at[0], (east, gy), has_e)

    for j in range(Y):
        yc_s[j] = rows(y_ref, j)
        p_s[j] = rows(p_ref, j)
    for m in range(3, 6):
        loads[m].wait()
    for j in range(Y):
        zv = jnp.where(level < Z - 1, rows(z_ref, j), 0.0)
        zt_s[j] = zv
        zl = pltpu.roll(zv, 1, 0)
        zl_s[j] = zl
        zd_s[j] = zv + zl + rows(d_ref, j)
        fo_s[j] = rows(f_ref, j)

    first, last = lane3 == 0, lane3 == X - 1

    def x_factor(lo, hi, above):
        part = slice(lo, hi)
        c = xc_s[part]
        a = jnp.where(first, 1.0, pltpu.roll(c, 1, 2))
        e = above + yc_s[part] + zd_s[part]
        for n, s in enumerate(strides_of(X)):
            low, high = lane3 >= s, lane3 < X - s
            inv = 1.0 / (a + c + e)
            ai, ci = a * inv, c * inv
            am, cm = jnp.where(low, ai, 0.0), jnp.where(high, ci, 0.0)
            wx_s[n, 0, part], wx_s[n, 1, part] = cm, am
            a = a * jnp.where(low, pltpu.roll(ai, s, 2), 1.0)
            c = c * jnp.where(high, pltpu.roll(ci, X - s, 2), 1.0)
            e = e + pltpu.roll(cm * e, s, 2) + pltpu.roll(am * e, X - s, 2)
        inv = 1.0 / (a + c + e)
        ix_s[part], lx_s[part], rx_s[part] = inv, a * inv, c * inv

    def z_terms(v, part):
        return zl_s[part] * pltpu.roll(v, 1, 1) + zt_s[part] * pltpu.roll(v, Z - 1, 1)

    def x_source(lo, hi, lower, upper):
        part = slice(lo, hi)
        r_s[part] = fo_s[part] + yl_s[part] * lower + yc_s[part] * upper + z_terms(p_s[part], part)

    ends = jnp.logical_or(lane == 0, lane == X - 1)

    def edge_sums(j):
        r = r_s[j]
        return jnp.sum(lx_s[j] * r, axis=1, keepdims=True), jnp.sum(rx_s[j] * r, axis=1, keepdims=True)

    def pack_row(packed, j):
        gs, ge = edge_sums(j)
        v = jnp.where(ends, lx_s[j], pltpu.roll(rx_s[j], 2, 1))
        v = jnp.where(item < GS, pltpu.roll(v, SLOTS * j + 1, 1), jnp.where(item == GS, gs, ge))
        return jnp.where(group == j, v, packed)

    yl_s[1:Y] = yc_s[0:Y - 1]
    packed = jnp.zeros((Z, X), f32)
    for lo in range(0, Y, CH):
        hi = lo + CH
        at = max(lo, 1)
        x_factor(at, hi, yl_s[at:hi])
        at, to = max(lo, 1), min(hi, Y - 1)
        x_source(at, to, p_s[at - 1:to - 1], p_s[at + 1:to + 1])
        for j in range(at, to):
            packed = pack_row(packed, j)

    @pl.when(jnp.logical_not(has_w))
    def _():
        hx[...] = jnp.zeros_like(hx)
        cbuf[0] = jnp.zeros_like(cbuf[0])
        ebuf[0] = jnp.zeros_like(ebuf[0])

    @pl.when(jnp.logical_not(has_e))
    def _():
        cbuf[2] = jnp.zeros_like(cbuf[2])
        ebuf[1] = jnp.zeros_like(ebuf[1])

    @pl.when(jnp.logical_not(has_n))
    def _():
        hyd[...] = jnp.zeros_like(hyd)
        nbuf[0] = jnp.zeros_like(nbuf[0])
        for d in range(3):
            cbuf[d, :, 0:3] = jnp.zeros_like(cbuf[d, :, 0:3])
        for d in range(2):
            ebuf[d, 0] = jnp.zeros_like(ebuf[d, 0])

    @pl.when(jnp.logical_not(has_s))
    def _():
        hyu[...] = jnp.zeros_like(hyu)
        nbuf[1] = jnp.zeros_like(nbuf[1])
        for d in range(3):
            cbuf[d, :, 3 + CY:] = jnp.zeros_like(cbuf[d, :, 3 + CY:])
        for d in range(2):
            ebuf[d, 2] = jnp.zeros_like(ebuf[d, 2])

    await_recv(sx0, hx, ssem, s0.at[0], (east, gy), has_w)
    await_recv(sy0.at[0:2], hyd, ssem, s0.at[1], (gx, south), has_n)
    await_recv(sy0.at[2:3], hyu, ssem, s0.at[2], (gx, north), has_s)

    yl_s[0] = hyd[0]
    for j in range(Y):
        xl_s[j] = jnp.where(lane == 0, hx[:, SLOTS * j + XC:SLOTS * j + XC + 1], pltpu.roll(xc_s[j], 1, 1))

    ysteps = strides_of(Y)
    for lo in range(0, Z, 8):
        zs = slice(lo, lo + 8)
        a = [yl_s[j, zs] for j in range(Y)]
        c = [yc_s[j, zs] for j in range(Y)]
        e = [xl_s[j, zs] + xc_s[j, zs] + zd_s[j, zs] for j in range(Y)]
        for n, s in enumerate(ysteps):
            inv = [1.0 / (a[j] + c[j] + e[j]) for j in range(Y)]
            ai, ci = [a[j] * inv[j] for j in range(Y)], [c[j] * inv[j] for j in range(Y)]
            for j in range(Y):
                if j + s < Y:
                    wy_s[n, 0, j, zs] = ci[j]
                if j >= s:
                    wy_s[n, 1, j, zs] = ai[j]
            e2 = []
            for j in range(Y):
                v = e[j]
                if j >= s:
                    v = v + ci[j - s] * e[j - s]
                if j + s < Y:
                    v = v + ai[j + s] * e[j + s]
                e2.append(v)
            a = [a[j] * ai[j - s] if j >= s else a[j] for j in range(Y)]
            c = [c[j] * ci[j + s] if j + s < Y else c[j] for j in range(Y)]
            e = e2
        for j in range(Y):
            inv = 1.0 / (a[j] + c[j] + e[j])
            iy_s[j, zs], ly_s[j, zs], ry_s[j, zs] = inv, a[j] * inv, c[j] * inv

    k_top, k_end = jnp.sqrt(yl_s[0]), jnp.sqrt(yc_s[Y - 1])
    i_top = jnp.where(has_n, 1.0 / jnp.where(has_n, k_top, 1.0), 0.0)
    ysc[0], ysc[1] = i_top, 1.0 / k_end
    syc[0], syc[1], syc[2] = ly_s[0], ly_s[Y - 1] * k_end * i_top, ry_s[Y - 1]
    ycb[gy] = syc[...]
    for j in y_peers:
        comm.send(syc, ycb.at[gy], syco.at[gy], (gx, j))

    x_factor(0, 1, yl_s[0:1])
    x_source(0, 1, hyd[1:2], p_s[1:2])
    x_source(Y - 1, Y, p_s[Y - 2:Y - 1], hyu[0:1])
    for lo in range(0, Y, Y - 1):
        packed = pack_row(packed, lo)
    packed = jnp.where(item == XC, sx0[...], packed)
    sxb[...] = packed
    xb[gx] = packed
    for i in x_peers:
        comm.send(sxb, xb.at[gx], sx.at[0, gx], (i, gy))

    def x_local():
        for lo in range(0, Y, CH):
            part = slice(lo, lo + CH)
            r = r_s[part]
            for n, s in enumerate(strides_of(X)):
                r = r + pltpu.roll(wx_s[n, 0, part] * r, s, 2) + pltpu.roll(wx_s[n, 1, part] * r, X - s, 2)
            g_s[part] = r * ix_s[part]

    def y_local():
        for lo in range(0, Z, 8):
            zs = slice(lo, lo + 8)
            r = [r_s[j, zs] for j in range(Y)]
            for n, s in enumerate(ysteps):
                low = [wy_s[n, 0, j, zs] * r[j] if j + s < Y else None for j in range(Y)]
                high = [wy_s[n, 1, j, zs] * r[j] if j >= s else None for j in range(Y)]
                r2 = []
                for j in range(Y):
                    v = r[j]
                    if j >= s:
                        v = v + low[j - s]
                    if j + s < Y:
                        v = v + high[j + s]
                    r2.append(v)
                r = r2
            for j in range(Y):
                g_s[j, zs] = r[j] * iy_s[j, zs]

    x_local()

    half = X // 2
    off = half // 2
    ii = lax.broadcasted_iota(jnp.int32, (X, X), 0)
    mm = lax.broadcasted_iota(jnp.int32, (X, X), 1)

    def selection(step, start):
        target = lax.rem((ii + (step + 2)) // 2 - 1 + start + X, X)
        return jnp.where(mm == target, 0.125, 0.0)

    def pairs(field):
        v = field.reshape(CY, 2, Z, X)
        pair_s[...] = (v[:, 0] + v[:, 1]).reshape(CY * Z, X)
        return pair_s[pl.ds(0, CY * CZ, stride=2), :] + pair_s[pl.ds(1, CY * CZ, stride=2), :]

    def mxu(a, b):
        return jnp.dot(a, b, precision=lax.Precision.HIGHEST, preferred_element_type=f32)

    here, there = selection(0, off), selection(0, half + off)
    sel2 = jnp.concatenate([here, there], axis=0)
    zfull = jnp.stack([rows(z_ref, j) for j in range(Y)])
    damp = jnp.stack([rows(d_ref, j) for j in range(Y)])
    for m, (u, v) in enumerate(((xc_s[...], yc_s[...]), (zfull, damp))):
        both_pairs = jnp.concatenate([pairs(u), pairs(v)], axis=1)
        part = mxu(both_pairs, sel2).reshape(CY, CZ, X)
        cown[m] = part
        cbuf[1, m, 3:3 + CY] = part

    def coarse_parts(straight):
        def rows_of(slot, lo, n):
            return cbuf.at[slot, :, pl.ds(lo, n)]

        out = []
        for slot, i, ok, back in ((0, west, has_w, 2), (1, gx, None, 1), (2, east, has_e, 0)):
            both_ok = (lambda c: c) if ok is None else (lambda c, ok=ok: jnp.logical_and(c, ok))
            if straight:
                if ok is not None:
                    out.append((cown, 3, CY, 0, slot, back, (i, gy), ok, ok))
            else:
                out.append((cown.at[:, pl.ds(CY - 3, 3)], 0, 3, 1, slot, back, (i, south), both_ok(has_s), both_ok(has_n)))
                out.append((cown.at[:, pl.ds(0, 2)], 3 + CY, 2, 2, slot, back, (i, north), both_ok(has_n), both_ok(has_s)))
        return rows_of, out

    def coarse_send(straight):
        rows_of, parts = coarse_parts(straight)
        for src, lo, n, kind, slot, back, dev, ok, _ in parts:
            comm.send(src, rows_of(back, lo, n), sc.at[kind, back], dev, ok)

    def coarse_wait():
        for straight in (True, False):
            rows_of, parts = coarse_parts(straight)
            for src, lo, n, kind, slot, back, dev, _, ok in parts:
                await_recv(src, rows_of(slot, lo, n), ssem, sc.at[kind, slot], dev, ok)

    def slot(v, k):
        return v if k == 0 else pltpu.roll(v, X - k, 1)

    def expand(v):
        return jnp.concatenate([v, pltpu.roll(v, X - 1, 1)], axis=0)

    def x_solve(hl, hr, gs, ge):
        alpha = jnp.zeros((Z, X), f32)
        for d in range(nx - 1):
            alpha = jnp.where(d < gx, hl(d) + xtau[d] * alpha, alpha)
        gamma = jnp.zeros((Z, X), f32)
        for d in reversed(range(1, nx)):
            gamma = jnp.where(d > gx, hr(d) + xtau2[d] * gamma, gamma)
        p = xrho[gx] * alpha + xbet[gx] * gs
        q = gamma + xdlt[gx] * ge
        return xkk[0] * p + xkk[1] * q, xkk[2] * q + xkk[3] * p

    def x_first():
        for i in x_peers:
            await_recv(sxb, xb.at[i], ssem, sx.at[0, i], (i, gy))
        tiles = [xb[d] for d in range(nx)]
        cut = [[slot(t, k) for t in tiles] for k in range(SLOTS - 1)]
        own = [slot(sxb[...], k) for k in range(SLOTS - 1)]
        inv = [1.0 / v for v in cut[XC]]
        ge = [cut[GE][d] * inv[d] for d in range(nx)]
        gs = cut[GS]
        xown[0] = 1.0 / own[XC]
        chain_factor(nx, gx, cut[LS], cut[LE], cut[RS], cut[RE], cut[XC], [own[LS], own[LE], own[RS], own[RE]],
                     xrho, xtau, xsig, xbet, xtau2, xsig2, xscl, xdlt, xkk)
        return x_solve(
            lambda d: ge[d] + xsig[d] * gs[d], lambda d: xscl[d] * gs[d] + xsig2[d] * ge[d], own[GS], own[GE] * xown[0]
        )

    def x_second():
        packed = jnp.zeros((Z, X), f32)
        for j in range(Y):
            gs, ge = edge_sums(j)
            packed = jnp.where(group == j, jnp.where(item == 0, gs, ge), packed)
        gs, ge = packed, pltpu.roll(packed, X - 1, 1) * xown[0]
        for side, h in enumerate((ge + xsig[gx] * gs, xscl[gx] * gs + xsig2[gx] * ge)):
            sx1[side] = jnp.where(item[:CZ] == 0, h[:CZ], pltpu.roll(h[CZ:], 1, 1))
        for i in x_peers:
            comm.send(sx1.at[jnp.where(i > gx, 0, 1)], xb1.at[gx], sx.at[1, gx], (i, gy))
        x_local()
        coarse_send(False)
        for i in x_peers:
            await_recv(sx1.at[0], xb1.at[i], ssem, sx.at[1, i], (i, gy))
        return x_solve(lambda d: expand(xb1[d]), lambda d: expand(xb1[d]), gs, ge)

    def y_half(m, left, right):
        top, end = jnp.zeros((Z, X), f32), jnp.zeros((Z, X), f32)
        for j in range(Y):
            u = jnp.broadcast_to(left[:, SLOTS * j:SLOTS * j + 1], (Z, X))
            w = jnp.broadcast_to(right[:, SLOTS * j:SLOTS * j + 1], (Z, X))
            v = g_s[j] + lx_s[j] * u + rx_s[j] * w
            q_s[j] = v
            before = jnp.where(lane == 0, v, pltpu.roll(v, 1, 1))
            after = jnp.where(lane == X - 1, w, pltpu.roll(v, X - 1, 1))
            r = fo_s[j] + xl_s[j] * before + xc_s[j] * after + jnp.where(lane == 0, u - v, 0.0)
            r = r + zl_s[j] * pltpu.roll(v, 1, 0) + zt_s[j] * pltpu.roll(v, Z - 1, 0)
            r_s[j] = r
            top, end = top + ly_s[j] * r, end + ry_s[j] * r
        top, end = top * ysc[0], end * ysc[1]
        if m == 0:
            for j in y_peers:
                await_recv(syc, ycb.at[j], ssem, syco.at[j], (gx, j))
            ls, mid, re = [[ycb[d, k] for d in range(ny)] for k in range(3)]
            interface_factor(
                ny, gy, ls, mid, mid, re, [syc[0], syc[1], syc[1], syc[2]],
                ytau, ysig, ybet, ytau2, ysig2, ydlt, ykk,
            )
        shy[m, 0] = end + ysig[gy] * top
        shy[m, 1] = top + ysig2[gy] * end
        yb[m, gy] = shy[m, 0]
        for j in y_peers:
            side = jnp.where(j > gy, 0, 1)
            comm.send(shy.at[m, side], yb.at[m, gy], sy.at[m, gy], (gx, j))
        y_local()
        if m == 0:
            coarse_send(True)
        else:
            coarse_wait()
            coefs = planes()
        for j in y_peers:
            await_recv(shy.at[m, 0], yb.at[m, j], ssem, sy.at[m, j], (gx, j))
        above, below = interface_solve(ny, gy, lambda d: yb[m, d], lambda d: yb[m, d], top, end, ytau, ytau2, ykk)
        above, below = above * ysc[0], below * ysc[1]
        return above, below, (coefs if m else None)

    centre = jnp.logical_and(lane3 >= off, lane3 < off + half)
    H = CY + 4
    row = lax.broadcasted_iota(jnp.int32, (H, 1, 1), 0)
    inside = jnp.logical_and(
        jnp.logical_or(row >= 2, has_n), jnp.logical_or(row < 2 + CY, has_s)
    )
    inside = jnp.logical_and(
        inside,
        jnp.logical_and(jnp.logical_or(lane3 >= off, has_w), jnp.logical_or(lane3 < off + half, has_e)),
    )

    def planes():
        out = []
        for m in range(2):
            w, o, e = cbuf[0, m], cbuf[1, m], cbuf[2, m]
            out.append(jnp.where(centre, o, pltpu.roll(jnp.where(lane3 >= half, w, e), half, 2)))
            out.append(jnp.where(centre, pltpu.roll(o, half, 2), jnp.where(lane3 < half, w, e)))
        cx, cy, cz, cd = out
        czl = lax.broadcasted_iota(jnp.int32, (1, CZ, 1), 1)
        cyl, cy = cy[:H], cy[1:]
        cx, cz, cd = cx[1:], cz[1:], cd[1:]
        cd = jnp.where(inside, cd, 1.0)
        ct = jnp.where(czl < CZ - 1, cz, 0.0)
        cl = pltpu.roll(ct, 1, 1)
        cxl = pltpu.roll(cx, 1, 2)
        diag = cxl + cx + cyl + cy + cl + ct + cd
        return cx, cxl, cy, cyl, cl, ct, diag, RELAX / diag

    left, right = x_first()
    above, below, _ = y_half(0, left, right)
    p_s[...] = g_s[...] + ly_s[...] * above[None] + ry_s[...] * below[None]
    for lo in range(0, Y, CH):
        hi = lo + CH
        lower = jnp.concatenate([above[None], p_s[0:hi - 1]], axis=0) if lo == 0 else p_s[lo - 1:hi - 1]
        upper = jnp.concatenate([p_s[lo + 1:Y], below[None]], axis=0) if hi == Y else p_s[lo + 1:hi + 1]
        x_source(lo, hi, lower, upper)
    left, right = x_second()
    above, below, coefs = y_half(1, left, right)
    v = g_s[...] + ly_s[...] * above[None] + ry_s[...] * below[None]
    for j in range(Y):
        op_ref[pl.ds(j, Z, stride=Y), :] = v[j]

    whole = slice(0, Y)
    change = v - q_s[...]
    stacked = jnp.concatenate(
        [pairs(xc_s[...] * change), pairs(xl_s[...] * change), pairs(z_terms(change, whole))], axis=1
    )
    sel3 = jnp.concatenate([selection(1, off), selection(-1, off), here], axis=0)
    partial = mxu(stacked, sel3).reshape(CY, CZ, X)
    rown[0], rown[1] = partial[0:2], partial[CY - 2:]
    clane = lax.broadcasted_iota(jnp.int32, (CZ, X), 1)
    inner = clane % half
    edge = jnp.zeros((CZ, X), f32)
    for r in range(CY):
        edge = jnp.where(inner >= 4 * r, pltpu.roll(partial[r], half - off + 2 + 4 * r, 1), edge)
    sedge[...] = edge

    def residual_exchange(starting):
        for n, (dev, ok, back) in enumerate((((gx, south), has_s, 0), ((gx, north), has_n, 1))):
            if starting:
                comm.send(rown.at[1 - n], nbuf.at[back], sr.at[2, back], dev, ok)
            else:
                await_recv(rown.at[n], nbuf.at[n], ssem, sr.at[2, n], dev, (has_n, has_s)[n])
        for n, (i, ok) in enumerate(((west, has_w), (east, has_e))):
            for r, (j, okj) in enumerate(((north, has_n), (gy, None), (south, has_s))):
                cond = ok if okj is None else jnp.logical_and(ok, okj)
                if starting:
                    comm.send(sedge, ebuf.at[1 - n, 2 - r], sr.at[1 - n, 2 - r], (i, j), cond)
                else:
                    await_recv(sedge, ebuf.at[n, r], ssem, sr.at[n, r], (i, j), cond)

    residual_exchange(True)
    cx, cxl, cy, cyl, cl, ct, diag, scale = coefs
    residual_exchange(False)
    fringe = []
    for n in range(3):
        both = jnp.where(clane < half, ebuf[0, n], ebuf[1, n])
        for r in ((CY - 2, CY - 1), range(CY), (0, 1))[n]:
            fringe.append(pltpu.roll(both, (off - 2 - 4 * r) % X, 1))
    near = jnp.logical_or(
        jnp.logical_and(lane3 >= off - 2, lane3 <= off), jnp.logical_and(lane3 >= off + half - 1, lane3 <= off + half + 1)
    )
    res = jnp.concatenate([nbuf[0], partial, nbuf[1]], axis=0) + jnp.where(near, jnp.stack(fringe), 0.0)
    res = jnp.where(inside, res, 0.0)
    cor = scale * res
    for repeat in range(COARSE - 1):
        lo, n = 1 + repeat, H - 2 - 2 * repeat
        cut = slice(lo, lo + n)
        mid, over, under = cor[1:-1], cor[:-2], cor[2:]
        applied = (
            diag[cut] * mid
            - cxl[cut] * pltpu.roll(mid, 1, 2)
            - cx[cut] * pltpu.roll(mid, X - 1, 2)
            - cyl[cut] * over
            - cy[cut] * under
            - cl[cut] * pltpu.roll(mid, 1, 1)
            - ct[cut] * pltpu.roll(mid, CZ - 1, 1)
        )
        cor = jnp.where(inside[cut], mid + scale[cut] * (res[cut] - applied), 0.0)
    hj = CY // 2
    mine = jnp.where(lane3 < half, pltpu.roll(cor[:hj], X - off, 2), pltpu.roll(cor[hj:], off, 2))
    fown[...] = mine
    fbuf[gx] = mine
    for i in x_peers:
        comm.send(fown, fbuf.at[gx], sf.at[gx], (i, gy))
    own = pltpu.roll(res[2:2 + CY], X - off, 2)
    for j in range(CY):
        flip[pl.ds(j, CZ, stride=CY), :] = own[j]
    or_ref[...] = flip[0:CZ * CY, :half]
    for i in x_peers:
        await_recv(fown, fbuf.at[i], ssem, sf.at[i], (i, gy))
    for t in range(nx // 2):
        u, v = fbuf[2 * t], fbuf[2 * t + 1]
        top = jnp.where(lane3 < half, u, pltpu.roll(v, half, 2))
        low = jnp.where(lane3 < half, pltpu.roll(u, half, 2), v)
        base = (t + 1) * CZ * CY
        for j in range(CY):
            flip[pl.ds(base + j, CZ, stride=CY), :] = top[j] if j < hj else low[j - hj]
        oc_ref[:, t * X:(t + 1) * X] = flip[base:base + CZ * CY, :]
    comm.finish()


def put(*refs):
    sems = refs[6]
    give = [pltpu.make_async_copy(refs[m], refs[3 + m], sems.at[m]) for m in range(3)]
    for copy in give:
        copy.start()
    for copy in give:
        copy.wait()


def body(nx, ny, *args):
    Z, Y, X = args[0].shape
    CZ, CY = Z // 2, Y // 2
    flat = [v.reshape(Z * Y, X) for v in args]
    f32 = jnp.float32

    def vm(*shape):
        return pltpu.VMEM(shape, f32)

    block = (Y, Z, X)
    assert Y * SLOTS <= X and 4 * CY <= X // 2
    nsx, nsy = len(strides_of(X)), len(strides_of(Y))
    sends = 3 + (ny - 1) * 3 + (nx - 1) * 3 + 8 * 2
    dma = pltpu.SemaphoreType.DMA
    scratch = (
        [vm(*block) for _ in range(12)]
        + [vm(*block), vm(*block), vm(*block), vm(nsx, 2, *block), vm(*block), vm(*block), vm(*block), vm(nsy, 2, *block)]
        + [vm(Z, X), vm(3, Z, X), vm(Z, X), vm(2, Z, X), vm(1, Z, X)]
        + [vm(nx, Z, X), vm(Z, X), vm(nx, CZ, X), vm(2, CZ, X)]
        + [vm(ny, 3, Z, X), vm(3, Z, X), vm(2, ny, Z, X), vm(2, 2, Z, X)]
        + [vm(1, Z, X)] + [vm(nx, Z, X) for _ in range(8)] + [vm(4, Z, X)]
        + [vm(ny, Z, X) for _ in range(6)] + [vm(6, Z, X), vm(2, Z, X)]
        + [vm(CY * Z, X), vm(2, CY, CZ, X), vm(3, 2, CY + 5, CZ, X), vm(2, 2, CZ, X), vm(2, 2, CZ, X),
           vm(2, 3, CZ, X), vm(CZ, X), vm(CY // 2, CZ, X), vm(nx, CY // 2, CZ, X), vm((nx // 2 + 1) * CZ * CY, X)]
        + [dma((sends,)), dma((3,)), dma((2, nx)), dma((ny,)), dma((2, ny)), dma((3, 3)), dma((3, 3)), dma((nx,))]
        + [vm(6, Z * Y, X), dma((6,))]
    )
    p, r, c = pl.pallas_call(
        functools.partial(kernel, nx, ny),
        out_shape=(
            vm(Z * Y, X),
            vm(CZ * CY, X // 2),
            vm(CZ * CY, nx * X // 2),
        ),
        in_specs=[pl.BlockSpec(memory_space=pltpu.HBM)] * 6,
        out_specs=[pl.BlockSpec(memory_space=pltpu.VMEM)] * 3,
        scratch_shapes=scratch,
        compiler_params=pltpu.CompilerParams(
            collective_id=0, has_side_effects=True, vmem_limit_bytes=60000000
        ),
    )(*flat)
    p, r, c = pl.pallas_call(
        put,
        out_shape=tuple(jax.ShapeDtypeStruct(v.shape, f32) for v in (p, r, c)),
        in_specs=[pl.BlockSpec(memory_space=pltpu.VMEM)] * 3,
        out_specs=[pl.BlockSpec(memory_space=pltpu.HBM)] * 3,
        scratch_shapes=[dma((3,))],
    )(*[pltpu.with_memory_space_constraint(v, pltpu.VMEM) for v in (p, r, c)])
    return p.reshape(Z, Y, X), r.reshape(CZ, CY, X // 2), c.reshape(CZ, CY, nx * X // 2)


def solution(mesh):
    nx, ny = mesh.shape["gx"], mesh.shape["gy"]
    split = P(None, "gy", "gx")
    return jax.shard_map(
        functools.partial(body, nx, ny),
        mesh=mesh,
        in_specs=(split,) * 6,
        out_specs=(split, split, P(None, "gy", None)),
        check_vma=False,
    )
```

time: 35.9 us -> 34 us (0.947)
  Pallas kernels: 35.1 us -> 33.2 us
    pallas_call x1, Pallas kernels: 34.4 us -> 32.5 us  [body(): pl.pallas_call(functools.partial(kernel, nx, ny), out_shape=(vm(Z * Y, X)...]
where the time goes in v1:
time: 34 us; the launch traced here: 33.8 us
  Pallas kernels  33.2 us (98%)
  between operations  0.64 us (2%)
    pallas_call x1, Pallas kernels, body(): pl.pallas_call(functools.partial(kernel, nx, ny), out_shape=(vm(Z * Y, X)...  32.5 us
    pallas_call x1, Pallas kernels, body(): pl.pallas_call(put, out_shape=tuple((jax.ShapeDtypeStruct(v.shape, f32) f...  0.71 us

profile of v1, /device:TPU:0, one launch (start us, length us, event | category | flops | bytes accessed | tf_op | source)
XLA Modules:
  0.0 33.8 jit_solution(13492546029407964482)
XLA Ops:
  0.6 32.5 %shard_map.85 = (f32[256,128]{1,0:T(8,128)S(1)}, f32[64,64]{1,0:T(8,128)S(1)}, f32[64,256]{1,0:T(8,128)S(1)}) custom-call(f32[256,128]{1,0:T(8,128)} %bitcast.9, f32[256,128]{1,0:T(8,128)} %bitcast.10, f32[256,128]{1,0:T(8,128)} %bitcast.11, f32[256,128]{1,0:T(8,128)} %bitcast.12, f32[256,128]{1,0:T(8,128)} %bitcast.13, f32[256,128]{1,0:T(8,128)} %bitcast.14), custom_call_target="tpu_custom_call" | custom-call | tf_op jit(solution)/shard_map/pallas_call | solution.py:701
  33.1 0.7 %shard_map.86 = (f32[256,128]{1,0:T(8,128)}, f32[64,64]{1,0:T(8,128)}, f32[64,256]{1,0:T(8,128)}) custom-call(f32[256,128]{1,0:T(8,128)S(1)} %get-tuple-element.9.refs_0_, f32[64,64]{1,0:T(8,128)S(1)} %get-tuple-element.10.refs_1_, f32[64,256]{1,0:T(8,128)S(1)} %get-tuple-element.11.refs_2_), custom_call_target="tpu_custom_call" | custom-call | tf_op jit(solution)/shard_map/pallas_call | solution.py:715

commit v2 on v1

--- a/solution.py
+++ b/solution.py
@@ -159,8 +159,8 @@
            sx0, sy0, hx, hyd, hyu, xb, sxb, xb1, sx1, ycb, syc, yb, shy,
            xown, xrho, xtau, xsig, xbet, xtau2, xsig2, xscl, xdlt, xkk,
            ytau, ysig, ybet, ytau2, ysig2, ydlt, ykk, ysc,
-           pair_s, cown, cbuf, rown, nbuf, ebuf, sedge, fown, fbuf, flip,
-           ssem, s0, sx, syco, sy, sc, sr, sf, ins, sin):
+           pair_s, sel_s, cown, cbuf, wbuf, pbuf, sxt, xtr, ebuf, sedge, fown, fbuf, flip,
+           ssem, s0, sx, syco, sy, sc, sr, sw, sf, ins, sin):
     Y, Z, X = xc_s.shape
     CY, CZ = Y // 2, Z // 2
     f32 = jnp.float32
@@ -298,20 +298,20 @@
     @pl.when(jnp.logical_not(has_n))
     def _():
         hyd[...] = jnp.zeros_like(hyd)
-        nbuf[0] = jnp.zeros_like(nbuf[0])
+        wbuf[0:2] = jnp.zeros_like(wbuf[0:2])
+        pbuf[0:2] = jnp.zeros_like(pbuf[0:2])
+        xtr[0] = jnp.zeros_like(xtr[0])
         for d in range(3):
             cbuf[d, :, 0:3] = jnp.zeros_like(cbuf[d, :, 0:3])
-        for d in range(2):
-            ebuf[d, 0] = jnp.zeros_like(ebuf[d, 0])
 
     @pl.when(jnp.logical_not(has_s))
     def _():
         hyu[...] = jnp.zeros_like(hyu)
-        nbuf[1] = jnp.zeros_like(nbuf[1])
+        wbuf[CY + 2:] = jnp.zeros_like(wbuf[CY + 2:])
+        pbuf[CY + 2:] = jnp.zeros_like(pbuf[CY + 2:])
+        xtr[1] = jnp.zeros_like(xtr[1])
         for d in range(3):
             cbuf[d, :, 3 + CY:] = jnp.zeros_like(cbuf[d, :, 3 + CY:])
-        for d in range(2):
-            ebuf[d, 2] = jnp.zeros_like(ebuf[d, 2])
 
     await_recv(sx0, hx, ssem, s0.at[0], (east, gy), has_w)
     await_recv(sy0.at[0:2], hyd, ssem, s0.at[1], (gx, south), has_n)
@@ -407,23 +407,49 @@
         target = lax.rem((ii + (step + 2)) // 2 - 1 + start + X, X)
         return jnp.where(mm == target, 0.125, 0.0)
 
-    def pairs(field):
-        v = field.reshape(CY, 2, Z, X)
-        pair_s[...] = (v[:, 0] + v[:, 1]).reshape(CY * Z, X)
-        return pair_s[pl.ds(0, CY * CZ, stride=2), :] + pair_s[pl.ds(1, CY * CZ, stride=2), :]
-
-    def mxu(a, b):
-        return jnp.dot(a, b, precision=lax.Precision.HIGHEST, preferred_element_type=f32)
-
-    here, there = selection(0, off), selection(0, half + off)
-    sel2 = jnp.concatenate([here, there], axis=0)
-    zfull = jnp.stack([rows(z_ref, j) for j in range(Y)])
-    damp = jnp.stack([rows(d_ref, j) for j in range(Y)])
-    for m, (u, v) in enumerate(((xc_s[...], yc_s[...]), (zfull, damp))):
-        both_pairs = jnp.concatenate([pairs(u), pairs(v)], axis=1)
-        part = mxu(both_pairs, sel2).reshape(CY, CZ, X)
+    def level_pairs(n, levels):
+        for k, v in enumerate(levels):
+            pair_s[n, k * Z:(k + 1) * Z] = v
+        count = len(levels) * CZ
+        return pair_s[n, pl.ds(0, count, stride=2), :] + pair_s[n, pl.ds(1, count, stride=2), :]
+
+    def pairs(n, field):
+        return level_pairs(n, [field(2 * k) + field(2 * k + 1) for k in range(CY)])
+
+    def gathered(parts, first):
+        v = jnp.concatenate(parts, axis=1)
+        high = v.astype(jnp.bfloat16)
+        v = v - high.astype(f32)
+        mid = v.astype(jnp.bfloat16)
+        low = (v - mid.astype(f32)).astype(jnp.bfloat16)
+        sel = sel_s[first * X:(first + len(parts)) * X]
+        return sum(jnp.dot(u, sel, preferred_element_type=f32) for u in (low, mid, high))
+
+    for n, sel in enumerate((selection(1, off), selection(-1, off), selection(0, off), selection(0, half + off))):
+        sel_s[n * X:(n + 1) * X] = sel.astype(jnp.bfloat16)
+    for m, (u, v) in enumerate(((lambda j: xc_s[j], lambda j: yc_s[j]), (lambda j: rows(z_ref, j), lambda j: rows(d_ref, j)))):
+        part = gathered([pairs(0, u), pairs(1, v)], 2).reshape(CY, CZ, X)
         cown[m] = part
         cbuf[1, m, 3:3 + CY] = part
+
+    for k in range(CY):
+        j = 2 * k
+        for n, (g, scale) in enumerate(((ly_s, ysc[0]), (ry_s, ysc[1]))):
+            u, v = g[j] * scale, g[j + 1] * scale
+            at = 2 + k
+            wbuf[at, n] = xc_s[j] * u + xc_s[j + 1] * v
+            wbuf[at, 2 + n] = xl_s[j] * u + xl_s[j + 1] * v
+            wbuf[at, 4 + n] = zl_s[j] * pltpu.roll(u, 1, 0) + zl_s[j + 1] * pltpu.roll(v, 1, 0)
+            wbuf[at, 6 + n] = zt_s[j] * pltpu.roll(u, Z - 1, 0) + zt_s[j + 1] * pltpu.roll(v, Z - 1, 0)
+
+    def to_rows(buf, sems, starting):
+        for n, (dev, there, here) in enumerate((((gx, north), has_n, has_s), ((gx, south), has_s, has_n))):
+            src = buf.at[pl.ds(2 if n == 0 else CY, 2)]
+            dst = buf.at[pl.ds(CY + 2 if n == 0 else 0, 2)]
+            if starting:
+                comm.send(src, dst, sems.at[n], dev, there)
+            else:
+                await_recv(src, dst, ssem, sems.at[n], dev, here)
 
     def coarse_parts(straight):
         def rows_of(slot, lo, n):
@@ -494,8 +520,9 @@
             sx1[side] = jnp.where(item[:CZ] == 0, h[:CZ], pltpu.roll(h[CZ:], 1, 1))
         for i in x_peers:
             comm.send(sx1.at[jnp.where(i > gx, 0, 1)], xb1.at[gx], sx.at[1, gx], (i, gy))
+        to_rows(wbuf, sw.at[0], True)
+        coarse_send(False)
         x_local()
-        coarse_send(False)
         for i in x_peers:
             await_recv(sx1.at[0], xb1.at[i], ssem, sx.at[1, i], (i, gy))
         return x_solve(lambda d: expand(xb1[d]), lambda d: expand(xb1[d]), gs, ge)
@@ -528,17 +555,43 @@
         for j in y_peers:
             side = jnp.where(j > gy, 0, 1)
             comm.send(shy.at[m, side], yb.at[m, gy], sy.at[m, gy], (gx, j))
+        if m:
+            sxt[0], sxt[1] = end, top
+            comm.send(sxt.at[0], xtr.at[1], sw.at[1, 0], (gx, north), has_n)
+            comm.send(sxt.at[1], xtr.at[0], sw.at[1, 1], (gx, south), has_s)
         y_local()
         if m == 0:
             coarse_send(True)
         else:
+            for j in range(Y):
+                r_s[j] = g_s[j] - q_s[j]
+            pbuf[2:CY + 2] = gathered([
+                pairs(0, lambda j: xc_s[j] * r_s[j]),
+                pairs(1, lambda j: xl_s[j] * r_s[j]),
+                pairs(2, lambda j: zl_s[j] * pltpu.roll(r_s[j], 1, 0) + zt_s[j] * pltpu.roll(r_s[j], Z - 1, 0)),
+            ], 0).reshape(CY, CZ, X)
+            to_rows(pbuf, sw.at[2], True)
             coarse_wait()
             coefs = planes()
+            to_rows(wbuf, sw.at[0], False)
         for j in y_peers:
             await_recv(shy.at[m, 0], yb.at[m, j], ssem, sy.at[m, j], (gx, j))
         above, below = interface_solve(ny, gy, lambda d: yb[m, d], lambda d: yb[m, d], top, end, ytau, ytau2, ykk)
-        above, below = above * ysc[0], below * ysc[1]
-        return above, below, (coefs if m else None)
+        if m == 0:
+            return above * ysc[0], below * ysc[1]
+        await_recv(sxt.at[0], xtr.at[1], ssem, sw.at[1, 0], (gx, north), has_s)
+        await_recv(sxt.at[1], xtr.at[0], ssem, sw.at[1, 1], (gx, south), has_n)
+        alpha, gamma = jnp.zeros((Z, X), f32), jnp.zeros((Z, X), f32)
+        for d in range(ny - 2):
+            alpha = jnp.where(d < gy - 1, yb[m, d] + ytau[d] * alpha, alpha)
+        for d in reversed(range(2, ny)):
+            gamma = jnp.where(d > gy + 1, yb[m, d] + ytau2[d] * gamma, gamma)
+        q_top = top + syc[0] * above + syc[1] * below
+        q_end = end + syc[1] * above + syc[2] * below
+        beta, delta = ybet[north], ydlt[south]
+        over = (alpha + beta * (xtr[0] + ycb[north, 1] * q_top)) / (1.0 - beta * ycb[north, 0])
+        under = (gamma + delta * (xtr[1] + ycb[south, 1] * q_end)) / (1.0 - delta * ycb[south, 2])
+        return above, below, coefs, [(over, q_top), (above, below), (q_end, under)]
 
     centre = jnp.logical_and(lane3 >= off, lane3 < off + half)
     H = CY + 4
@@ -569,7 +622,7 @@
         return cx, cxl, cy, cyl, cl, ct, diag, RELAX / diag
 
     left, right = x_first()
-    above, below, _ = y_half(0, left, right)
+    above, below = y_half(0, left, right)
     p_s[...] = g_s[...] + ly_s[...] * above[None] + ry_s[...] * below[None]
     for lo in range(0, Y, CH):
         hi = lo + CH
@@ -577,53 +630,28 @@
         upper = jnp.concatenate([p_s[lo + 1:Y], below[None]], axis=0) if hi == Y else p_s[lo + 1:hi + 1]
         x_source(lo, hi, lower, upper)
     left, right = x_second()
-    above, below, coefs = y_half(1, left, right)
-    v = g_s[...] + ly_s[...] * above[None] + ry_s[...] * below[None]
-    for j in range(Y):
-        op_ref[pl.ds(j, Z, stride=Y), :] = v[j]
-
-    whole = slice(0, Y)
-    change = v - q_s[...]
-    stacked = jnp.concatenate(
-        [pairs(xc_s[...] * change), pairs(xl_s[...] * change), pairs(z_terms(change, whole))], axis=1
-    )
-    sel3 = jnp.concatenate([selection(1, off), selection(-1, off), here], axis=0)
-    partial = mxu(stacked, sel3).reshape(CY, CZ, X)
-    rown[0], rown[1] = partial[0:2], partial[CY - 2:]
+    above, below, coefs, ghosts = y_half(1, left, right)
+    cx, cxl, cy, cyl, cl, ct, diag, scale = coefs
+    sides = [[], [], []]
+    for at in range(H):
+        a, b = ghosts[0 if at < 2 else 1 if at < CY + 2 else 2]
+        w = [wbuf[at, n] for n in range(8)]
+        sides[0].append(w[0] * a + w[1] * b)
+        sides[1].append(w[2] * a + w[3] * b)
+        a1, b1, a2, b2 = pltpu.roll(a, 1, 0), pltpu.roll(b, 1, 0), pltpu.roll(a, Z - 1, 0), pltpu.roll(b, Z - 1, 0)
+        sides[2].append(w[4] * a1 + w[5] * b1 + w[6] * a2 + w[7] * b2)
+    partial = gathered([level_pairs(n, v) for n, v in enumerate(sides)], 0).reshape(H, CZ, X)
+    to_rows(pbuf, sw.at[2], False)
+    res = jnp.where(inside, partial + pbuf[...], 0.0)
     clane = lax.broadcasted_iota(jnp.int32, (CZ, X), 1)
     inner = clane % half
-    edge = jnp.zeros((CZ, X), f32)
-    for r in range(CY):
-        edge = jnp.where(inner >= 4 * r, pltpu.roll(partial[r], half - off + 2 + 4 * r, 1), edge)
-    sedge[...] = edge
-
-    def residual_exchange(starting):
-        for n, (dev, ok, back) in enumerate((((gx, south), has_s, 0), ((gx, north), has_n, 1))):
-            if starting:
-                comm.send(rown.at[1 - n], nbuf.at[back], sr.at[2, back], dev, ok)
-            else:
-                await_recv(rown.at[n], nbuf.at[n], ssem, sr.at[2, n], dev, (has_n, has_s)[n])
-        for n, (i, ok) in enumerate(((west, has_w), (east, has_e))):
-            for r, (j, okj) in enumerate(((north, has_n), (gy, None), (south, has_s))):
-                cond = ok if okj is None else jnp.logical_and(ok, okj)
-                if starting:
-                    comm.send(sedge, ebuf.at[1 - n, 2 - r], sr.at[1 - n, 2 - r], (i, j), cond)
-                else:
-                    await_recv(sedge, ebuf.at[n, r], ssem, sr.at[n, r], (i, j), cond)
-
-    residual_exchange(True)
-    cx, cxl, cy, cyl, cl, ct, diag, scale = coefs
-    residual_exchange(False)
-    fringe = []
-    for n in range(3):
-        both = jnp.where(clane < half, ebuf[0, n], ebuf[1, n])
-        for r in ((CY - 2, CY - 1), range(CY), (0, 1))[n]:
-            fringe.append(pltpu.roll(both, (off - 2 - 4 * r) % X, 1))
-    near = jnp.logical_or(
-        jnp.logical_and(lane3 >= off - 2, lane3 <= off), jnp.logical_and(lane3 >= off + half - 1, lane3 <= off + half + 1)
-    )
-    res = jnp.concatenate([nbuf[0], partial, nbuf[1]], axis=0) + jnp.where(near, jnp.stack(fringe), 0.0)
-    res = jnp.where(inside, res, 0.0)
+
+    def fringe(v):
+        edge = jnp.zeros((CZ, X), f32)
+        for r in range(CY):
+            edge = jnp.where(inner >= SLOTS * r, pltpu.roll(v[r], half - off + 3 + SLOTS * r, 1), edge)
+        return edge
+
     cor = scale * res
     for repeat in range(COARSE - 1):
         lo, n = 1 + repeat, H - 2 - 2 * repeat
@@ -640,24 +668,44 @@
         )
         cor = jnp.where(inside[cut], mid + scale[cut] * (res[cut] - applied), 0.0)
     hj = CY // 2
-    mine = jnp.where(lane3 < half, pltpu.roll(cor[:hj], X - off, 2), pltpu.roll(cor[hj:], off, 2))
-    fown[...] = mine
-    fbuf[gx] = mine
+    fown[0:hj] = jnp.where(lane3 < half, pltpu.roll(cor[:hj], X - off, 2), pltpu.roll(cor[hj:], off, 2))
+    fown[hj] = fringe(cor)
+    fbuf[gx] = fown[...]
     for i in x_peers:
         comm.send(fown, fbuf.at[gx], sf.at[gx], (i, gy))
-    own = pltpu.roll(res[2:2 + CY], X - off, 2)
-    for j in range(CY):
-        flip[pl.ds(j, CZ, stride=CY), :] = own[j]
+    sedge[...] = fringe(res[2:CY + 2])
+    comm.send(sedge, ebuf.at[1], sr.at[1], (west, gy), has_w)
+    comm.send(sedge, ebuf.at[0], sr.at[0], (east, gy), has_e)
+    above, below = above * ysc[0], below * ysc[1]
+    for j in range(Y):
+        op_ref[pl.ds(j, Z, stride=Y), :] = g_s[j] + ly_s[j] * above + ry_s[j] * below
+    await_recv(sedge, ebuf.at[0], ssem, sr.at[0], (west, gy), has_w)
+    await_recv(sedge, ebuf.at[1], ssem, sr.at[1], (east, gy), has_e)
+    both = jnp.where(clane < half, ebuf[0], ebuf[1])
+    for r in range(CY):
+        v = pltpu.roll(both, (off - 3 - SLOTS * r) % X, 1)
+        v = res[2 + r] + jnp.where(jnp.logical_or(clane == off, clane == off + half - 1), v, 0.0)
+        flip[pl.ds(r, CZ, stride=CY), :] = pltpu.roll(v, X - off, 1)
     or_ref[...] = flip[0:CZ * CY, :half]
     for i in x_peers:
         await_recv(fown, fbuf.at[i], ssem, sf.at[i], (i, gy))
+    nothing = jnp.zeros((CZ, X), f32)
+    edges = [nothing] + [fbuf[d, hj] for d in range(nx)] + [nothing]
+    spill = jnp.logical_or(clane >= X - 3, jnp.logical_and(clane >= half, clane < half + 3))
+    spill2 = jnp.logical_or(clane < 3, jnp.logical_and(clane >= half - 3, clane < half))
     for t in range(nx // 2):
-        u, v = fbuf[2 * t], fbuf[2 * t + 1]
+        u, v = fbuf[2 * t, 0:hj], fbuf[2 * t + 1, 0:hj]
         top = jnp.where(lane3 < half, u, pltpu.roll(v, half, 2))
         low = jnp.where(lane3 < half, pltpu.roll(u, half, 2), v)
+        one = jnp.where(clane < half, edges[2 * t + 1], edges[2 * t + 3])
+        two = jnp.where(clane < half, edges[2 * t], edges[2 * t + 2])
         base = (t + 1) * CZ * CY
         for j in range(CY):
-            flip[pl.ds(base + j, CZ, stride=CY), :] = top[j] if j < hj else low[j - hj]
+            turn = (half - 3 - SLOTS * j) % X
+            v = top[j] if j < hj else low[j - hj]
+            v = v + jnp.where(spill, pltpu.roll(one, turn, 1), 0.0)
+            v = v + jnp.where(spill2, pltpu.roll(two, (turn + half) % X, 1), 0.0)
+            flip[pl.ds(base + j, CZ, stride=CY), :] = v
         oc_ref[:, t * X:(t + 1) * X] = flip[base:base + CZ * CY, :]
     comm.finish()
 
@@ -681,9 +729,9 @@
         return pltpu.VMEM(shape, f32)
 
     block = (Y, Z, X)
-    assert Y * SLOTS <= X and 4 * CY <= X // 2
+    assert Y * SLOTS <= X and CY * SLOTS <= X // 2
     nsx, nsy = len(strides_of(X)), len(strides_of(Y))
-    sends = 3 + (ny - 1) * 3 + (nx - 1) * 3 + 8 * 2
+    sends = 3 + (ny - 1) * 3 + (nx - 1) * 3 + 8 + 6 + 2
     dma = pltpu.SemaphoreType.DMA
     scratch = (
         [vm(*block) for _ in range(12)]
@@ -693,9 +741,10 @@
         + [vm(ny, 3, Z, X), vm(3, Z, X), vm(2, ny, Z, X), vm(2, 2, Z, X)]
         + [vm(1, Z, X)] + [vm(nx, Z, X) for _ in range(8)] + [vm(4, Z, X)]
         + [vm(ny, Z, X) for _ in range(6)] + [vm(6, Z, X), vm(2, Z, X)]
-        + [vm(CY * Z, X), vm(2, CY, CZ, X), vm(3, 2, CY + 5, CZ, X), vm(2, 2, CZ, X), vm(2, 2, CZ, X),
-           vm(2, 3, CZ, X), vm(CZ, X), vm(CY // 2, CZ, X), vm(nx, CY // 2, CZ, X), vm((nx // 2 + 1) * CZ * CY, X)]
-        + [dma((sends,)), dma((3,)), dma((2, nx)), dma((ny,)), dma((2, ny)), dma((3, 3)), dma((3, 3)), dma((nx,))]
+        + [vm(3, (CY + 4) * Z, X), pltpu.VMEM((4 * X, X), jnp.bfloat16), vm(2, CY, CZ, X), vm(3, 2, CY + 5, CZ, X),
+           vm(CY + 4, 8, Z, X), vm(CY + 4, CZ, X), vm(2, Z, X), vm(2, Z, X),
+           vm(2, CZ, X), vm(CZ, X), vm(CY // 2 + 1, CZ, X), vm(nx, CY // 2 + 1, CZ, X), vm((nx // 2 + 1) * CZ * CY, X)]
+        + [dma((sends,)), dma((3,)), dma((2, nx)), dma((ny,)), dma((2, ny)), dma((3, 3)), dma((2,)), dma((3, 2)), dma((nx,))]
         + [vm(6, Z * Y, X), dma((6,))]
     )
     p, r, c = pl.pallas_call(

time: 34 us -> 31.1 us (0.915)
  Pallas kernels: 33.2 us -> 30.3 us
    pallas_call x1, Pallas kernels: 32.5 us -> 29.6 us  [body(): pl.pallas_call(functools.partial(kernel, nx, ny), out_shape=(vm(Z * Y, X)...]
where the time goes in v2:
time: 31.1 us; the launch traced here: 30.9 us
  Pallas kernels  30.3 us (97%)
  between operations  0.64 us (2%)
    pallas_call x1, Pallas kernels, body(): pl.pallas_call(functools.partial(kernel, nx, ny), out_shape=(vm(Z * Y, X)...  29.6 us
    pallas_call x1, Pallas kernels, body(): pl.pallas_call(put, out_shape=tuple((jax.ShapeDtypeStruct(v.shape, f32) f...  0.71 us

profile of v2, /device:TPU:0, one launch (start us, length us, event | category | flops | bytes accessed | tf_op | source)
XLA Modules:
  0.0 30.9 jit_solution(3561253516622878493)
XLA Ops:
  0.6 29.6 %shard_map.85 = (f32[256,128]{1,0:T(8,128)S(1)}, f32[64,64]{1,0:T(8,128)S(1)}, f32[64,256]{1,0:T(8,128)S(1)}) custom-call(f32[256,128]{1,0:T(8,128)} %bitcast.9, f32[256,128]{1,0:T(8,128)} %bitcast.10, f32[256,128]{1,0:T(8,128)} %bitcast.11, f32[256,128]{1,0:T(8,128)} %bitcast.12, f32[256,128]{1,0:T(8,128)} %bitcast.13, f32[256,128]{1,0:T(8,128)} %bitcast.14), custom_call_target="tpu_custom_call" | custom-call | tf_op jit(solution)/shard_map/pallas_call | solution.py:750
  30.2 0.7 %shard_map.86 = (f32[256,128]{1,0:T(8,128)}, f32[64,64]{1,0:T(8,128)}, f32[64,256]{1,0:T(8,128)}) custom-call(f32[256,128]{1,0:T(8,128)S(1)} %get-tuple-element.9.refs_0_, f32[64,64]{1,0:T(8,128)S(1)} %get-tuple-element.10.refs_1_, f32[64,256]{1,0:T(8,128)S(1)} %get-tuple-element.11.refs_2_), custom_call_target="tpu_custom_call" | custom-call | tf_op jit(solution)/shard_map/pallas_call | solution.py:764

commit v3 on v2

--- a/solution.py
+++ b/solution.py
@@ -9,7 +9,6 @@
 
 COARSE = 3
 RELAX = 0.8
-CH = 4
 LE, LS, RE, RS, GS, GE, XC = range(7)
 SLOTS = 8
 MESH = pl.DeviceIdType.MESH
@@ -45,6 +44,7 @@
                 copy.wait_send()
             else:
                 pl.when(cond)(copy.wait_send)
+        self.pending = []
 
 
 def await_recv(src, dst, sems, recv, dev, cond=None):
@@ -155,7 +155,7 @@
 
 def kernel(nx, ny, f_hbm, p_hbm, x_hbm, y_hbm, z_hbm, d_hbm, op_ref, or_ref, oc_ref,
            xl_s, xc_s, yl_s, yc_s, zl_s, zt_s, zd_s, fo_s, p_s, r_s, g_s, q_s,
-           lx_s, rx_s, ix_s, wx_s, ly_s, ry_s, iy_s, wy_s,
+           ct_s, rt_s, gt_s, lx_s, rx_s, ix_s, wx_s, ly_s, ry_s, iy_s, wy_s,
            sx0, sy0, hx, hyd, hyu, xb, sxb, xb1, sx1, ycb, syc, yb, shy,
            xown, xrho, xtau, xsig, xbet, xtau2, xsig2, xscl, xdlt, xkk,
            ytau, ysig, ybet, ytau2, ysig2, ydlt, ykk, ysc,
@@ -173,10 +173,10 @@
     y_peers = flipped(gy, ny)
 
     loads = []
-    for m, ref in enumerate((x_hbm, y_hbm, p_hbm, z_hbm, d_hbm, f_hbm)):
+    for m, ref in enumerate((y_hbm, p_hbm, x_hbm, z_hbm, d_hbm, f_hbm)):
         loads.append(pltpu.make_async_copy(ref, ins.at[m], sin.at[m]))
         loads[m].start()
-    x_ref, y_ref, p_ref, z_ref, d_ref, f_ref = [ins.at[m] for m in range(6)]
+    y_ref, p_ref, x_ref, z_ref, d_ref, f_ref = [ins.at[m] for m in range(6)]
 
     barrier = pltpu.get_barrier_semaphore()
 
@@ -197,29 +197,30 @@
     lane = lax.broadcasted_iota(jnp.int32, (Z, X), 1)
     level = lax.broadcasted_iota(jnp.int32, (Z, X), 0)
     lane3 = lax.broadcasted_iota(jnp.int32, (1, 1, X), 2)
-    item, group = lane % SLOTS, lane // SLOTS
 
     def rows(ref, j):
         return ref[pl.ds(j, Z, stride=Y), :]
 
-    for m in range(3):
+    for m in range(2):
         loads[m].wait()
+    sy0[0] = rows(y_ref, Y - 1)
+    sy0[1] = rows(p_ref, Y - 1)
+    sy0[2] = rows(p_ref, 0)
+
+    n_corners = sum(cond.astype(jnp.int32) for cond, _ in corners)
+    pl.semaphore_wait(barrier, (nx - 1) + (ny - 1) + n_corners)
+
+    comm = Comm(ssem)
+    comm.send(sy0.at[0:2], hyd, s0.at[1], (gx, south), has_s)
+    comm.send(sy0.at[2:3], hyu, s0.at[2], (gx, north), has_n)
+
+    loads[2].wait()
     packed = jnp.zeros((Z, X), f32)
     for j in range(Y):
         v = rows(x_ref, j)
         xc_s[j] = v
         packed = jnp.where(lane == SLOTS * j + XC, v[:, X - 1:], packed)
     sx0[...] = packed
-    sy0[0] = rows(y_ref, Y - 1)
-    sy0[1] = rows(p_ref, Y - 1)
-    sy0[2] = rows(p_ref, 0)
-
-    n_corners = sum(cond.astype(jnp.int32) for cond, _ in corners)
-    pl.semaphore_wait(barrier, (nx - 1) + (ny - 1) + n_corners)
-
-    comm = Comm(ssem)
-    comm.send(sy0.at[0:2], hyd, s0.at[1], (gx, south), has_s)
-    comm.send(sy0.at[2:3], hyu, s0.at[2], (gx, north), has_n)
     comm.send(sx0, hx, s0.at[0], (east, gy), has_e)
 
     for j in range(Y):
@@ -235,24 +236,77 @@
         zd_s[j] = zv + zl + rows(d_ref, j)
         fo_s[j] = rows(f_ref, j)
 
-    first, last = lane3 == 0, lane3 == X - 1
-
-    def x_factor(lo, hi, above):
-        part = slice(lo, hi)
-        c = xc_s[part]
-        a = jnp.where(first, 1.0, pltpu.roll(c, 1, 2))
-        e = above + yc_s[part] + zd_s[part]
-        for n, s in enumerate(strides_of(X)):
-            low, high = lane3 >= s, lane3 < X - s
-            inv = 1.0 / (a + c + e)
-            ai, ci = a * inv, c * inv
-            am, cm = jnp.where(low, ai, 0.0), jnp.where(high, ci, 0.0)
-            wx_s[n, 0, part], wx_s[n, 1, part] = cm, am
-            a = a * jnp.where(low, pltpu.roll(ai, s, 2), 1.0)
-            c = c * jnp.where(high, pltpu.roll(ci, X - s, 2), 1.0)
-            e = e + pltpu.roll(cm * e, s, 2) + pltpu.roll(am * e, X - s, 2)
-        inv = 1.0 / (a + c + e)
-        ix_s[part], lx_s[part], rx_s[part] = inv, a * inv, c * inv
+    per, groups, blocks = X // Z, Y * Z // X, X // 8
+    sub = lax.broadcasted_iota(jnp.int32, (8, X), 0)
+
+    def turned(ref, g):
+        return ref[g * per:(g + 1) * per].reshape(X, X).T
+
+    def split(v):
+        return [v[8 * k:8 * k + 8] for k in range(blocks)]
+
+    def shift(v, s, fill):
+        if s % 8 == 0:
+            m = s // 8
+            return [v[k - m] if 0 <= k - m < blocks else fill for k in range(blocks)]
+        turn = [pltpu.roll(u, s % 8, 0) for u in v]
+        if s > 0:
+            return [jnp.where(sub < s, fill if k == 0 else turn[k - 1], turn[k]) for k in range(blocks)]
+        return [jnp.where(sub >= 8 + s, fill if k == blocks - 1 else turn[k + 1], turn[k]) for k in range(blocks)]
+
+    def scaled(u, v):
+        return [a if b is None else b if a is None else a * b for a, b in zip(u, v)]
+
+    def added(u, v):
+        return [a if b is None else a + b for a, b in zip(u, v)]
+
+    def fill_of(s, value):
+        return None if s % 8 == 0 else value
+
+    def store(ref, at, v):
+        for k in range(blocks):
+            ref[at + (slice(8 * k, 8 * k + 8),)] = v[k]
+
+    def load(ref, at):
+        return [ref[at + (slice(8 * k, 8 * k + 8),)] for k in range(blocks)]
+
+    xsteps = strides_of(X)
+
+    def x_factor(g):
+        c = load(ct_s, (g,))
+        a = shift(c, 1, 1.0)
+        for j in range(g * per, (g + 1) * per):
+            g_s[j] = yl_s[j] + yc_s[j] + zd_s[j]
+        e = split(turned(g_s, g))
+        for n, s in enumerate(xsteps):
+            inv = [1.0 / (u + v + w) for u, v, w in zip(a, c, e)]
+            ai, ci = scaled(a, inv), scaled(c, inv)
+            store(wx_s, (n, 0, g), ci)
+            store(wx_s, (n, 1, g), ai)
+            ae, ce = scaled(ai, e), scaled(ci, e)
+            a = scaled(a, shift(ai, s, fill_of(s, 1.0)))
+            c = scaled(c, shift(ci, -s, fill_of(s, 1.0)))
+            e = added(added(e, shift(ce, s, fill_of(s, 0.0))), shift(ae, -s, fill_of(s, 0.0)))
+        inv = [1.0 / (u + v + w) for u, v, w in zip(a, c, e)]
+        a, c = scaled(a, inv), scaled(c, inv)
+        store(ix_s, (g,), inv)
+        store(lx_s, (g,), a)
+        store(rx_s, (g,), c)
+        one = slice(g, g + 1)
+        sxb[LE, one], sxb[LS, one] = a[-1][7:8], a[0][0:1]
+        sxb[RE, one], sxb[RS, one] = c[-1][7:8], c[0][0:1]
+        sxb[XC, one] = ct_s[g, X - 1:X]
+
+    def edge_sums(g):
+        r = split(turned(r_s, g))
+        store(rt_s, (g,), r)
+        out = []
+        for ref in (lx_s, rx_s):
+            v = scaled(load(ref, (g,)), r)
+            while len(v) > 1:
+                v = [a + b for a, b in zip(v[0::2], v[1::2])]
+            out.append(jnp.sum(v[0], axis=0, keepdims=True))
+        return out
 
     def z_terms(v, part):
         return zl_s[part] * pltpu.roll(v, 1, 1) + zt_s[part] * pltpu.roll(v, Z - 1, 1)
@@ -261,28 +315,12 @@
         part = slice(lo, hi)
         r_s[part] = fo_s[part] + yl_s[part] * lower + yc_s[part] * upper + z_terms(p_s[part], part)
 
-    ends = jnp.logical_or(lane == 0, lane == X - 1)
-
-    def edge_sums(j):
-        r = r_s[j]
-        return jnp.sum(lx_s[j] * r, axis=1, keepdims=True), jnp.sum(rx_s[j] * r, axis=1, keepdims=True)
-
-    def pack_row(packed, j):
-        gs, ge = edge_sums(j)
-        v = jnp.where(ends, lx_s[j], pltpu.roll(rx_s[j], 2, 1))
-        v = jnp.where(item < GS, pltpu.roll(v, SLOTS * j + 1, 1), jnp.where(item == GS, gs, ge))
-        return jnp.where(group == j, v, packed)
-
+    for g in range(groups):
+        store(ct_s, (g,), split(turned(xc_s, g)))
     yl_s[1:Y] = yc_s[0:Y - 1]
-    packed = jnp.zeros((Z, X), f32)
-    for lo in range(0, Y, CH):
-        hi = lo + CH
-        at = max(lo, 1)
-        x_factor(at, hi, yl_s[at:hi])
-        at, to = max(lo, 1), min(hi, Y - 1)
-        x_source(at, to, p_s[at - 1:to - 1], p_s[at + 1:to + 1])
-        for j in range(at, to):
-            packed = pack_row(packed, j)
+    for g in range(1, groups):
+        x_factor(g)
+    x_source(1, Y - 1, p_s[0:Y - 2], p_s[2:Y])
 
     @pl.when(jnp.logical_not(has_w))
     def _():
@@ -318,6 +356,16 @@
     await_recv(sy0.at[2:3], hyu, ssem, s0.at[2], (gx, north), has_s)
 
     yl_s[0] = hyd[0]
+    x_factor(0)
+    x_source(0, 1, hyd[1:2], p_s[1:2])
+    x_source(Y - 1, Y, p_s[Y - 2:Y - 1], hyu[0:1])
+    for g in range(groups):
+        one = slice(g, g + 1)
+        sxb[GS, one], sxb[GE, one] = edge_sums(g)
+    xb[gx] = sxb[...]
+    for i in x_peers:
+        comm.send(sxb, xb.at[gx], sx.at[0, gx], (i, gy))
+
     for j in range(Y):
         xl_s[j] = jnp.where(lane == 0, hx[:, SLOTS * j + XC:SLOTS * j + XC + 1], pltpu.roll(xc_s[j], 1, 1))
 
@@ -358,24 +406,14 @@
     for j in y_peers:
         comm.send(syc, ycb.at[gy], syco.at[gy], (gx, j))
 
-    x_factor(0, 1, yl_s[0:1])
-    x_source(0, 1, hyd[1:2], p_s[1:2])
-    x_source(Y - 1, Y, p_s[Y - 2:Y - 1], hyu[0:1])
-    for lo in range(0, Y, Y - 1):
-        packed = pack_row(packed, lo)
-    packed = jnp.where(item == XC, sx0[...], packed)
-    sxb[...] = packed
-    xb[gx] = packed
-    for i in x_peers:
-        comm.send(sxb, xb.at[gx], sx.at[0, gx], (i, gy))
-
     def x_local():
-        for lo in range(0, Y, CH):
-            part = slice(lo, lo + CH)
-            r = r_s[part]
-            for n, s in enumerate(strides_of(X)):
-                r = r + pltpu.roll(wx_s[n, 0, part] * r, s, 2) + pltpu.roll(wx_s[n, 1, part] * r, X - s, 2)
-            g_s[part] = r * ix_s[part]
+        for g in range(groups):
+            r = load(rt_s, (g,))
+            for n, s in enumerate(xsteps):
+                low = shift(scaled(load(wx_s, (n, 0, g)), r), s, fill_of(s, 0.0))
+                high = shift(scaled(load(wx_s, (n, 1, g)), r), -s, fill_of(s, 0.0))
+                r = added(added(r, low), high)
+            store(gt_s, (g,), scaled(r, load(ix_s, (g,))))
 
     def y_local():
         for lo in range(0, Z, 8):
@@ -477,17 +515,11 @@
             for src, lo, n, kind, slot, back, dev, _, ok in parts:
                 await_recv(src, rows_of(slot, lo, n), ssem, sc.at[kind, slot], dev, ok)
 
-    def slot(v, k):
-        return v if k == 0 else pltpu.roll(v, X - k, 1)
-
-    def expand(v):
-        return jnp.concatenate([v, pltpu.roll(v, X - 1, 1)], axis=0)
-
     def x_solve(hl, hr, gs, ge):
-        alpha = jnp.zeros((Z, X), f32)
+        alpha = jnp.zeros((groups, X), f32)
         for d in range(nx - 1):
             alpha = jnp.where(d < gx, hl(d) + xtau[d] * alpha, alpha)
-        gamma = jnp.zeros((Z, X), f32)
+        gamma = jnp.zeros((groups, X), f32)
         for d in reversed(range(1, nx)):
             gamma = jnp.where(d > gx, hr(d) + xtau2[d] * gamma, gamma)
         p = xrho[gx] * alpha + xbet[gx] * gs
@@ -497,9 +529,8 @@
     def x_first():
         for i in x_peers:
             await_recv(sxb, xb.at[i], ssem, sx.at[0, i], (i, gy))
-        tiles = [xb[d] for d in range(nx)]
-        cut = [[slot(t, k) for t in tiles] for k in range(SLOTS - 1)]
-        own = [slot(sxb[...], k) for k in range(SLOTS - 1)]
+        cut = [[xb[d, k] for d in range(nx)] for k in range(XC + 1)]
+        own = [sxb[k] for k in range(XC + 1)]
         inv = [1.0 / v for v in cut[XC]]
         ge = [cut[GE][d] * inv[d] for d in range(nx)]
         gs = cut[GS]
@@ -511,35 +542,36 @@
         )
 
     def x_second():
-        packed = jnp.zeros((Z, X), f32)
-        for j in range(Y):
-            gs, ge = edge_sums(j)
-            packed = jnp.where(group == j, jnp.where(item == 0, gs, ge), packed)
-        gs, ge = packed, pltpu.roll(packed, X - 1, 1) * xown[0]
-        for side, h in enumerate((ge + xsig[gx] * gs, xscl[gx] * gs + xsig2[gx] * ge)):
-            sx1[side] = jnp.where(item[:CZ] == 0, h[:CZ], pltpu.roll(h[CZ:], 1, 1))
+        sums = [edge_sums(g) for g in range(groups)]
+        gs, ge = [jnp.concatenate([v[n] for v in sums], axis=0) for n in range(2)]
+        ge = ge * xown[0]
+        sx1[0], sx1[1] = ge + xsig[gx] * gs, xscl[gx] * gs + xsig2[gx] * ge
         for i in x_peers:
             comm.send(sx1.at[jnp.where(i > gx, 0, 1)], xb1.at[gx], sx.at[1, gx], (i, gy))
+        coarse_send(False)
         to_rows(wbuf, sw.at[0], True)
-        coarse_send(False)
         x_local()
         for i in x_peers:
             await_recv(sx1.at[0], xb1.at[i], ssem, sx.at[1, i], (i, gy))
-        return x_solve(lambda d: expand(xb1[d]), lambda d: expand(xb1[d]), gs, ge)
+        return x_solve(lambda d: xb1[d], lambda d: xb1[d], gs, ge)
 
     def y_half(m, left, right):
         top, end = jnp.zeros((Z, X), f32), jnp.zeros((Z, X), f32)
-        for j in range(Y):
-            u = jnp.broadcast_to(left[:, SLOTS * j:SLOTS * j + 1], (Z, X))
-            w = jnp.broadcast_to(right[:, SLOTS * j:SLOTS * j + 1], (Z, X))
-            v = g_s[j] + lx_s[j] * u + rx_s[j] * w
-            q_s[j] = v
-            before = jnp.where(lane == 0, v, pltpu.roll(v, 1, 1))
-            after = jnp.where(lane == X - 1, w, pltpu.roll(v, X - 1, 1))
-            r = fo_s[j] + xl_s[j] * before + xc_s[j] * after + jnp.where(lane == 0, u - v, 0.0)
-            r = r + zl_s[j] * pltpu.roll(v, 1, 0) + zt_s[j] * pltpu.roll(v, Z - 1, 0)
-            r_s[j] = r
-            top, end = top + ly_s[j] * r, end + ry_s[j] * r
+        for g in range(groups):
+            u, w = left[g:g + 1], right[g:g + 1]
+            c, v = load(ct_s, (g,)), []
+            for a, b, d in zip(load(gt_s, (g,)), load(lx_s, (g,)), load(rx_s, (g,))):
+                v.append(a + b * u + d * w)
+            edge = u + (xrho[gx][g:g + 1] - 1.0) * v[0][0:1]
+            t = added(shift(scaled(c, v), 1, edge), scaled(c, shift(v, -1, w)))
+            v = jnp.concatenate(v, axis=0).T.reshape(per, Z, X)
+            t = jnp.concatenate(t, axis=0).T.reshape(per, Z, X)
+            for n in range(per):
+                j = g * per + n
+                q_s[j] = v[n]
+                r = fo_s[j] + t[n] + zl_s[j] * pltpu.roll(v[n], 1, 0) + zt_s[j] * pltpu.roll(v[n], Z - 1, 0)
+                r_s[j] = r
+                top, end = top + ly_s[j] * r, end + ry_s[j] * r
         top, end = top * ysc[0], end * ysc[1]
         if m == 0:
             for j in y_peers:
@@ -624,8 +656,8 @@
     left, right = x_first()
     above, below = y_half(0, left, right)
     p_s[...] = g_s[...] + ly_s[...] * above[None] + ry_s[...] * below[None]
-    for lo in range(0, Y, CH):
-        hi = lo + CH
+    for lo in range(0, Y, 4):
+        hi = lo + 4
         lower = jnp.concatenate([above[None], p_s[0:hi - 1]], axis=0) if lo == 0 else p_s[lo - 1:hi - 1]
         upper = jnp.concatenate([p_s[lo + 1:Y], below[None]], axis=0) if hi == Y else p_s[lo + 1:hi + 1]
         x_source(lo, hi, lower, upper)
@@ -652,6 +684,9 @@
             edge = jnp.where(inner >= SLOTS * r, pltpu.roll(v[r], half - off + 3 + SLOTS * r, 1), edge)
         return edge
 
+    sedge[...] = fringe(res[2:CY + 2])
+    comm.send(sedge, ebuf.at[1], sr.at[1], (west, gy), has_w)
+    comm.send(sedge, ebuf.at[0], sr.at[0], (east, gy), has_e)
     cor = scale * res
     for repeat in range(COARSE - 1):
         lo, n = 1 + repeat, H - 2 - 2 * repeat
@@ -673,12 +708,10 @@
     fbuf[gx] = fown[...]
     for i in x_peers:
         comm.send(fown, fbuf.at[gx], sf.at[gx], (i, gy))
-    sedge[...] = fringe(res[2:CY + 2])
-    comm.send(sedge, ebuf.at[1], sr.at[1], (west, gy), has_w)
-    comm.send(sedge, ebuf.at[0], sr.at[0], (east, gy), has_e)
     above, below = above * ysc[0], below * ysc[1]
     for j in range(Y):
         op_ref[pl.ds(j, Z, stride=Y), :] = g_s[j] + ly_s[j] * above + ry_s[j] * below
+    comm.finish()
     await_recv(sedge, ebuf.at[0], ssem, sr.at[0], (west, gy), has_w)
     await_recv(sedge, ebuf.at[1], ssem, sr.at[1], (east, gy), has_e)
     both = jnp.where(clane < half, ebuf[0], ebuf[1])
@@ -728,18 +761,18 @@
     def vm(*shape):
         return pltpu.VMEM(shape, f32)
 
-    block = (Y, Z, X)
-    assert Y * SLOTS <= X and CY * SLOTS <= X // 2
+    block, square, groups = (Y, Z, X), (Y * Z // X, X, X), Y * Z // X
+    assert Y * SLOTS <= X and CY * SLOTS <= X // 2 and X % Z == 0 and Y * Z % X == 0 and X % 8 == 0
     nsx, nsy = len(strides_of(X)), len(strides_of(Y))
     sends = 3 + (ny - 1) * 3 + (nx - 1) * 3 + 8 + 6 + 2
     dma = pltpu.SemaphoreType.DMA
     scratch = (
         [vm(*block) for _ in range(12)]
-        + [vm(*block), vm(*block), vm(*block), vm(nsx, 2, *block), vm(*block), vm(*block), vm(*block), vm(nsy, 2, *block)]
+        + [vm(*square) for _ in range(6)] + [vm(nsx, 2, *square), vm(*block), vm(*block), vm(*block), vm(nsy, 2, *block)]
         + [vm(Z, X), vm(3, Z, X), vm(Z, X), vm(2, Z, X), vm(1, Z, X)]
-        + [vm(nx, Z, X), vm(Z, X), vm(nx, CZ, X), vm(2, CZ, X)]
+        + [vm(nx, XC + 1, groups, X), vm(XC + 1, groups, X), vm(nx, groups, X), vm(2, groups, X)]
         + [vm(ny, 3, Z, X), vm(3, Z, X), vm(2, ny, Z, X), vm(2, 2, Z, X)]
-        + [vm(1, Z, X)] + [vm(nx, Z, X) for _ in range(8)] + [vm(4, Z, X)]
+        + [vm(1, groups, X)] + [vm(nx, groups, X) for _ in range(8)] + [vm(4, groups, X)]
         + [vm(ny, Z, X) for _ in range(6)] + [vm(6, Z, X), vm(2, Z, X)]
         + [vm(3, (CY + 4) * Z, X), pltpu.VMEM((4 * X, X), jnp.bfloat16), vm(2, CY, CZ, X), vm(3, 2, CY + 5, CZ, X),
            vm(CY + 4, 8, Z, X), vm(CY + 4, CZ, X), vm(2, Z, X), vm(2, Z, X),

time: 31.1 us -> 29.8 us (0.958)
  Pallas kernels: 30.3 us -> 29.1 us
    pallas_call x1, Pallas kernels: 29.6 us -> 28.3 us  [body(): pl.pallas_call(functools.partial(kernel, nx, ny), out_shape=(vm(Z * Y, X)...]
where the time goes in v3:
time: 29.8 us; the launch traced here: 29.7 us
  Pallas kernels  29.1 us (98%)
  between operations  0.64 us (2%)
    pallas_call x1, Pallas kernels, body(): pl.pallas_call(functools.partial(kernel, nx, ny), out_shape=(vm(Z * Y, X)...  28.3 us
    pallas_call x1, Pallas kernels, body(): pl.pallas_call(put, out_shape=tuple((jax.ShapeDtypeStruct(v.shape, f32) f...  0.71 us

profile of v3, /device:TPU:0, one launch (start us, length us, event | category | flops | bytes accessed | tf_op | source)
XLA Modules:
  0.0 29.7 jit_solution(6462755051465757999)
XLA Ops:
  0.6 28.3 %shard_map.85 = (f32[256,128]{1,0:T(8,128)S(1)}, f32[64,64]{1,0:T(8,128)S(1)}, f32[64,256]{1,0:T(8,128)S(1)}) custom-call(f32[256,128]{1,0:T(8,128)} %bitcast.9, f32[256,128]{1,0:T(8,128)} %bitcast.10, f32[256,128]{1,0:T(8,128)} %bitcast.11, f32[256,128]{1,0:T(8,128)} %bitcast.12, f32[256,128]{1,0:T(8,128)} %bitcast.13, f32[256,128]{1,0:T(8,128)} %bitcast.14), custom_call_target="tpu_custom_call" | custom-call | tf_op jit(solution)/shard_map/pallas_call | solution.py:783
  29.0 0.7 %shard_map.86 = (f32[256,128]{1,0:T(8,128)}, f32[64,64]{1,0:T(8,128)}, f32[64,256]{1,0:T(8,128)}) custom-call(f32[256,128]{1,0:T(8,128)S(1)} %get-tuple-element.9.refs_0_, f32[64,64]{1,0:T(8,128)S(1)} %get-tuple-element.10.refs_1_, f32[64,256]{1,0:T(8,128)S(1)} %get-tuple-element.11.refs_2_), custom_call_target="tpu_custom_call" | custom-call | tf_op jit(solution)/shard_map/pallas_call | solution.py:797

commit v4 on v3

--- a/solution.py
+++ b/solution.py
@@ -11,6 +11,7 @@
 RELAX = 0.8
 LE, LS, RE, RS, GS, GE, XC = range(7)
 SLOTS = 8
+EDGE = 4
 MESH = pl.DeviceIdType.MESH
 
 
@@ -26,11 +27,13 @@
     def __init__(self, send_sems):
         self.sems, self.used, self.pending = send_sems, 0, []
 
+    def copy(self, src, dst, sem, recv, dev):
+        return pltpu.make_async_remote_copy(
+            src_ref=src, dst_ref=dst, send_sem=sem, recv_sem=recv, device_id=dev, device_id_type=MESH
+        )
+
     def send(self, src, dst, recv, dev, cond=None):
-        copy = pltpu.make_async_remote_copy(
-            src_ref=src, dst_ref=dst, send_sem=self.sems.at[self.used], recv_sem=recv,
-            device_id=dev, device_id_type=MESH,
-        )
+        copy = self.copy(src, dst, self.sems.at[self.used], recv, dev)
         self.used += 1
         self.pending.append((copy, cond))
         if cond is None:
@@ -38,13 +41,20 @@
         else:
             pl.when(cond)(copy.start)
 
+    def send_all(self, src, dst, recv, devs, received):
+        sem = self.sems.at[self.used]
+        self.used += 1
+        for dev in devs:
+            self.copy(src(dev), dst, sem, recv, dev).start()
+        self.pending.append((self.copy(received, received, sem, recv, devs[0]), None))
+
     def finish(self):
         for copy, cond in self.pending:
             if cond is None:
                 copy.wait_send()
             else:
                 pl.when(cond)(copy.wait_send)
-        self.pending = []
+        self.used, self.pending = 0, []
 
 
 def await_recv(src, dst, sems, recv, dev, cond=None):
@@ -57,6 +67,12 @@
         pl.when(cond)(copy.wait_recv)
 
 
+def await_all(part, recv, dev):
+    pltpu.make_async_remote_copy(
+        src_ref=part, dst_ref=part, send_sem=recv, recv_sem=recv, device_id=dev, device_id_type=MESH
+    ).wait_recv()
+
+
 def farthest_first(me, n):
     out = []
     for k in range(n - 1):
@@ -69,15 +85,18 @@
 def flipped(me, n):
     if n & (n - 1):
         return [lax.rem(me + o, n) for o in range(1, n)]
-    out = []
-    for mask in range(n - 1, 0, -1):
+    def peer_of(mask):
         peer, bit = 0, 1
         while bit < n:
             value = lax.rem(me // bit, 2)
             peer = peer + bit * (1 - value if mask & bit else value)
             bit *= 2
-        out.append(peer)
-    return out
+        return peer
+
+    masks = list(range(n - 1, 0, -1))
+    even, odd = [m for m in masks if m % 2 == 0], [m for m in masks if m % 2]
+    first = lax.rem(me, 2) == 0
+    return [jnp.where(first, peer_of(a), peer_of(b)) for a, b in zip(even + odd, odd + even)]
 
 
 def interface_factor(n, me, ls, le, rs, re, own, tau, sig, bet, tau2, sig2, dlt, kk):
@@ -156,11 +175,11 @@
 def kernel(nx, ny, f_hbm, p_hbm, x_hbm, y_hbm, z_hbm, d_hbm, op_ref, or_ref, oc_ref,
            xl_s, xc_s, yl_s, yc_s, zl_s, zt_s, zd_s, fo_s, p_s, r_s, g_s, q_s,
            ct_s, rt_s, gt_s, lx_s, rx_s, ix_s, wx_s, ly_s, ry_s, iy_s, wy_s,
-           sx0, sy0, hx, hyd, hyu, xb, sxb, xb1, sx1, ycb, syc, yb, shy,
+           sx0, sy0, hx, hyd, hyu, xb, sxb, xb1, sx1, ycb, syc, yb0, yb1, shy,
            xown, xrho, xtau, xsig, xbet, xtau2, xsig2, xscl, xdlt, xkk,
            ytau, ysig, ybet, ytau2, ysig2, ydlt, ykk, ysc,
-           pair_s, sel_s, cown, cbuf, wbuf, pbuf, sxt, xtr, ebuf, sedge, fown, fbuf, flip,
-           ssem, s0, sx, syco, sy, sc, sr, sw, sf, ins, sin):
+           pair_s, sel_s, cown, cbuf, wbuf, elr, nbr, pbuf, sxt, xtr, ebuf, sedge, fown, fbuf, flip,
+           ssem, s0, sx, sy, sc, sr, sw, sf, ins, sin):
     Y, Z, X = xc_s.shape
     CY, CZ = Y // 2, Z // 2
     f32 = jnp.float32
@@ -169,13 +188,19 @@
     has_n, has_s = gy > 0, gy < ny - 1
     west, east = jnp.maximum(gx - 1, 0), jnp.minimum(gx + 1, nx - 1)
     north, south = jnp.maximum(gy - 1, 0), jnp.minimum(gy + 1, ny - 1)
-    x_peers = farthest_first(gx, nx)
-    y_peers = flipped(gy, ny)
-
-    loads = []
-    for m, ref in enumerate((y_hbm, p_hbm, x_hbm, z_hbm, d_hbm, f_hbm)):
-        loads.append(pltpu.make_async_copy(ref, ins.at[m], sin.at[m]))
-        loads[m].start()
+    x_peers = [(i, gy) for i in farthest_first(gx, nx)]
+    y_peers = [(gx, j) for j in flipped(gy, ny)]
+
+    stages = ((0, 2), (2, 3), (3, 6))
+    sources = (y_hbm, p_hbm, x_hbm, z_hbm, d_hbm, f_hbm)
+    for n, (lo, hi) in enumerate(stages):
+        for m in range(lo, hi):
+            pltpu.make_async_copy(sources[m], ins.at[m], sin.at[n]).start()
+
+    def loaded(n):
+        part = ins.at[pl.ds(stages[n][0], stages[n][1] - stages[n][0])]
+        pltpu.make_async_copy(part, part, sin.at[n]).wait()
+
     y_ref, p_ref, x_ref, z_ref, d_ref, f_ref = [ins.at[m] for m in range(6)]
 
     barrier = pltpu.get_barrier_semaphore()
@@ -183,10 +208,8 @@
     def greet(dev):
         pl.semaphore_signal(barrier, inc=1, device_id=dev, device_id_type=MESH)
 
-    for i in x_peers:
-        greet((i, gy))
-    for j in y_peers:
-        greet((gx, j))
+    for dev in x_peers + y_peers:
+        greet(dev)
 
     corners = [
         (jnp.logical_and(h, v), (i, j)) for h, i in ((has_w, west), (has_e, east)) for v, j in ((has_n, north), (has_s, south))
@@ -201,8 +224,7 @@
     def rows(ref, j):
         return ref[pl.ds(j, Z, stride=Y), :]
 
-    for m in range(2):
-        loads[m].wait()
+    loaded(0)
     sy0[0] = rows(y_ref, Y - 1)
     sy0[1] = rows(p_ref, Y - 1)
     sy0[2] = rows(p_ref, 0)
@@ -214,7 +236,7 @@
     comm.send(sy0.at[0:2], hyd, s0.at[1], (gx, south), has_s)
     comm.send(sy0.at[2:3], hyu, s0.at[2], (gx, north), has_n)
 
-    loads[2].wait()
+    loaded(1)
     packed = jnp.zeros((Z, X), f32)
     for j in range(Y):
         v = rows(x_ref, j)
@@ -226,8 +248,7 @@
     for j in range(Y):
         yc_s[j] = rows(y_ref, j)
         p_s[j] = rows(p_ref, j)
-    for m in range(3, 6):
-        loads[m].wait()
+    loaded(2)
     for j in range(Y):
         zv = jnp.where(level < Z - 1, rows(z_ref, j), 0.0)
         zt_s[j] = zv
@@ -235,6 +256,12 @@
         zl_s[j] = zl
         zd_s[j] = zv + zl + rows(d_ref, j)
         fo_s[j] = rows(f_ref, j)
+
+    to_sides = (((gx, south), has_s, has_n), ((gx, north), has_n, has_s))
+    for n, (dev, there, _) in enumerate(to_sides):
+        for k, ref in enumerate((xc_s, zt_s)):
+            src = ref.at[pl.ds(0 if n else Y - EDGE, EDGE)]
+            comm.send(src, nbr.at[n, pl.ds(k * EDGE, EDGE)], sw.at[0, n], dev, there)
 
     per, groups, blocks = X // Z, Y * Z // X, X // 8
     sub = lax.broadcasted_iota(jnp.int32, (8, X), 0)
@@ -336,7 +363,7 @@
     @pl.when(jnp.logical_not(has_n))
     def _():
         hyd[...] = jnp.zeros_like(hyd)
-        wbuf[0:2] = jnp.zeros_like(wbuf[0:2])
+        nbr[0] = jnp.zeros_like(nbr[0])
         pbuf[0:2] = jnp.zeros_like(pbuf[0:2])
         xtr[0] = jnp.zeros_like(xtr[0])
         for d in range(3):
@@ -345,13 +372,12 @@
     @pl.when(jnp.logical_not(has_s))
     def _():
         hyu[...] = jnp.zeros_like(hyu)
-        wbuf[CY + 2:] = jnp.zeros_like(wbuf[CY + 2:])
+        nbr[1] = jnp.zeros_like(nbr[1])
         pbuf[CY + 2:] = jnp.zeros_like(pbuf[CY + 2:])
         xtr[1] = jnp.zeros_like(xtr[1])
         for d in range(3):
             cbuf[d, :, 3 + CY:] = jnp.zeros_like(cbuf[d, :, 3 + CY:])
 
-    await_recv(sx0, hx, ssem, s0.at[0], (east, gy), has_w)
     await_recv(sy0.at[0:2], hyd, ssem, s0.at[1], (gx, south), has_n)
     await_recv(sy0.at[2:3], hyu, ssem, s0.at[2], (gx, north), has_s)
 
@@ -363,9 +389,9 @@
         one = slice(g, g + 1)
         sxb[GS, one], sxb[GE, one] = edge_sums(g)
     xb[gx] = sxb[...]
-    for i in x_peers:
-        comm.send(sxb, xb.at[gx], sx.at[0, gx], (i, gy))
-
+    comm.send_all(lambda dev: sxb, xb.at[gx], sx.at[0], x_peers, xb.at[pl.ds(0, nx - 1)])
+
+    await_recv(sx0, hx, ssem, s0.at[0], (east, gy), has_w)
     for j in range(Y):
         xl_s[j] = jnp.where(lane == 0, hx[:, SLOTS * j + XC:SLOTS * j + XC + 1], pltpu.roll(xc_s[j], 1, 1))
 
@@ -403,8 +429,7 @@
     ysc[0], ysc[1] = i_top, 1.0 / k_end
     syc[0], syc[1], syc[2] = ly_s[0], ly_s[Y - 1] * k_end * i_top, ry_s[Y - 1]
     ycb[gy] = syc[...]
-    for j in y_peers:
-        comm.send(syc, ycb.at[gy], syco.at[gy], (gx, j))
+    comm.send_all(lambda dev: syc, ycb.at[gy], sy.at[2], y_peers, ycb.at[pl.ds(0, ny - 1)])
 
     def x_local():
         for g in range(groups):
@@ -470,15 +495,38 @@
         cown[m] = part
         cbuf[1, m, 3:3 + CY] = part
 
+    def operator(at, xc, xl, zl, zt, sides):
+        for n, (u, v) in enumerate(sides):
+            wbuf[at, n] = xc[0] * u + xc[1] * v
+            wbuf[at, 2 + n] = xl[0] * u + xl[1] * v
+            wbuf[at, 4 + n] = zl[0] * pltpu.roll(u, 1, 0) + zl[1] * pltpu.roll(v, 1, 0)
+            wbuf[at, 6 + n] = zt[0] * pltpu.roll(u, Z - 1, 0) + zt[1] * pltpu.roll(v, Z - 1, 0)
+
+    for k in range(EDGE):
+        for n, j in enumerate((Y - EDGE + k, k)):
+            elr[n, k], elr[n, EDGE + k] = ly_s[j] * ysc[0], ry_s[j] * ysc[1]
+    for n in range(2):
+        elr[n, 2 * EDGE] = hx[...]
     for k in range(CY):
-        j = 2 * k
-        for n, (g, scale) in enumerate(((ly_s, ysc[0]), (ry_s, ysc[1]))):
-            u, v = g[j] * scale, g[j + 1] * scale
-            at = 2 + k
-            wbuf[at, n] = xc_s[j] * u + xc_s[j + 1] * v
-            wbuf[at, 2 + n] = xl_s[j] * u + xl_s[j + 1] * v
-            wbuf[at, 4 + n] = zl_s[j] * pltpu.roll(u, 1, 0) + zl_s[j + 1] * pltpu.roll(v, 1, 0)
-            wbuf[at, 6 + n] = zt_s[j] * pltpu.roll(u, Z - 1, 0) + zt_s[j + 1] * pltpu.roll(v, Z - 1, 0)
+        two = (2 * k, 2 * k + 1)
+        operator(2 + k, *[[ref[j] for j in two] for ref in (xc_s, xl_s, zl_s, zt_s)],
+                 [[ref[j] * ysc[n] for j in two] for n, ref in enumerate((ly_s, ry_s))])
+
+    def edge_columns():
+        for n, (dev, there, _) in enumerate(to_sides):
+            comm.send(elr.at[n], nbr.at[n, pl.ds(2 * EDGE, 2 * EDGE + 1)], sw.at[0, n], dev, there)
+
+    def edge_operators():
+        for n, (dev, _, here) in enumerate(to_sides):
+            await_recv(nbr.at[n], nbr.at[n], ssem, sw.at[0, n], dev, here)
+        for n, first in enumerate((Y - EDGE, 0)):
+            for k in range(0, EDGE, 2):
+                xc = [nbr[n, k + i] for i in range(2)]
+                zt = [nbr[n, EDGE + k + i] for i in range(2)]
+                cols = [SLOTS * (first + k + i) + XC for i in range(2)]
+                xl = [jnp.where(lane == 0, nbr[n, 4 * EDGE, :, c:c + 1], pltpu.roll(v, 1, 1)) for c, v in zip(cols, xc)]
+                operator(n * (CY + 2) + k // 2, xc, xl, [pltpu.roll(v, 1, 0) for v in zt], zt,
+                         [[nbr[n, (2 + m) * EDGE + k + i] for i in range(2)] for m in range(2)])
 
     def to_rows(buf, sems, starting):
         for n, (dev, there, here) in enumerate((((gx, north), has_n, has_s), ((gx, south), has_s, has_n))):
@@ -489,31 +537,24 @@
             else:
                 await_recv(src, dst, ssem, sems.at[n], dev, here)
 
-    def coarse_parts(straight):
-        def rows_of(slot, lo, n):
-            return cbuf.at[slot, :, pl.ds(lo, n)]
-
-        out = []
-        for slot, i, ok, back in ((0, west, has_w, 2), (1, gx, None, 1), (2, east, has_e, 0)):
-            both_ok = (lambda c: c) if ok is None else (lambda c, ok=ok: jnp.logical_and(c, ok))
+    def coarse_send(straight):
+        for i, ok, back in ((west, has_w, 2), (gx, None, 1), (east, has_e, 0)):
+            both = (lambda c: c) if ok is None else (lambda c, ok=ok: jnp.logical_and(c, ok))
             if straight:
                 if ok is not None:
-                    out.append((cown, 3, CY, 0, slot, back, (i, gy), ok, ok))
+                    comm.send(cown, cbuf.at[back, :, pl.ds(3, CY)], sc.at[back], (i, gy), ok)
             else:
-                out.append((cown.at[:, pl.ds(CY - 3, 3)], 0, 3, 1, slot, back, (i, south), both_ok(has_s), both_ok(has_n)))
-                out.append((cown.at[:, pl.ds(0, 2)], 3 + CY, 2, 2, slot, back, (i, north), both_ok(has_n), both_ok(has_s)))
-        return rows_of, out
-
-    def coarse_send(straight):
-        rows_of, parts = coarse_parts(straight)
-        for src, lo, n, kind, slot, back, dev, ok, _ in parts:
-            comm.send(src, rows_of(back, lo, n), sc.at[kind, back], dev, ok)
+                comm.send(cown.at[:, pl.ds(CY - 3, 3)], cbuf.at[back, :, pl.ds(0, 3)], sc.at[back], (i, south), both(has_s))
+                comm.send(cown.at[:, pl.ds(0, 2)], cbuf.at[back, :, pl.ds(3 + CY, 2)], sc.at[back], (i, north), both(has_n))
 
     def coarse_wait():
-        for straight in (True, False):
-            rows_of, parts = coarse_parts(straight)
-            for src, lo, n, kind, slot, back, dev, _, ok in parts:
-                await_recv(src, rows_of(slot, lo, n), ssem, sc.at[kind, slot], dev, ok)
+        for slot, i, ok in ((0, west, has_w), (1, gx, None), (2, east, has_e)):
+            kept = 0 if ok is None else CY
+            for n, s in ((True, True), (True, False), (False, True)):
+                cond = jnp.logical_and(has_n if n else jnp.logical_not(has_n), has_s if s else jnp.logical_not(has_s))
+                cond = cond if ok is None else jnp.logical_and(cond, ok)
+                part = cbuf.at[slot, :, pl.ds(0, kept + (3 if n else 0) + (2 if s else 0))]
+                await_recv(part, part, ssem, sc.at[slot], (i, gy), cond)
 
     def x_solve(hl, hr, gs, ge):
         alpha = jnp.zeros((groups, X), f32)
@@ -527,8 +568,7 @@
         return xkk[0] * p + xkk[1] * q, xkk[2] * q + xkk[3] * p
 
     def x_first():
-        for i in x_peers:
-            await_recv(sxb, xb.at[i], ssem, sx.at[0, i], (i, gy))
+        await_all(xb.at[pl.ds(0, nx - 1)], sx.at[0], x_peers[0])
         cut = [[xb[d, k] for d in range(nx)] for k in range(XC + 1)]
         own = [sxb[k] for k in range(XC + 1)]
         inv = [1.0 / v for v in cut[XC]]
@@ -546,13 +586,13 @@
         gs, ge = [jnp.concatenate([v[n] for v in sums], axis=0) for n in range(2)]
         ge = ge * xown[0]
         sx1[0], sx1[1] = ge + xsig[gx] * gs, xscl[gx] * gs + xsig2[gx] * ge
-        for i in x_peers:
-            comm.send(sx1.at[jnp.where(i > gx, 0, 1)], xb1.at[gx], sx.at[1, gx], (i, gy))
+        comm.send_all(
+            lambda dev: sx1.at[jnp.where(dev[0] > gx, 0, 1)], xb1.at[gx], sx.at[1], x_peers, xb1.at[pl.ds(0, nx - 1)]
+        )
         coarse_send(False)
-        to_rows(wbuf, sw.at[0], True)
+        edge_columns()
         x_local()
-        for i in x_peers:
-            await_recv(sx1.at[0], xb1.at[i], ssem, sx.at[1, i], (i, gy))
+        await_all(xb1.at[pl.ds(0, nx - 1)], sx.at[1], x_peers[0])
         return x_solve(lambda d: xb1[d], lambda d: xb1[d], gs, ge)
 
     def y_half(m, left, right):
@@ -574,19 +614,16 @@
                 top, end = top + ly_s[j] * r, end + ry_s[j] * r
         top, end = top * ysc[0], end * ysc[1]
         if m == 0:
-            for j in y_peers:
-                await_recv(syc, ycb.at[j], ssem, syco.at[j], (gx, j))
-            ls, mid, re = [[ycb[d, k] for d in range(ny)] for k in range(3)]
-            interface_factor(
-                ny, gy, ls, mid, mid, re, [syc[0], syc[1], syc[1], syc[2]],
-                ytau, ysig, ybet, ytau2, ysig2, ydlt, ykk,
+            shy[0, 0], shy[0, 1] = top, end
+            yb0[gy] = shy[0]
+            comm.send_all(lambda dev: shy.at[0], yb0.at[gy], sy.at[0], y_peers, yb0.at[pl.ds(0, ny - 1)])
+        else:
+            shy[1, 0] = end + ysig[gy] * top
+            shy[1, 1] = top + ysig2[gy] * end
+            yb1[gy] = shy[1, 0]
+            comm.send_all(
+                lambda dev: shy.at[1, jnp.where(dev[1] > gy, 0, 1)], yb1.at[gy], sy.at[1], y_peers, yb1.at[pl.ds(0, ny - 1)]
             )
-        shy[m, 0] = end + ysig[gy] * top
-        shy[m, 1] = top + ysig2[gy] * end
-        yb[m, gy] = shy[m, 0]
-        for j in y_peers:
-            side = jnp.where(j > gy, 0, 1)
-            comm.send(shy.at[m, side], yb.at[m, gy], sy.at[m, gy], (gx, j))
         if m:
             sxt[0], sxt[1] = end, top
             comm.send(sxt.at[0], xtr.at[1], sw.at[1, 0], (gx, north), has_n)
@@ -594,6 +631,19 @@
         y_local()
         if m == 0:
             coarse_send(True)
+            await_all(ycb.at[pl.ds(0, ny - 1)], sy.at[2], y_peers[0])
+            ls, mid, re = [[ycb[d, k] for d in range(ny)] for k in range(3)]
+            interface_factor(
+                ny, gy, ls, mid, mid, re, [syc[0], syc[1], syc[1], syc[2]],
+                ytau, ysig, ybet, ytau2, ysig2, ydlt, ykk,
+            )
+            comm.finish()
+            await_all(yb0.at[pl.ds(0, ny - 1)], sy.at[0], y_peers[0])
+            above, below = interface_solve(
+                ny, gy, lambda d: yb0[d, 1] + ysig[d] * yb0[d, 0], lambda d: yb0[d, 0] + ysig2[d] * yb0[d, 1],
+                top, end, ytau, ytau2, ykk,
+            )
+            return above * ysc[0], below * ysc[1]
         else:
             for j in range(Y):
                 r_s[j] = g_s[j] - q_s[j]
@@ -605,19 +655,16 @@
             to_rows(pbuf, sw.at[2], True)
             coarse_wait()
             coefs = planes()
-            to_rows(wbuf, sw.at[0], False)
-        for j in y_peers:
-            await_recv(shy.at[m, 0], yb.at[m, j], ssem, sy.at[m, j], (gx, j))
-        above, below = interface_solve(ny, gy, lambda d: yb[m, d], lambda d: yb[m, d], top, end, ytau, ytau2, ykk)
-        if m == 0:
-            return above * ysc[0], below * ysc[1]
+            edge_operators()
+        await_all(yb1.at[pl.ds(0, ny - 1)], sy.at[1], y_peers[0])
+        above, below = interface_solve(ny, gy, lambda d: yb1[d], lambda d: yb1[d], top, end, ytau, ytau2, ykk)
         await_recv(sxt.at[0], xtr.at[1], ssem, sw.at[1, 0], (gx, north), has_s)
         await_recv(sxt.at[1], xtr.at[0], ssem, sw.at[1, 1], (gx, south), has_n)
         alpha, gamma = jnp.zeros((Z, X), f32), jnp.zeros((Z, X), f32)
         for d in range(ny - 2):
-            alpha = jnp.where(d < gy - 1, yb[m, d] + ytau[d] * alpha, alpha)
+            alpha = jnp.where(d < gy - 1, yb1[d] + ytau[d] * alpha, alpha)
         for d in reversed(range(2, ny)):
-            gamma = jnp.where(d > gy + 1, yb[m, d] + ytau2[d] * gamma, gamma)
+            gamma = jnp.where(d > gy + 1, yb1[d] + ytau2[d] * gamma, gamma)
         q_top = top + syc[0] * above + syc[1] * below
         q_end = end + syc[1] * above + syc[2] * below
         beta, delta = ybet[north], ydlt[south]
@@ -706,8 +753,7 @@
     fown[0:hj] = jnp.where(lane3 < half, pltpu.roll(cor[:hj], X - off, 2), pltpu.roll(cor[hj:], off, 2))
     fown[hj] = fringe(cor)
     fbuf[gx] = fown[...]
-    for i in x_peers:
-        comm.send(fown, fbuf.at[gx], sf.at[gx], (i, gy))
+    comm.send_all(lambda dev: fown, fbuf.at[gx], sf.at[0], x_peers, fbuf.at[pl.ds(0, nx - 1)])
     above, below = above * ysc[0], below * ysc[1]
     for j in range(Y):
         op_ref[pl.ds(j, Z, stride=Y), :] = g_s[j] + ly_s[j] * above + ry_s[j] * below
@@ -720,8 +766,7 @@
         v = res[2 + r] + jnp.where(jnp.logical_or(clane == off, clane == off + half - 1), v, 0.0)
         flip[pl.ds(r, CZ, stride=CY), :] = pltpu.roll(v, X - off, 1)
     or_ref[...] = flip[0:CZ * CY, :half]
-    for i in x_peers:
-        await_recv(fown, fbuf.at[i], ssem, sf.at[i], (i, gy))
+    await_all(fbuf.at[pl.ds(0, nx - 1)], sf.at[0], x_peers[0])
     nothing = jnp.zeros((CZ, X), f32)
     edges = [nothing] + [fbuf[d, hj] for d in range(nx)] + [nothing]
     spill = jnp.logical_or(clane >= X - 3, jnp.logical_and(clane >= half, clane < half + 3))
@@ -764,21 +809,21 @@
     block, square, groups = (Y, Z, X), (Y * Z // X, X, X), Y * Z // X
     assert Y * SLOTS <= X and CY * SLOTS <= X // 2 and X % Z == 0 and Y * Z % X == 0 and X % 8 == 0
     nsx, nsy = len(strides_of(X)), len(strides_of(Y))
-    sends = 3 + (ny - 1) * 3 + (nx - 1) * 3 + 8 + 6 + 2
+    assert nx > 1 and ny > 1
     dma = pltpu.SemaphoreType.DMA
     scratch = (
         [vm(*block) for _ in range(12)]
         + [vm(*square) for _ in range(6)] + [vm(nsx, 2, *square), vm(*block), vm(*block), vm(*block), vm(nsy, 2, *block)]
         + [vm(Z, X), vm(3, Z, X), vm(Z, X), vm(2, Z, X), vm(1, Z, X)]
         + [vm(nx, XC + 1, groups, X), vm(XC + 1, groups, X), vm(nx, groups, X), vm(2, groups, X)]
-        + [vm(ny, 3, Z, X), vm(3, Z, X), vm(2, ny, Z, X), vm(2, 2, Z, X)]
+        + [vm(ny, 3, Z, X), vm(3, Z, X), vm(ny, 2, Z, X), vm(ny, Z, X), vm(2, 2, Z, X)]
         + [vm(1, groups, X)] + [vm(nx, groups, X) for _ in range(8)] + [vm(4, groups, X)]
         + [vm(ny, Z, X) for _ in range(6)] + [vm(6, Z, X), vm(2, Z, X)]
         + [vm(3, (CY + 4) * Z, X), pltpu.VMEM((4 * X, X), jnp.bfloat16), vm(2, CY, CZ, X), vm(3, 2, CY + 5, CZ, X),
-           vm(CY + 4, 8, Z, X), vm(CY + 4, CZ, X), vm(2, Z, X), vm(2, Z, X),
+           vm(CY + 4, 8, Z, X), vm(2, 2 * EDGE + 1, Z, X), vm(2, 4 * EDGE + 1, Z, X), vm(CY + 4, CZ, X), vm(2, Z, X), vm(2, Z, X),
            vm(2, CZ, X), vm(CZ, X), vm(CY // 2 + 1, CZ, X), vm(nx, CY // 2 + 1, CZ, X), vm((nx // 2 + 1) * CZ * CY, X)]
-        + [dma((sends,)), dma((3,)), dma((2, nx)), dma((ny,)), dma((2, ny)), dma((3, 3)), dma((2,)), dma((3, 2)), dma((nx,))]
-        + [vm(6, Z * Y, X), dma((6,))]
+        + [dma((18,)), dma((3,)), dma((2,)), dma((3,)), dma((3,)), dma((2,)), dma((3, 2)), dma((1,))]
+        + [vm(6, Z * Y, X), dma((3,))]
     )
     p, r, c = pl.pallas_call(
         functools.partial(kernel, nx, ny),

time: 29.8 us -> 28.3 us (0.950)
  Pallas kernels: 29.1 us -> 27.5 us
    pallas_call x1, Pallas kernels: 28.3 us -> 26.8 us  [body(): pl.pallas_call(functools.partial(kernel, nx, ny), out_shape=(vm(Z * Y, X)...]
where the time goes in v4:
time: 28.3 us; the launch traced here: 28.2 us
  Pallas kernels  27.5 us (97%)
  between operations  0.64 us (2%)
    pallas_call x1, Pallas kernels, body(): pl.pallas_call(functools.partial(kernel, nx, ny), out_shape=(vm(Z * Y, X)...  26.8 us
    pallas_call x1, Pallas kernels, body(): pl.pallas_call(put, out_shape=tuple((jax.ShapeDtypeStruct(v.shape, f32) f...  0.71 us

profile of v4, /device:TPU:0, one launch (start us, length us, event | category | flops | bytes accessed | tf_op | source)
XLA Modules:
  0.0 28.2 jit_solution(8451548999133262587)
XLA Ops:
  0.6 26.8 %shard_map.85 = (f32[256,128]{1,0:T(8,128)S(1)}, f32[64,64]{1,0:T(8,128)S(1)}, f32[64,256]{1,0:T(8,128)S(1)}) custom-call(f32[256,128]{1,0:T(8,128)} %bitcast.9, f32[256,128]{1,0:T(8,128)} %bitcast.10, f32[256,128]{1,0:T(8,128)} %bitcast.11, f32[256,128]{1,0:T(8,128)} %bitcast.12, f32[256,128]{1,0:T(8,128)} %bitcast.13, f32[256,128]{1,0:T(8,128)} %bitcast.14), custom_call_target="tpu_custom_call" | custom-call | tf_op jit(solution)/shard_map/pallas_call | solution.py:828
  27.5 0.7 %shard_map.86 = (f32[256,128]{1,0:T(8,128)}, f32[64,64]{1,0:T(8,128)}, f32[64,256]{1,0:T(8,128)}) custom-call(f32[256,128]{1,0:T(8,128)S(1)} %get-tuple-element.9.refs_0_, f32[64,64]{1,0:T(8,128)S(1)} %get-tuple-element.10.refs_1_, f32[64,256]{1,0:T(8,128)S(1)} %get-tuple-element.11.refs_2_), custom_call_target="tpu_custom_call" | custom-call | tf_op jit(solution)/shard_map/pallas_call | solution.py:842

commit v5 on v0

v5 whole, which is shorter than its diff:
```python
import functools

import jax
import jax.numpy as jnp
from jax import lax
from jax.experimental import pallas as pl
from jax.experimental.pallas import tpu as pltpu
from jax.sharding import PartitionSpec as P

COARSE = 3
RELAX = 0.8
LE, LS, RE, RS, GS, GE, XC = range(7)
SLOTS = 8
EDGE = 4
MESH = pl.DeviceIdType.MESH


def strides_of(length):
    out, s = [], 1
    while s < length:
        out.append(s)
        s *= 2
    return out


class Comm:
    def __init__(self, send_sems):
        self.sems, self.used, self.pending = send_sems, 0, []

    def copy(self, src, dst, sem, recv, dev):
        return pltpu.make_async_remote_copy(
            src_ref=src, dst_ref=dst, send_sem=sem, recv_sem=recv, device_id=dev, device_id_type=MESH
        )

    def send(self, src, dst, recv, dev, cond=None):
        copy = self.copy(src, dst, self.sems.at[self.used], recv, dev)
        self.used += 1
        self.pending.append((copy, cond))
        if cond is None:
            copy.start()
        else:
            pl.when(cond)(copy.start)

    def send_all(self, src, dst, recv, devs, received):
        sem = self.sems.at[self.used]
        self.used += 1
        for dev in devs:
            self.copy(src(dev), dst, sem, recv, dev).start()
        self.pending.append((self.copy(received, received, sem, recv, devs[0]), None))

    def finish(self):
        for copy, cond in self.pending:
            if cond is None:
                copy.wait_send()
            else:
                pl.when(cond)(copy.wait_send)
        self.used, self.pending = 0, []


def await_recv(src, dst, sems, recv, dev, cond=None):
    copy = pltpu.make_async_remote_copy(
        src_ref=src, dst_ref=dst, send_sem=sems.at[0], recv_sem=recv, device_id=dev, device_id_type=MESH
    )
    if cond is None:
        copy.wait_recv()
    else:
        pl.when(cond)(copy.wait_recv)


def await_sides(buf, recv, dev, one, two):
    both = jnp.logical_and(one, two)
    pl.when(both)(lambda: await_all(buf, recv, dev))
    pl.when(jnp.logical_and(jnp.logical_or(one, two), jnp.logical_not(both)))(lambda: await_all(buf.at[0], recv, dev))


def await_all(part, recv, dev):
    pltpu.make_async_remote_copy(
        src_ref=part, dst_ref=part, send_sem=recv, recv_sem=recv, device_id=dev, device_id_type=MESH
    ).wait_recv()


def farthest_first(me, n):
    out = []
    for k in range(n - 1):
        down = jnp.where(n - 1 - k > me, n - 1 - k, n - 2 - k)
        up = jnp.where(k < me, k, k + 1)
        out.append(jnp.where(2 * me < n, down, up))
    return out


def flipped(me, n):
    if n & (n - 1):
        return [lax.rem(me + o, n) for o in range(1, n)]
    def peer_of(mask):
        peer, bit = 0, 1
        while bit < n:
            value = lax.rem(me // bit, 2)
            peer = peer + bit * (1 - value if mask & bit else value)
            bit *= 2
        return peer

    masks = list(range(n - 1, 0, -1))
    even, odd = [m for m in masks if m % 2 == 0], [m for m in masks if m % 2]
    first = lax.rem(me, 2) == 0
    return [jnp.where(first, peer_of(a), peer_of(b)) for a, b in zip(even + odd, odd + even)]


def interface_factor(n, me, ls, le, rs, re, own, tau, sig, bet, tau2, sig2, dlt, kk):
    beta = jnp.zeros_like(ls[0])
    for d in range(n):
        bet[d] = beta
        w = 1.0 / (1.0 - ls[d] * beta)
        t = le[d] * w
        tau[d] = t
        s = t * beta
        sig[d] = s
        beta = re[d] + s * rs[d]
    delta = jnp.zeros_like(ls[0])
    for d in reversed(range(n)):
        dlt[d] = delta
        w = 1.0 / (1.0 - re[d] * delta)
        t = rs[d] * w
        tau2[d] = t
        s = t * delta
        sig2[d] = s
        delta = ls[d] + s * le[d]
    ls_m, le_m, rs_m, re_m = own
    beta, delta = bet[me], dlt[me]
    a, b = 1.0 - beta * ls_m, 1.0 - delta * re_m
    o1, o2 = beta * rs_m, delta * le_m
    inv = 1.0 / (a * b - o1 * o2)
    kk[0], kk[1], kk[2], kk[3] = b * inv, o1 * inv, a * inv, o2 * inv
    kk[4], kk[5] = beta, delta


def interface_solve(n, me, h_left, h_right, gs, ge, tau, tau2, kk):
    alpha = jnp.zeros_like(gs)
    for d in range(n - 1):
        alpha = jnp.where(d < me, h_left(d) + tau[d] * alpha, alpha)
    gamma = jnp.zeros_like(gs)
    for d in reversed(range(1, n)):
        gamma = jnp.where(d > me, h_right(d) + tau2[d] * gamma, gamma)
    p = alpha + kk[4] * gs
    q = gamma + kk[5] * ge
    return kk[0] * p + kk[1] * q, kk[2] * q + kk[3] * p


def chain_factor(n, me, ls, le, rs, re, xc, own, rho, tau, sig, bet, tau2, sig2, scl, dlt, kk):
    one, zero = jnp.ones_like(ls[0]), jnp.zeros_like(ls[0])
    beta = zero
    for d in range(n):
        r = zero if d == 0 else xc[d - 1]
        b = one if d == 0 else 1.0 - r * (1.0 - beta)
        rho[d], bet[d] = r, b
        w = 1.0 / (1.0 - ls[d] * b)
        t = le[d] * w
        tau[d] = t * r
        s = t * b
        sig[d] = s
        beta = re[d] + s * rs[d]
    delta = zero
    for d in reversed(range(n)):
        dlt[d] = delta
        t = rs[d] / (1.0 - re[d] * delta)
        s = t * delta
        q = ls[d] + s * le[d]
        if d > 0:
            v = 1.0 / (1.0 - q + q * xc[d - 1])
            scl[d], tau2[d], sig2[d] = v, v * t, v * s
            delta = v * q * xc[d - 1]
        else:
            scl[d], tau2[d], sig2[d] = zero, zero, zero
    ls_m, le_m, rs_m, re_m = own
    beta, delta = bet[me], dlt[me]
    a, b = 1.0 - beta * ls_m, 1.0 - delta * re_m
    o1, o2 = beta * rs_m, delta * le_m
    inv = 1.0 / (a * b - o1 * o2)
    kk[0], kk[1], kk[2], kk[3] = b * inv, o1 * inv, a * inv, o2 * inv


def kernel(nx, ny, f_hbm, p_hbm, x_hbm, y_hbm, z_hbm, d_hbm, op_ref, or_ref, oc_ref,
           xl_s, xc_s, yl_s, yc_s, zl_s, zt_s, zd_s, fo_s, p_s, r_s, g_s, q_s,
           ct_s, rt_s, gt_s, lx_s, rx_s, ix_s, wx_s, ly_s, ry_s, iy_s, wy_s,
           sx0, sy0, hx, hy, xb, sxb, xb1, sx1, ycb, syc, yb0, yb1, shy,
           xown, xrho, xtau, xsig, xbet, xtau2, xsig2, xscl, xdlt, xkk,
           ytau, ysig, ybet, ytau2, ysig2, ydlt, ykk, ysc,
           pair_s, sel_s, cown, cbuf, wbuf, elr, nbr, pbuf, sxt, xtr, ebuf, sedge, fown, fbuf, flip,
           ssem, s0, sx, sy, sc, sr, sw, ins):
    Y, Z, X = xc_s.shape
    CY, CZ = Y // 2, Z // 2
    f32 = jnp.float32
    gx, gy = lax.axis_index("gx"), lax.axis_index("gy")
    has_w, has_e = gx > 0, gx < nx - 1
    has_n, has_s = gy > 0, gy < ny - 1
    west, east = jnp.maximum(gx - 1, 0), jnp.minimum(gx + 1, nx - 1)
    north, south = jnp.maximum(gy - 1, 0), jnp.minimum(gy + 1, ny - 1)
    x_peers = [(i, gy) for i in farthest_first(gx, nx)]
    y_peers = [(gx, j) for j in flipped(gy, ny)]

    half = X // 2
    off = half // 2
    hj = CY // 2
    clane = lax.broadcasted_iota(jnp.int32, (CZ, X), 1)
    lane3 = lax.broadcasted_iota(jnp.int32, (1, 1, X), 2)
    inner = clane % half

    def fringe(v):
        edge = jnp.zeros((CZ, X), f32)
        for r in range(CY):
            edge = jnp.where(inner >= SLOTS * r, pltpu.roll(v[r], half - off + 3 + SLOTS * r, 1), edge)
        return edge

    def sweeps(ssem, sin):
        stages = ((0, 2), (2, 3), (3, 6))
        sources = (y_hbm, p_hbm, x_hbm, z_hbm, d_hbm, f_hbm)
        for n, (lo, hi) in enumerate(stages):
            for m in range(lo, hi):
                pltpu.make_async_copy(sources[m], ins.at[m], sin.at[n]).start()

        def loaded(n):
            part = ins.at[pl.ds(stages[n][0], stages[n][1] - stages[n][0])]
            pltpu.make_async_copy(part, part, sin.at[n]).wait()

        y_ref, p_ref, x_ref, z_ref, d_ref, f_ref = [ins.at[m] for m in range(6)]

        barrier = pltpu.get_barrier_semaphore()

        def greet(dev):
            pl.semaphore_signal(barrier, inc=1, device_id=dev, device_id_type=MESH)

        for dev in x_peers + y_peers:
            greet(dev)

        lane = lax.broadcasted_iota(jnp.int32, (Z, X), 1)
        level = lax.broadcasted_iota(jnp.int32, (Z, X), 0)

        def rows(ref, j):
            return ref[pl.ds(j, Z, stride=Y), :]

        loaded(0)
        sy0[0] = rows(y_ref, Y - 1)
        sy0[1] = rows(p_ref, Y - 1)
        sy0[2] = rows(p_ref, 0)

        pl.semaphore_wait(barrier, (nx - 1) + (ny - 1))

        comm = Comm(ssem)
        comm.send(sy0.at[0:2], hy.at[0:2], s0.at[1], (gx, south), has_s)
        comm.send(sy0.at[2:3], hy.at[2:3], s0.at[1], (gx, north), has_n)

        loaded(1)
        packed = jnp.zeros((Z, X), f32)
        for j in range(Y):
            v = rows(x_ref, j)
            xc_s[j] = v
            packed = jnp.where(lane == SLOTS * j + XC, v[:, X - 1:], packed)
        sx0[...] = packed
        comm.send(sx0, hx, s0.at[0], (east, gy), has_e)

        for j in range(Y):
            yc_s[j] = rows(y_ref, j)
            p_s[j] = rows(p_ref, j)
        loaded(2)
        for j in range(Y):
            zv = jnp.where(level < Z - 1, rows(z_ref, j), 0.0)
            zt_s[j] = zv
            zl = pltpu.roll(zv, 1, 0)
            zl_s[j] = zl
            zd_s[j] = zv + zl + rows(d_ref, j)
            fo_s[j] = rows(f_ref, j)

        to_sides = (((gx, south), has_s, has_n), ((gx, north), has_n, has_s))
        per, groups, blocks = X // Z, Y * Z // X, X // 8
        sub = lax.broadcasted_iota(jnp.int32, (8, X), 0)

        def turned(ref, g):
            return ref[g * per:(g + 1) * per].reshape(X, X).T

        def split(v):
            return [v[8 * k:8 * k + 8] for k in range(blocks)]

        def shift(v, s, fill):
            if s % 8 == 0:
                m = s // 8
                return [v[k - m] if 0 <= k - m < blocks else fill for k in range(blocks)]
            turn = [pltpu.roll(u, s % 8, 0) for u in v]
            if s > 0:
                return [jnp.where(sub < s, fill if k == 0 else turn[k - 1], turn[k]) for k in range(blocks)]
            return [jnp.where(sub >= 8 + s, fill if k == blocks - 1 else turn[k + 1], turn[k]) for k in range(blocks)]

        def scaled(u, v):
            return [a if b is None else b if a is None else a * b for a, b in zip(u, v)]

        def added(u, v):
            return [a if b is None else a + b for a, b in zip(u, v)]

        def fill_of(s, value):
            return None if s % 8 == 0 else value

        def store(ref, at, v):
            for k in range(blocks):
                ref[at + (slice(8 * k, 8 * k + 8),)] = v[k]

        def load(ref, at):
            return [ref[at + (slice(8 * k, 8 * k + 8),)] for k in range(blocks)]

        xsteps = strides_of(X)

        def x_factor(g):
            c = load(ct_s, (g,))
            a = shift(c, 1, 1.0)
            for j in range(g * per, (g + 1) * per):
                g_s[j] = yl_s[j] + yc_s[j] + zd_s[j]
            e = split(turned(g_s, g))
            for n, s in enumerate(xsteps):
                inv = [1.0 / (u + v + w) for u, v, w in zip(a, c, e)]
                ai, ci = scaled(a, inv), scaled(c, inv)
                store(wx_s, (n, 0, g), ci)
                store(wx_s, (n, 1, g), ai)
                ae, ce = scaled(ai, e), scaled(ci, e)
                a = scaled(a, shift(ai, s, fill_of(s, 1.0)))
                c = scaled(c, shift(ci, -s, fill_of(s, 1.0)))
                e = added(added(e, shift(ce, s, fill_of(s, 0.0))), shift(ae, -s, fill_of(s, 0.0)))
            inv = [1.0 / (u + v + w) for u, v, w in zip(a, c, e)]
            a, c = scaled(a, inv), scaled(c, inv)
            store(ix_s, (g,), inv)
            store(lx_s, (g,), a)
            store(rx_s, (g,), c)
            one = slice(g, g + 1)
            sxb[LE, one], sxb[LS, one] = a[-1][7:8], a[0][0:1]
            sxb[RE, one], sxb[RS, one] = c[-1][7:8], c[0][0:1]
            sxb[XC, one] = ct_s[g, X - 1:X]

        def edge_sums(g):
            r = split(turned(r_s, g))
            store(rt_s, (g,), r)
            out = []
            for ref in (lx_s, rx_s):
                v = scaled(load(ref, (g,)), r)
                while len(v) > 1:
                    v = [a + b for a, b in zip(v[0::2], v[1::2])]
                out.append(jnp.sum(v[0], axis=0, keepdims=True))
            return out

        def z_terms(v, part):
            return zl_s[part] * pltpu.roll(v, 1, 1) + zt_s[part] * pltpu.roll(v, Z - 1, 1)

        def x_source(lo, hi, lower, upper):
            part = slice(lo, hi)
            r_s[part] = fo_s[part] + yl_s[part] * lower + yc_s[part] * upper + z_terms(p_s[part], part)

        for g in range(groups):
            store(ct_s, (g,), split(turned(xc_s, g)))
        yl_s[1:Y] = yc_s[0:Y - 1]
        for g in range(1, groups):
            x_factor(g)
        x_source(1, Y - 1, p_s[0:Y - 2], p_s[2:Y])

        @pl.when(jnp.logical_not(has_w))
        def _():
            hx[...] = jnp.zeros_like(hx)
            cbuf[0] = jnp.zeros_like(cbuf[0])
            ebuf[0] = jnp.zeros_like(ebuf[0])

        @pl.when(jnp.logical_not(has_e))
        def _():
            cbuf[2] = jnp.zeros_like(cbuf[2])
            ebuf[1] = jnp.zeros_like(ebuf[1])

        @pl.when(jnp.logical_not(has_n))
        def _():
            hy[0:2] = jnp.zeros_like(hy[0:2])
            nbr[0] = jnp.zeros_like(nbr[0])
            pbuf[0:2] = jnp.zeros_like(pbuf[0:2])
            xtr[0] = jnp.zeros_like(xtr[0])
            for d in range(3):
                cbuf[d, :, 0:3] = jnp.zeros_like(cbuf[d, :, 0:3])

        @pl.when(jnp.logical_not(has_s))
        def _():
            hy[2] = jnp.zeros_like(hy[2])
            nbr[1] = jnp.zeros_like(nbr[1])
            pbuf[CY + 2:] = jnp.zeros_like(pbuf[CY + 2:])
            xtr[1] = jnp.zeros_like(xtr[1])
            for d in range(3):
                cbuf[d, :, 3 + CY:] = jnp.zeros_like(cbuf[d, :, 3 + CY:])

        for n, u in ((True, True), (True, False), (False, True)):
            cond = jnp.logical_and(has_n if n else jnp.logical_not(has_n), has_s if u else jnp.logical_not(has_s))
            part = hy.at[pl.ds(0, (2 if n else 0) + (1 if u else 0))]
            await_recv(part, part, ssem, s0.at[1], (gx, north), cond)

        yl_s[0] = hy[0]
        x_factor(0)
        x_source(0, 1, hy[1:2], p_s[1:2])
        x_source(Y - 1, Y, p_s[Y - 2:Y - 1], hy[2:3])
        for g in range(groups):
            one = slice(g, g + 1)
            sxb[GS, one], sxb[GE, one] = edge_sums(g)
        xb[gx] = sxb[...]
        comm.send_all(lambda dev: sxb, xb.at[gx], sx.at[0], x_peers, xb.at[pl.ds(0, nx - 1)])

        for n, (dev, there, _) in enumerate(to_sides):
            for k, ref in enumerate((xc_s, zt_s)):
                src = ref.at[pl.ds(0 if n else Y - EDGE, EDGE)]
                comm.send(src, nbr.at[n, pl.ds(k * EDGE, EDGE)], sw.at[0], dev, there)

        await_recv(sx0, hx, ssem, s0.at[0], (east, gy), has_w)
        for j in range(Y):
            xl_s[j] = jnp.where(lane == 0, hx[:, SLOTS * j + XC:SLOTS * j + XC + 1], pltpu.roll(xc_s[j], 1, 1))

        ysteps = strides_of(Y)
        for lo in range(0, Z, 8):
            zs = slice(lo, lo + 8)
            a = [yl_s[j, zs] for j in range(Y)]
            c = [yc_s[j, zs] for j in range(Y)]
            e = [xl_s[j, zs] + xc_s[j, zs] + zd_s[j, zs] for j in range(Y)]
            for n, s in enumerate(ysteps):
                inv = [1.0 / (a[j] + c[j] + e[j]) for j in range(Y)]
                ai, ci = [a[j] * inv[j] for j in range(Y)], [c[j] * inv[j] for j in range(Y)]
                for j in range(Y):
                    if j + s < Y:
                        wy_s[n, 0, j, zs] = ci[j]
                    if j >= s:
                        wy_s[n, 1, j, zs] = ai[j]
                e2 = []
                for j in range(Y):
                    v = e[j]
                    if j >= s:
                        v = v + ci[j - s] * e[j - s]
                    if j + s < Y:
                        v = v + ai[j + s] * e[j + s]
                    e2.append(v)
                a = [a[j] * ai[j - s] if j >= s else a[j] for j in range(Y)]
                c = [c[j] * ci[j + s] if j + s < Y else c[j] for j in range(Y)]
                e = e2
            for j in range(Y):
                inv = 1.0 / (a[j] + c[j] + e[j])
                iy_s[j, zs], ly_s[j, zs], ry_s[j, zs] = inv, a[j] * inv, c[j] * inv

        k_top, k_end = jnp.sqrt(yl_s[0]), jnp.sqrt(yc_s[Y - 1])
        i_top = jnp.where(has_n, 1.0 / jnp.where(has_n, k_top, 1.0), 0.0)
        ysc[0], ysc[1] = i_top, 1.0 / k_end
        syc[0], syc[1], syc[2] = ly_s[0], ly_s[Y - 1] * k_end * i_top, ry_s[Y - 1]
        ycb[gy] = syc[...]
        comm.send_all(lambda dev: syc, ycb.at[gy], sy.at[2], y_peers, ycb.at[pl.ds(0, ny - 1)])

        def x_local():
            for g in range(groups):
                r = load(rt_s, (g,))
                for n, s in enumerate(xsteps):
                    low = shift(scaled(load(wx_s, (n, 0, g)), r), s, fill_of(s, 0.0))
                    high = shift(scaled(load(wx_s, (n, 1, g)), r), -s, fill_of(s, 0.0))
                    r = added(added(r, low), high)
                store(gt_s, (g,), scaled(r, load(ix_s, (g,))))

        def y_local():
            for lo in range(0, Z, 8):
                zs = slice(lo, lo + 8)
                r = [r_s[j, zs] for j in range(Y)]
                for n, s in enumerate(ysteps):
                    low = [wy_s[n, 0, j, zs] * r[j] if j + s < Y else None for j in range(Y)]
                    high = [wy_s[n, 1, j, zs] * r[j] if j >= s else None for j in range(Y)]
                    r2 = []
                    for j in range(Y):
                        v = r[j]
                        if j >= s:
                            v = v + low[j - s]
                        if j + s < Y:
                            v = v + high[j + s]
                        r2.append(v)
                    r = r2
                for j in range(Y):
                    g_s[j, zs] = r[j] * iy_s[j, zs]

        x_local()

        ii = lax.broadcasted_iota(jnp.int32, (X, X), 0)
        mm = lax.broadcasted_iota(jnp.int32, (X, X), 1)

        def selection(step, start):
            target = lax.rem((ii + (step + 2)) // 2 - 1 + start + X, X)
            return jnp.where(mm == target, 0.125, 0.0)

        def level_pairs(n, levels):
            for k, v in enumerate(levels):
                pair_s[n, k * Z:(k + 1) * Z] = v
            count = len(levels) * CZ
            return pair_s[n, pl.ds(0, count, stride=2), :] + pair_s[n, pl.ds(1, count, stride=2), :]

        def pairs(n, field):
            return level_pairs(n, [field(2 * k) + field(2 * k + 1) for k in range(CY)])

        def gathered(parts, first):
            v = jnp.concatenate(parts, axis=1)
            high = v.astype(jnp.bfloat16)
            v = v - high.astype(f32)
            mid = v.astype(jnp.bfloat16)
            low = (v - mid.astype(f32)).astype(jnp.bfloat16)
            sel = sel_s[first * X:(first + len(parts)) * X]
            return sum(jnp.dot(u, sel, preferred_element_type=f32) for u in (low, mid, high))

        for n, sel in enumerate((selection(1, off), selection(-1, off), selection(0, off), selection(0, half + off))):
            sel_s[n * X:(n + 1) * X] = sel.astype(jnp.bfloat16)
        for m, (u, v) in enumerate(((lambda j: xc_s[j], lambda j: yc_s[j]), (lambda j: rows(z_ref, j), lambda j: rows(d_ref, j)))):
            part = gathered([pairs(0, u), pairs(1, v)], 2).reshape(CY, CZ, X)
            cown[m] = part
            cbuf[1, m, 3:3 + CY] = part

        def operator(at, xc, xl, zl, zt, sides):
            for n, (u, v) in enumerate(sides):
                wbuf[at, n] = xc[0] * u + xc[1] * v
                wbuf[at, 2 + n] = xl[0] * u + xl[1] * v
                wbuf[at, 4 + n] = zl[0] * pltpu.roll(u, 1, 0) + zl[1] * pltpu.roll(v, 1, 0)
                wbuf[at, 6 + n] = zt[0] * pltpu.roll(u, Z - 1, 0) + zt[1] * pltpu.roll(v, Z - 1, 0)

        for k in range(EDGE):
            for n, j in enumerate((Y - EDGE + k, k)):
                elr[n, k], elr[n, EDGE + k] = ly_s[j] * ysc[0], ry_s[j] * ysc[1]
        for n in range(2):
            elr[n, 2 * EDGE] = hx[...]
        for k in range(CY):
            two = (2 * k, 2 * k + 1)
            operator(2 + k, *[[ref[j] for j in two] for ref in (xc_s, xl_s, zl_s, zt_s)],
                     [[ref[j] * ysc[n] for j in two] for n, ref in enumerate((ly_s, ry_s))])

        def edge_columns():
            for n, (dev, there, _) in enumerate(to_sides):
                comm.send(elr.at[n], nbr.at[n, pl.ds(2 * EDGE, 2 * EDGE + 1)], sw.at[0], dev, there)

        def edge_operators():
            await_sides(nbr, sw.at[0], (gx, north), has_n, has_s)
            for n, first in enumerate((Y - EDGE, 0)):
                for k in range(0, EDGE, 2):
                    xc = [nbr[n, k + i] for i in range(2)]
                    zt = [nbr[n, EDGE + k + i] for i in range(2)]
                    cols = [SLOTS * (first + k + i) + XC for i in range(2)]
                    xl = [jnp.where(lane == 0, nbr[n, 4 * EDGE, :, c:c + 1], pltpu.roll(v, 1, 1)) for c, v in zip(cols, xc)]
                    operator(n * (CY + 2) + k // 2, xc, xl, [pltpu.roll(v, 1, 0) for v in zt], zt,
                             [[nbr[n, (2 + m) * EDGE + k + i] for i in range(2)] for m in range(2)])

        def edge_rows():
            for dev, there, src, dst in (((gx, north), has_n, 2, CY + 2), ((gx, south), has_s, CY, 0)):
                comm.send(pbuf.at[pl.ds(src, 2)], pbuf.at[pl.ds(dst, 2)], sw.at[2], dev, there)

        def coarse_send(straight):
            for i, ok, back in ((west, has_w, 2), (gx, None, 1), (east, has_e, 0)):
                both = (lambda c: c) if ok is None else (lambda c, ok=ok: jnp.logical_and(c, ok))
                if straight:
                    if ok is not None:
                        comm.send(cown, cbuf.at[back, :, pl.ds(3, CY)], sc.at[back], (i, gy), ok)
                else:
                    comm.send(cown.at[:, pl.ds(CY - 3, 3)], cbuf.at[back, :, pl.ds(0, 3)], sc.at[back], (i, south), both(has_s))
                    comm.send(cown.at[:, pl.ds(0, 2)], cbuf.at[back, :, pl.ds(3 + CY, 2)], sc.at[back], (i, north), both(has_n))

        def coarse_wait():
            for slot, i, ok in ((0, west, has_w), (1, gx, None), (2, east, has_e)):
                kept = 0 if ok is None else CY
                for n, s in ((True, True), (True, False), (False, True)):
                    cond = jnp.logical_and(has_n if n else jnp.logical_not(has_n), has_s if s else jnp.logical_not(has_s))
                    cond = cond if ok is None else jnp.logical_and(cond, ok)
                    part = cbuf.at[slot, :, pl.ds(0, kept + (3 if n else 0) + (2 if s else 0))]
                    await_recv(part, part, ssem, sc.at[slot], (i, gy), cond)

        def x_solve(hl, hr, gs, ge):
            alpha = jnp.zeros((groups, X), f32)
            for d in range(nx - 1):
                alpha = jnp.where(d < gx, hl(d) + xtau[d] * alpha, alpha)
            gamma = jnp.zeros((groups, X), f32)
            for d in reversed(range(1, nx)):
                gamma = jnp.where(d > gx, hr(d) + xtau2[d] * gamma, gamma)
            p = xrho[gx] * alpha + xbet[gx] * gs
            q = gamma + xdlt[gx] * ge
            return xkk[0] * p + xkk[1] * q, xkk[2] * q + xkk[3] * p

        def x_first():
            await_all(xb.at[pl.ds(0, nx - 1)], sx.at[0], x_peers[0])
            cut = [[xb[d, k] for d in range(nx)] for k in range(XC + 1)]
            own = [sxb[k] for k in range(XC + 1)]
            inv = [1.0 / v for v in cut[XC]]
            ge = [cut[GE][d] * inv[d] for d in range(nx)]
            gs = cut[GS]
            xown[0] = 1.0 / own[XC]
            chain_factor(nx, gx, cut[LS], cut[LE], cut[RS], cut[RE], cut[XC], [own[LS], own[LE], own[RS], own[RE]],
                         xrho, xtau, xsig, xbet, xtau2, xsig2, xscl, xdlt, xkk)
            return x_solve(
                lambda d: ge[d] + xsig[d] * gs[d], lambda d: xscl[d] * gs[d] + xsig2[d] * ge[d], own[GS], own[GE] * xown[0]
            )

        def x_second():
            sums = [edge_sums(g) for g in range(groups)]
            gs, ge = [jnp.concatenate([v[n] for v in sums], axis=0) for n in range(2)]
            ge = ge * xown[0]
            sx1[0], sx1[1] = ge + xsig[gx] * gs, xscl[gx] * gs + xsig2[gx] * ge
            comm.send_all(
                lambda dev: sx1.at[jnp.where(dev[0] > gx, 0, 1)], xb1.at[gx], sx.at[1], x_peers, xb1.at[pl.ds(0, nx - 1)]
            )
            coarse_send(False)
            edge_columns()
            x_local()
            await_all(xb1.at[pl.ds(0, nx - 1)], sx.at[1], x_peers[0])
            return x_solve(lambda d: xb1[d], lambda d: xb1[d], gs, ge)

        def y_half(m, left, right):
            top, end = jnp.zeros((Z, X), f32), jnp.zeros((Z, X), f32)
            for g in range(groups):
                u, w = left[g:g + 1], right[g:g + 1]
                c, v = load(ct_s, (g,)), []
                for a, b, d in zip(load(gt_s, (g,)), load(lx_s, (g,)), load(rx_s, (g,))):
                    v.append(a + b * u + d * w)
                edge = u + (xrho[gx][g:g + 1] - 1.0) * v[0][0:1]
                t = added(shift(scaled(c, v), 1, edge), scaled(c, shift(v, -1, w)))
                v = jnp.concatenate(v, axis=0).T.reshape(per, Z, X)
                t = jnp.concatenate(t, axis=0).T.reshape(per, Z, X)
                for n in range(per):
                    j = g * per + n
                    q_s[j] = v[n]
                    r = fo_s[j] + t[n] + zl_s[j] * pltpu.roll(v[n], 1, 0) + zt_s[j] * pltpu.roll(v[n], Z - 1, 0)
                    r_s[j] = r
                    top, end = top + ly_s[j] * r, end + ry_s[j] * r
            top, end = top * ysc[0], end * ysc[1]
            if m == 0:
                shy[0, 0], shy[0, 1] = top, end
                yb0[gy] = shy[0]
                comm.send_all(lambda dev: shy.at[0], yb0.at[gy], sy.at[0], y_peers, yb0.at[pl.ds(0, ny - 1)])
            else:
                shy[1, 0] = end + ysig[gy] * top
                shy[1, 1] = top + ysig2[gy] * end
                yb1[gy] = shy[1, 0]
                comm.send_all(
                    lambda dev: shy.at[1, jnp.where(dev[1] > gy, 0, 1)], yb1.at[gy], sy.at[1], y_peers, yb1.at[pl.ds(0, ny - 1)]
                )
            if m:
                sxt[0], sxt[1] = end, top
                comm.send(sxt.at[0], xtr.at[1], sw.at[1], (gx, north), has_n)
                comm.send(sxt.at[1], xtr.at[0], sw.at[1], (gx, south), has_s)
            y_local()
            if m == 0:
                coarse_send(True)
                await_all(ycb.at[pl.ds(0, ny - 1)], sy.at[2], y_peers[0])
                ls, mid, re = [[ycb[d, k] for d in range(ny)] for k in range(3)]
                interface_factor(
                    ny, gy, ls, mid, mid, re, [syc[0], syc[1], syc[1], syc[2]],
                    ytau, ysig, ybet, ytau2, ysig2, ydlt, ykk,
                )
                comm.finish()
                await_all(yb0.at[pl.ds(0, ny - 1)], sy.at[0], y_peers[0])
                above, below = interface_solve(
                    ny, gy, lambda d: yb0[d, 1] + ysig[d] * yb0[d, 0], lambda d: yb0[d, 0] + ysig2[d] * yb0[d, 1],
                    top, end, ytau, ytau2, ykk,
                )
                return above * ysc[0], below * ysc[1]
            else:
                for j in range(Y):
                    r_s[j] = g_s[j] - q_s[j]
                pbuf[2:CY + 2] = gathered([
                    pairs(0, lambda j: xc_s[j] * r_s[j]),
                    pairs(1, lambda j: xl_s[j] * r_s[j]),
                    pairs(2, lambda j: zl_s[j] * pltpu.roll(r_s[j], 1, 0) + zt_s[j] * pltpu.roll(r_s[j], Z - 1, 0)),
                ], 0).reshape(CY, CZ, X)
                edge_rows()
                comm.finish()
                coarse_wait()
                coefs = planes()
                edge_operators()
            await_all(yb1.at[pl.ds(0, ny - 1)], sy.at[1], y_peers[0])
            above, below = interface_solve(ny, gy, lambda d: yb1[d], lambda d: yb1[d], top, end, ytau, ytau2, ykk)
            await_sides(xtr, sw.at[1], (gx, north), has_n, has_s)
            alpha, gamma = jnp.zeros((Z, X), f32), jnp.zeros((Z, X), f32)
            for d in range(ny - 2):
                alpha = jnp.where(d < gy - 1, yb1[d] + ytau[d] * alpha, alpha)
            for d in reversed(range(2, ny)):
                gamma = jnp.where(d > gy + 1, yb1[d] + ytau2[d] * gamma, gamma)
            q_top = top + syc[0] * above + syc[1] * below
            q_end = end + syc[1] * above + syc[2] * below
            beta, delta = ybet[north], ydlt[south]
            over = (alpha + beta * (xtr[0] + ycb[north, 1] * q_top)) / (1.0 - beta * ycb[north, 0])
            under = (gamma + delta * (xtr[1] + ycb[south, 1] * q_end)) / (1.0 - delta * ycb[south, 2])
            return above, below, coefs, [(over, q_top), (above, below), (q_end, under)]

        centre = jnp.logical_and(lane3 >= off, lane3 < off + half)
        H = CY + 4
        row = lax.broadcasted_iota(jnp.int32, (H, 1, 1), 0)
        inside = jnp.logical_and(
            jnp.logical_or(row >= 2, has_n), jnp.logical_or(row < 2 + CY, has_s)
        )
        inside = jnp.logical_and(
            inside,
            jnp.logical_and(jnp.logical_or(lane3 >= off, has_w), jnp.logical_or(lane3 < off + half, has_e)),
        )

        def planes():
            out = []
            for m in range(2):
                w, o, e = cbuf[0, m], cbuf[1, m], cbuf[2, m]
                out.append(jnp.where(centre, o, pltpu.roll(jnp.where(lane3 >= half, w, e), half, 2)))
                out.append(jnp.where(centre, pltpu.roll(o, half, 2), jnp.where(lane3 < half, w, e)))
            cx, cy, cz, cd = out
            czl = lax.broadcasted_iota(jnp.int32, (1, CZ, 1), 1)
            cyl, cy = cy[:H], cy[1:]
            cx, cz, cd = cx[1:], cz[1:], cd[1:]
            cd = jnp.where(inside, cd, 1.0)
            ct = jnp.where(czl < CZ - 1, cz, 0.0)
            cl = pltpu.roll(ct, 1, 1)
            cxl = pltpu.roll(cx, 1, 2)
            diag = cxl + cx + cyl + cy + cl + ct + cd
            return cx, cxl, cy, cyl, cl, ct, diag, RELAX / diag

        left, right = x_first()
        above, below = y_half(0, left, right)
        p_s[...] = g_s[...] + ly_s[...] * above[None] + ry_s[...] * below[None]
        for lo in range(0, Y, 4):
            hi = lo + 4
            lower = jnp.concatenate([above[None], p_s[0:hi - 1]], axis=0) if lo == 0 else p_s[lo - 1:hi - 1]
            upper = jnp.concatenate([p_s[lo + 1:Y], below[None]], axis=0) if hi == Y else p_s[lo + 1:hi + 1]
            x_source(lo, hi, lower, upper)
        left, right = x_second()
        above, below, coefs, ghosts = y_half(1, left, right)
        cx, cxl, cy, cyl, cl, ct, diag, scale = coefs
        sides = [[], [], []]
        for at in range(H):
            a, b = ghosts[0 if at < 2 else 1 if at < CY + 2 else 2]
            w = [wbuf[at, n] for n in range(8)]
            sides[0].append(w[0] * a + w[1] * b)
            sides[1].append(w[2] * a + w[3] * b)
            a1, b1, a2, b2 = pltpu.roll(a, 1, 0), pltpu.roll(b, 1, 0), pltpu.roll(a, Z - 1, 0), pltpu.roll(b, Z - 1, 0)
            sides[2].append(w[4] * a1 + w[5] * b1 + w[6] * a2 + w[7] * b2)
        partial = gathered([level_pairs(n, v) for n, v in enumerate(sides)], 0).reshape(H, CZ, X)
        await_sides(pbuf.at[pl.ds(0, 4)].reshape(2, 2, CZ, X), sw.at[2], (gx, north), has_n, has_s)
        res = jnp.where(inside, partial + pbuf[...], 0.0)
        cor = scale * res
        for repeat in range(COARSE - 1):
            lo, n = 1 + repeat, H - 2 - 2 * repeat
            cut = slice(lo, lo + n)
            mid, over, under = cor[1:-1], cor[:-2], cor[2:]
            applied = (
                diag[cut] * mid
                - cxl[cut] * pltpu.roll(mid, 1, 2)
                - cx[cut] * pltpu.roll(mid, X - 1, 2)
                - cyl[cut] * over
                - cy[cut] * under
                - cl[cut] * pltpu.roll(mid, 1, 1)
                - ct[cut] * pltpu.roll(mid, CZ - 1, 1)
            )
            cor = jnp.where(inside[cut], mid + scale[cut] * (res[cut] - applied), 0.0)
        fown[0:hj] = jnp.where(lane3 < half, pltpu.roll(cor[:hj], X - off, 2), pltpu.roll(cor[hj:], off, 2))
        fown[hj] = fringe(cor)
        fbuf[gx] = fown[...]
        return res, above, below

    res, above, below = pl.run_scoped(sweeps, pltpu.SemaphoreType.DMA((14,)), pltpu.SemaphoreType.DMA((3,)))
    comm = Comm(ssem)
    comm.send_all(lambda dev: fown, fbuf.at[gx], sx.at[0], x_peers, fbuf.at[pl.ds(0, nx - 1)])
    sedge[...] = fringe(res[2:CY + 2])
    comm.send(sedge, ebuf.at[1], sr.at[0], (west, gy), has_w)
    comm.send(sedge, ebuf.at[0], sr.at[0], (east, gy), has_e)
    above, below = above * ysc[0], below * ysc[1]
    for j in range(Y):
        op_ref[pl.ds(j, Z, stride=Y), :] = g_s[j] + ly_s[j] * above + ry_s[j] * below
    comm.finish()
    await_sides(ebuf, sr.at[0], (west, gy), has_w, has_e)
    both = jnp.where(clane < half, ebuf[0], ebuf[1])
    for r in range(CY):
        v = pltpu.roll(both, (off - 3 - SLOTS * r) % X, 1)
        v = res[2 + r] + jnp.where(jnp.logical_or(clane == off, clane == off + half - 1), v, 0.0)
        flip[pl.ds(r, CZ, stride=CY), :] = pltpu.roll(v, X - off, 1)
    or_ref[...] = flip[0:CZ * CY, :half]
    await_all(fbuf.at[pl.ds(0, nx - 1)], sx.at[0], x_peers[0])
    nothing = jnp.zeros((CZ, X), f32)
    edges = [nothing] + [fbuf[d, hj] for d in range(nx)] + [nothing]
    spill = jnp.logical_or(clane >= X - 3, jnp.logical_and(clane >= half, clane < half + 3))
    spill2 = jnp.logical_or(clane < 3, jnp.logical_and(clane >= half - 3, clane < half))
    for t in range(nx // 2):
        u, v = fbuf[2 * t, 0:hj], fbuf[2 * t + 1, 0:hj]
        top = jnp.where(lane3 < half, u, pltpu.roll(v, half, 2))
        low = jnp.where(lane3 < half, pltpu.roll(u, half, 2), v)
        one = jnp.where(clane < half, edges[2 * t + 1], edges[2 * t + 3])
        two = jnp.where(clane < half, edges[2 * t], edges[2 * t + 2])
        base = (t + 1) * CZ * CY
        for j in range(CY):
            turn = (half - 3 - SLOTS * j) % X
            v = top[j] if j < hj else low[j - hj]
            v = v + jnp.where(spill, pltpu.roll(one, turn, 1), 0.0)
            v = v + jnp.where(spill2, pltpu.roll(two, (turn + half) % X, 1), 0.0)
            flip[pl.ds(base + j, CZ, stride=CY), :] = v
        oc_ref[:, t * X:(t + 1) * X] = flip[base:base + CZ * CY, :]
    comm.finish()


def put(*refs):
    sems = refs[6]
    give = [pltpu.make_async_copy(refs[m], refs[3 + m], sems.at[m]) for m in range(3)]
    for copy in give:
        copy.start()
    for copy in give:
        copy.wait()


def body(nx, ny, *args):
    Z, Y, X = args[0].shape
    CZ, CY = Z // 2, Y // 2
    flat = [v.reshape(Z * Y, X) for v in args]
    f32 = jnp.float32

    def vm(*shape):
        return pltpu.VMEM(shape, f32)

    block, square, groups = (Y, Z, X), (Y * Z // X, X, X), Y * Z // X
    assert Y * SLOTS <= X and CY * SLOTS <= X // 2 and X % Z == 0 and Y * Z % X == 0 and X % 8 == 0
    nsx, nsy = len(strides_of(X)), len(strides_of(Y))
    assert nx > 1 and ny > 1
    dma = pltpu.SemaphoreType.DMA
    scratch = (
        [vm(*block) for _ in range(12)]
        + [vm(*square) for _ in range(6)] + [vm(nsx, 2, *square), vm(*block), vm(*block), vm(*block), vm(nsy, 2, *block)]
        + [vm(Z, X), vm(3, Z, X), vm(Z, X), vm(3, Z, X)]
        + [vm(nx, XC + 1, groups, X), vm(XC + 1, groups, X), vm(nx, groups, X), vm(2, groups, X)]
        + [vm(ny, 3, Z, X), vm(3, Z, X), vm(ny, 2, Z, X), vm(ny, Z, X), vm(2, 2, Z, X)]
        + [vm(1, groups, X)] + [vm(nx, groups, X) for _ in range(8)] + [vm(4, groups, X)]
        + [vm(ny, Z, X) for _ in range(6)] + [vm(6, Z, X), vm(2, Z, X)]
        + [vm(3, (CY + 4) * Z, X), pltpu.VMEM((4 * X, X), jnp.bfloat16), vm(2, CY, CZ, X), vm(3, 2, CY + 5, CZ, X),
           vm(CY + 4, 8, Z, X), vm(2, 2 * EDGE + 1, Z, X), vm(2, 4 * EDGE + 1, Z, X), vm(CY + 4, CZ, X), vm(2, Z, X), vm(2, Z, X),
           vm(2, CZ, X), vm(CZ, X), vm(CY // 2 + 1, CZ, X), vm(nx, CY // 2 + 1, CZ, X), vm((nx // 2 + 1) * CZ * CY, X)]
        + [dma((3,)), dma((2,)), dma((2,)), dma((3,)), dma((3,)), dma((1,)), dma((3,))]
        + [vm(6, Z * Y, X)]
    )
    p, r, c = pl.pallas_call(
        functools.partial(kernel, nx, ny),
        out_shape=(
            vm(Z * Y, X),
            vm(CZ * CY, X // 2),
            vm(CZ * CY, nx * X // 2),
        ),
        in_specs=[pl.BlockSpec(memory_space=pltpu.HBM)] * 6,
        out_specs=[pl.BlockSpec(memory_space=pltpu.VMEM)] * 3,
        scratch_shapes=scratch,
        compiler_params=pltpu.CompilerParams(
            collective_id=0, has_side_effects=True, vmem_limit_bytes=60000000
        ),
    )(*flat)
    p, r, c = pl.pallas_call(
        put,
        out_shape=tuple(jax.ShapeDtypeStruct(v.shape, f32) for v in (p, r, c)),
        in_specs=[pl.BlockSpec(memory_space=pltpu.VMEM)] * 3,
        out_specs=[pl.BlockSpec(memory_space=pltpu.HBM)] * 3,
        scratch_shapes=[dma((3,))],
    )(*[pltpu.with_memory_space_constraint(v, pltpu.VMEM) for v in (p, r, c)])
    return p.reshape(Z, Y, X), r.reshape(CZ, CY, X // 2), c.reshape(CZ, CY, nx * X // 2)


def solution(mesh):
    nx, ny = mesh.shape["gx"], mesh.shape["gy"]
    split = P(None, "gy", "gx")
    return jax.shard_map(
        functools.partial(body, nx, ny),
        mesh=mesh,
        in_specs=(split,) * 6,
        out_specs=(split, split, P(None, "gy", None)),
        check_vma=False,
    )
```

time: 35.9 us -> 28.2 us (0.79)
  Pallas kernels: 35.1 us -> 27.4 us
    pallas_call x1, Pallas kernels: 34.4 us -> 26.7 us  [body(): pl.pallas_call(functools.partial(kernel, nx, ny), out_shape=(vm(Z * Y, X)...]
where the time goes in v5:
time: 28.2 us; the launch traced here: 28 us
  Pallas kernels  27.4 us (97%)
  between operations  0.64 us (2%)
    pallas_call x1, Pallas kernels, body(): pl.pallas_call(functools.partial(kernel, nx, ny), out_shape=(vm(Z * Y, X)...  26.7 us
    pallas_call x1, Pallas kernels, body(): pl.pallas_call(put, out_shape=tuple((jax.ShapeDtypeStruct(v.shape, f32) f...  0.71 us

profile of v5, /device:TPU:0, one launch (start us, length us, event | category | flops | bytes accessed | tf_op | source)
XLA Modules:
  0.0 28.0 jit_solution(13031761662933245603)
XLA Ops:
  0.6 26.7 %shard_map.85 = (f32[256,128]{1,0:T(8,128)S(1)}, f32[64,64]{1,0:T(8,128)S(1)}, f32[64,256]{1,0:T(8,128)S(1)}) custom-call(f32[256,128]{1,0:T(8,128)} %bitcast.9, f32[256,128]{1,0:T(8,128)} %bitcast.10, f32[256,128]{1,0:T(8,128)} %bitcast.11, f32[256,128]{1,0:T(8,128)} %bitcast.12, f32[256,128]{1,0:T(8,128)} %bitcast.13, f32[256,128]{1,0:T(8,128)} %bitcast.14), custom_call_target="tpu_custom_call" | custom-call | tf_op jit(solution)/shard_map/pallas_call | solution.py:827
  27.3 0.7 %shard_map.86 = (f32[256,128]{1,0:T(8,128)}, f32[64,64]{1,0:T(8,128)}, f32[64,256]{1,0:T(8,128)}) custom-call(f32[256,128]{1,0:T(8,128)S(1)} %get-tuple-element.9.refs_0_, f32[64,64]{1,0:T(8,128)S(1)} %get-tuple-element.10.refs_1_, f32[64,256]{1,0:T(8,128)S(1)} %get-tuple-element.11.refs_2_), custom_call_target="tpu_custom_call" | custom-call | tf_op jit(solution)/shard_map/pallas_call | solution.py:841

commit v6 on v4

--- a/solution.py
+++ b/solution.py
@@ -65,6 +65,12 @@
         copy.wait_recv()
     else:
         pl.when(cond)(copy.wait_recv)
+
+
+def await_sides(buf, recv, dev, one, two):
+    both = jnp.logical_and(one, two)
+    pl.when(both)(lambda: await_all(buf, recv, dev))
+    pl.when(jnp.logical_and(jnp.logical_or(one, two), jnp.logical_not(both)))(lambda: await_all(buf.at[0], recv, dev))
 
 
 def await_all(part, recv, dev):
@@ -172,14 +178,14 @@
     kk[0], kk[1], kk[2], kk[3] = b * inv, o1 * inv, a * inv, o2 * inv
 
 
-def kernel(nx, ny, f_hbm, p_hbm, x_hbm, y_hbm, z_hbm, d_hbm, op_ref, or_ref, oc_ref,
+def work(nx, ny, f_hbm, p_hbm, x_hbm, y_hbm, z_hbm, d_hbm, op_ref, or_ref, oc_ref,
            xl_s, xc_s, yl_s, yc_s, zl_s, zt_s, zd_s, fo_s, p_s, r_s, g_s, q_s,
            ct_s, rt_s, gt_s, lx_s, rx_s, ix_s, wx_s, ly_s, ry_s, iy_s, wy_s,
-           sx0, sy0, hx, hyd, hyu, xb, sxb, xb1, sx1, ycb, syc, yb0, yb1, shy,
+           sx0, sy0, hx, hy, xb, sxb, xb1, sx1, ycb, syc, yb0, yb1, shy,
            xown, xrho, xtau, xsig, xbet, xtau2, xsig2, xscl, xdlt, xkk,
            ytau, ysig, ybet, ytau2, ysig2, ydlt, ykk, ysc,
            pair_s, sel_s, cown, cbuf, wbuf, elr, nbr, pbuf, sxt, xtr, ebuf, sedge, fown, fbuf, flip,
-           ssem, s0, sx, sy, sc, sr, sw, sf, ins, sin):
+           ins, ssem, s0, sx, sy, sc, sr, sw, sin):
     Y, Z, X = xc_s.shape
     CY, CZ = Y // 2, Z // 2
     f32 = jnp.float32
@@ -211,12 +217,6 @@
     for dev in x_peers + y_peers:
         greet(dev)
 
-    corners = [
-        (jnp.logical_and(h, v), (i, j)) for h, i in ((has_w, west), (has_e, east)) for v, j in ((has_n, north), (has_s, south))
-    ]
-    for cond, dev in corners:
-        pl.when(cond)(functools.partial(greet, dev))
-
     lane = lax.broadcasted_iota(jnp.int32, (Z, X), 1)
     level = lax.broadcasted_iota(jnp.int32, (Z, X), 0)
     lane3 = lax.broadcasted_iota(jnp.int32, (1, 1, X), 2)
@@ -229,12 +229,11 @@
     sy0[1] = rows(p_ref, Y - 1)
     sy0[2] = rows(p_ref, 0)
 
-    n_corners = sum(cond.astype(jnp.int32) for cond, _ in corners)
-    pl.semaphore_wait(barrier, (nx - 1) + (ny - 1) + n_corners)
+    pl.semaphore_wait(barrier, (nx - 1) + (ny - 1))
 
     comm = Comm(ssem)
-    comm.send(sy0.at[0:2], hyd, s0.at[1], (gx, south), has_s)
-    comm.send(sy0.at[2:3], hyu, s0.at[2], (gx, north), has_n)
+    comm.send(sy0.at[0:2], hy.at[0:2], s0.at[1], (gx, south), has_s)
+    comm.send(sy0.at[2:3], hy.at[2:3], s0.at[1], (gx, north), has_n)
 
     loaded(1)
     packed = jnp.zeros((Z, X), f32)
@@ -258,11 +257,6 @@
         fo_s[j] = rows(f_ref, j)
 
     to_sides = (((gx, south), has_s, has_n), ((gx, north), has_n, has_s))
-    for n, (dev, there, _) in enumerate(to_sides):
-        for k, ref in enumerate((xc_s, zt_s)):
-            src = ref.at[pl.ds(0 if n else Y - EDGE, EDGE)]
-            comm.send(src, nbr.at[n, pl.ds(k * EDGE, EDGE)], sw.at[0, n], dev, there)
-
     per, groups, blocks = X // Z, Y * Z // X, X // 8
     sub = lax.broadcasted_iota(jnp.int32, (8, X), 0)
 
@@ -362,7 +356,7 @@
 
     @pl.when(jnp.logical_not(has_n))
     def _():
-        hyd[...] = jnp.zeros_like(hyd)
+        hy[0:2] = jnp.zeros_like(hy[0:2])
         nbr[0] = jnp.zeros_like(nbr[0])
         pbuf[0:2] = jnp.zeros_like(pbuf[0:2])
         xtr[0] = jnp.zeros_like(xtr[0])
@@ -371,25 +365,32 @@
 
     @pl.when(jnp.logical_not(has_s))
     def _():
-        hyu[...] = jnp.zeros_like(hyu)
+        hy[2] = jnp.zeros_like(hy[2])
         nbr[1] = jnp.zeros_like(nbr[1])
         pbuf[CY + 2:] = jnp.zeros_like(pbuf[CY + 2:])
         xtr[1] = jnp.zeros_like(xtr[1])
         for d in range(3):
             cbuf[d, :, 3 + CY:] = jnp.zeros_like(cbuf[d, :, 3 + CY:])
 
-    await_recv(sy0.at[0:2], hyd, ssem, s0.at[1], (gx, south), has_n)
-    await_recv(sy0.at[2:3], hyu, ssem, s0.at[2], (gx, north), has_s)
-
-    yl_s[0] = hyd[0]
+    for n, u in ((True, True), (True, False), (False, True)):
+        cond = jnp.logical_and(has_n if n else jnp.logical_not(has_n), has_s if u else jnp.logical_not(has_s))
+        part = hy.at[pl.ds(0, (2 if n else 0) + (1 if u else 0))]
+        await_recv(part, part, ssem, s0.at[1], (gx, north), cond)
+
+    yl_s[0] = hy[0]
     x_factor(0)
-    x_source(0, 1, hyd[1:2], p_s[1:2])
-    x_source(Y - 1, Y, p_s[Y - 2:Y - 1], hyu[0:1])
+    x_source(0, 1, hy[1:2], p_s[1:2])
+    x_source(Y - 1, Y, p_s[Y - 2:Y - 1], hy[2:3])
     for g in range(groups):
         one = slice(g, g + 1)
         sxb[GS, one], sxb[GE, one] = edge_sums(g)
     xb[gx] = sxb[...]
     comm.send_all(lambda dev: sxb, xb.at[gx], sx.at[0], x_peers, xb.at[pl.ds(0, nx - 1)])
+
+    for n, (dev, there, _) in enumerate(to_sides):
+        for k, ref in enumerate((xc_s, zt_s)):
+            src = ref.at[pl.ds(0 if n else Y - EDGE, EDGE)]
+            comm.send(src, nbr.at[n, pl.ds(k * EDGE, EDGE)], sw.at[0], dev, there)
 
     await_recv(sx0, hx, ssem, s0.at[0], (east, gy), has_w)
     for j in range(Y):
@@ -514,11 +515,10 @@
 
     def edge_columns():
         for n, (dev, there, _) in enumerate(to_sides):
-            comm.send(elr.at[n], nbr.at[n, pl.ds(2 * EDGE, 2 * EDGE + 1)], sw.at[0, n], dev, there)
+            comm.send(elr.at[n], nbr.at[n, pl.ds(2 * EDGE, 2 * EDGE + 1)], sw.at[0], dev, there)
 
     def edge_operators():
-        for n, (dev, _, here) in enumerate(to_sides):
-            await_recv(nbr.at[n], nbr.at[n], ssem, sw.at[0, n], dev, here)
+        await_sides(nbr, sw.at[0], (gx, north), has_n, has_s)
         for n, first in enumerate((Y - EDGE, 0)):
             for k in range(0, EDGE, 2):
                 xc = [nbr[n, k + i] for i in range(2)]
@@ -528,14 +528,9 @@
                 operator(n * (CY + 2) + k // 2, xc, xl, [pltpu.roll(v, 1, 0) for v in zt], zt,
                          [[nbr[n, (2 + m) * EDGE + k + i] for i in range(2)] for m in range(2)])
 
-    def to_rows(buf, sems, starting):
-        for n, (dev, there, here) in enumerate((((gx, north), has_n, has_s), ((gx, south), has_s, has_n))):
-            src = buf.at[pl.ds(2 if n == 0 else CY, 2)]
-            dst = buf.at[pl.ds(CY + 2 if n == 0 else 0, 2)]
-            if starting:
-                comm.send(src, dst, sems.at[n], dev, there)
-            else:
-                await_recv(src, dst, ssem, sems.at[n], dev, here)
+    def edge_rows():
+        for dev, there, src, dst in (((gx, north), has_n, 2, CY + 2), ((gx, south), has_s, CY, 0)):
+            comm.send(pbuf.at[pl.ds(src, 2)], pbuf.at[pl.ds(dst, 2)], sw.at[2], dev, there)
 
     def coarse_send(straight):
         for i, ok, back in ((west, has_w, 2), (gx, None, 1), (east, has_e, 0)):
@@ -626,8 +621,8 @@
             )
         if m:
             sxt[0], sxt[1] = end, top
-            comm.send(sxt.at[0], xtr.at[1], sw.at[1, 0], (gx, north), has_n)
-            comm.send(sxt.at[1], xtr.at[0], sw.at[1, 1], (gx, south), has_s)
+            comm.send(sxt.at[0], xtr.at[1], sw.at[1], (gx, north), has_n)
+            comm.send(sxt.at[1], xtr.at[0], sw.at[1], (gx, south), has_s)
         y_local()
         if m == 0:
             coarse_send(True)
@@ -652,14 +647,14 @@
                 pairs(1, lambda j: xl_s[j] * r_s[j]),
                 pairs(2, lambda j: zl_s[j] * pltpu.roll(r_s[j], 1, 0) + zt_s[j] * pltpu.roll(r_s[j], Z - 1, 0)),
             ], 0).reshape(CY, CZ, X)
-            to_rows(pbuf, sw.at[2], True)
+            edge_rows()
+            comm.finish()
             coarse_wait()
             coefs = planes()
             edge_operators()
         await_all(yb1.at[pl.ds(0, ny - 1)], sy.at[1], y_peers[0])
         above, below = interface_solve(ny, gy, lambda d: yb1[d], lambda d: yb1[d], top, end, ytau, ytau2, ykk)
-        await_recv(sxt.at[0], xtr.at[1], ssem, sw.at[1, 0], (gx, north), has_s)
-        await_recv(sxt.at[1], xtr.at[0], ssem, sw.at[1, 1], (gx, south), has_n)
+        await_sides(xtr, sw.at[1], (gx, north), has_n, has_s)
         alpha, gamma = jnp.zeros((Z, X), f32), jnp.zeros((Z, X), f32)
         for d in range(ny - 2):
             alpha = jnp.where(d < gy - 1, yb1[d] + ytau[d] * alpha, alpha)
@@ -720,7 +715,7 @@
         a1, b1, a2, b2 = pltpu.roll(a, 1, 0), pltpu.roll(b, 1, 0), pltpu.roll(a, Z - 1, 0), pltpu.roll(b, Z - 1, 0)
         sides[2].append(w[4] * a1 + w[5] * b1 + w[6] * a2 + w[7] * b2)
     partial = gathered([level_pairs(n, v) for n, v in enumerate(sides)], 0).reshape(H, CZ, X)
-    to_rows(pbuf, sw.at[2], False)
+    await_sides(pbuf.at[pl.ds(0, 4)].reshape(2, 2, CZ, X), sw.at[2], (gx, north), has_n, has_s)
     res = jnp.where(inside, partial + pbuf[...], 0.0)
     clane = lax.broadcasted_iota(jnp.int32, (CZ, X), 1)
     inner = clane % half
@@ -731,9 +726,6 @@
             edge = jnp.where(inner >= SLOTS * r, pltpu.roll(v[r], half - off + 3 + SLOTS * r, 1), edge)
         return edge
 
-    sedge[...] = fringe(res[2:CY + 2])
-    comm.send(sedge, ebuf.at[1], sr.at[1], (west, gy), has_w)
-    comm.send(sedge, ebuf.at[0], sr.at[0], (east, gy), has_e)
     cor = scale * res
     for repeat in range(COARSE - 1):
         lo, n = 1 + repeat, H - 2 - 2 * repeat
@@ -753,20 +745,22 @@
     fown[0:hj] = jnp.where(lane3 < half, pltpu.roll(cor[:hj], X - off, 2), pltpu.roll(cor[hj:], off, 2))
     fown[hj] = fringe(cor)
     fbuf[gx] = fown[...]
-    comm.send_all(lambda dev: fown, fbuf.at[gx], sf.at[0], x_peers, fbuf.at[pl.ds(0, nx - 1)])
+    comm.send_all(lambda dev: fown, fbuf.at[gx], sx.at[0], x_peers, fbuf.at[pl.ds(0, nx - 1)])
+    sedge[...] = fringe(res[2:CY + 2])
+    comm.send(sedge, ebuf.at[1], sr.at[0], (west, gy), has_w)
+    comm.send(sedge, ebuf.at[0], sr.at[0], (east, gy), has_e)
     above, below = above * ysc[0], below * ysc[1]
     for j in range(Y):
         op_ref[pl.ds(j, Z, stride=Y), :] = g_s[j] + ly_s[j] * above + ry_s[j] * below
     comm.finish()
-    await_recv(sedge, ebuf.at[0], ssem, sr.at[0], (west, gy), has_w)
-    await_recv(sedge, ebuf.at[1], ssem, sr.at[1], (east, gy), has_e)
+    await_sides(ebuf, sr.at[0], (west, gy), has_w, has_e)
     both = jnp.where(clane < half, ebuf[0], ebuf[1])
     for r in range(CY):
         v = pltpu.roll(both, (off - 3 - SLOTS * r) % X, 1)
         v = res[2 + r] + jnp.where(jnp.logical_or(clane == off, clane == off + half - 1), v, 0.0)
         flip[pl.ds(r, CZ, stride=CY), :] = pltpu.roll(v, X - off, 1)
     or_ref[...] = flip[0:CZ * CY, :half]
-    await_all(fbuf.at[pl.ds(0, nx - 1)], sf.at[0], x_peers[0])
+    await_all(fbuf.at[pl.ds(0, nx - 1)], sx.at[0], x_peers[0])
     nothing = jnp.zeros((CZ, X), f32)
     edges = [nothing] + [fbuf[d, hj] for d in range(nx)] + [nothing]
     spill = jnp.logical_or(clane >= X - 3, jnp.logical_and(clane >= half, clane < half + 3))
@@ -788,6 +782,11 @@
     comm.finish()
 
 
+def kernel(nx, ny, *refs):
+    sems = [pltpu.SemaphoreType.DMA((n,)) for n in (14, 2, 2, 3, 3, 1, 3, 3)]
+    pl.run_scoped(functools.partial(work, nx, ny, *refs), *sems)
+
+
 def put(*refs):
     sems = refs[6]
     give = [pltpu.make_async_copy(refs[m], refs[3 + m], sems.at[m]) for m in range(3)]
@@ -814,7 +813,7 @@
     scratch = (
         [vm(*block) for _ in range(12)]
         + [vm(*square) for _ in range(6)] + [vm(nsx, 2, *square), vm(*block), vm(*block), vm(*block), vm(nsy, 2, *block)]
-        + [vm(Z, X), vm(3, Z, X), vm(Z, X), vm(2, Z, X), vm(1, Z, X)]
+        + [vm(Z, X), vm(3, Z, X), vm(Z, X), vm(3, Z, X)]
         + [vm(nx, XC + 1, groups, X), vm(XC + 1, groups, X), vm(nx, groups, X), vm(2, groups, X)]
         + [vm(ny, 3, Z, X), vm(3, Z, X), vm(ny, 2, Z, X), vm(ny, Z, X), vm(2, 2, Z, X)]
         + [vm(1, groups, X)] + [vm(nx, groups, X) for _ in range(8)] + [vm(4, groups, X)]
@@ -822,8 +821,7 @@
         + [vm(3, (CY + 4) * Z, X), pltpu.VMEM((4 * X, X), jnp.bfloat16), vm(2, CY, CZ, X), vm(3, 2, CY + 5, CZ, X),
            vm(CY + 4, 8, Z, X), vm(2, 2 * EDGE + 1, Z, X), vm(2, 4 * EDGE + 1, Z, X), vm(CY + 4, CZ, X), vm(2, Z, X), vm(2, Z, X),
            vm(2, CZ, X), vm(CZ, X), vm(CY // 2 + 1, CZ, X), vm(nx, CY // 2 + 1, CZ, X), vm((nx // 2 + 1) * CZ * CY, X)]
-        + [dma((18,)), dma((3,)), dma((2,)), dma((3,)), dma((3,)), dma((2,)), dma((3, 2)), dma((1,))]
-        + [vm(6, Z * Y, X), dma((3,))]
+        + [vm(6, Z * Y, X)]
     )
     p, r, c = pl.pallas_call(
         functools.partial(kernel, nx, ny),

time: 28.3 us -> 28 us (0.989)
    pallas_call x1, Pallas kernels: 26.8 us -> 26.5 us  [body(): pl.pallas_call(functools.partial(kernel, nx, ny), out_shape=(vm(Z * Y, X)...]
where the time goes in v6:
time: 28 us; the launch traced here: 27.9 us
  Pallas kernels  27.3 us (98%)
  between operations  0.64 us (2%)
    pallas_call x1, Pallas kernels, body(): pl.pallas_call(functools.partial(kernel, nx, ny), out_shape=(vm(Z * Y, X)...  26.5 us
    pallas_call x1, Pallas kernels, body(): pl.pallas_call(put, out_shape=tuple((jax.ShapeDtypeStruct(v.shape, f32) f...  0.71 us

profile of v6, /device:TPU:0, one launch (start us, length us, event | category | flops | bytes accessed | tf_op | source)
XLA Modules:
  0.0 27.9 jit_solution(16560528026949390602)
XLA Ops:
  0.6 26.5 %shard_map.85 = (f32[256,128]{1,0:T(8,128)S(1)}, f32[64,64]{1,0:T(8,128)S(1)}, f32[64,256]{1,0:T(8,128)S(1)}) custom-call(f32[256,128]{1,0:T(8,128)} %bitcast.9, f32[256,128]{1,0:T(8,128)} %bitcast.10, f32[256,128]{1,0:T(8,128)} %bitcast.11, f32[256,128]{1,0:T(8,128)} %bitcast.12, f32[256,128]{1,0:T(8,128)} %bitcast.13, f32[256,128]{1,0:T(8,128)} %bitcast.14), custom_call_target="tpu_custom_call" | custom-call | tf_op jit(solution)/shard_map/pallas_call | solution.py:826
  27.2 0.7 %shard_map.86 = (f32[256,128]{1,0:T(8,128)}, f32[64,64]{1,0:T(8,128)}, f32[64,256]{1,0:T(8,128)}) custom-call(f32[256,128]{1,0:T(8,128)S(1)} %get-tuple-element.9.refs_0_, f32[64,64]{1,0:T(8,128)S(1)} %get-tuple-element.10.refs_1_, f32[64,256]{1,0:T(8,128)S(1)} %get-tuple-element.11.refs_2_), custom_call_target="tpu_custom_call" | custom-call | tf_op jit(solution)/shard_map/pallas_call | solution.py:840

commit v7 on v6

--- a/solution.py
+++ b/solution.py
@@ -197,6 +197,10 @@
     x_peers = [(i, gy) for i in farthest_first(gx, nx)]
     y_peers = [(gx, j) for j in flipped(gy, ny)]
 
+    barrier = pltpu.get_barrier_semaphore()
+    for dev in y_peers + x_peers:
+        pl.semaphore_signal(barrier, inc=1, device_id=dev, device_id_type=MESH)
+
     stages = ((0, 2), (2, 3), (3, 6))
     sources = (y_hbm, p_hbm, x_hbm, z_hbm, d_hbm, f_hbm)
     for n, (lo, hi) in enumerate(stages):
@@ -208,14 +212,6 @@
         pltpu.make_async_copy(part, part, sin.at[n]).wait()
 
     y_ref, p_ref, x_ref, z_ref, d_ref, f_ref = [ins.at[m] for m in range(6)]
-
-    barrier = pltpu.get_barrier_semaphore()
-
-    def greet(dev):
-        pl.semaphore_signal(barrier, inc=1, device_id=dev, device_id_type=MESH)
-
-    for dev in x_peers + y_peers:
-        greet(dev)
 
     lane = lax.broadcasted_iota(jnp.int32, (Z, X), 1)
     level = lax.broadcasted_iota(jnp.int32, (Z, X), 0)

time: 28 us -> 28.1 us (level)
  no operation moved by 1% of the time
where the time goes in v7:
time: 28.1 us; the launch traced here: 27.9 us
  Pallas kernels  27.3 us (97%)
  between operations  0.64 us (2%)
    pallas_call x1, Pallas kernels, body(): pl.pallas_call(functools.partial(kernel, nx, ny), out_shape=(vm(Z * Y, X)...  26.6 us
    pallas_call x1, Pallas kernels, body(): pl.pallas_call(put, out_shape=tuple((jax.ShapeDtypeStruct(v.shape, f32) f...  0.71 us

profile of v7, /device:TPU:0, one launch (start us, length us, event | category | flops | bytes accessed | tf_op | source)
XLA Modules:
  0.0 27.9 jit_solution(9873266912626699631)
XLA Ops:
  0.6 26.6 %shard_map.85 = (f32[256,128]{1,0:T(8,128)S(1)}, f32[64,64]{1,0:T(8,128)S(1)}, f32[64,256]{1,0:T(8,128)S(1)}) custom-call(f32[256,128]{1,0:T(8,128)} %bitcast.9, f32[256,128]{1,0:T(8,128)} %bitcast.10, f32[256,128]{1,0:T(8,128)} %bitcast.11, f32[256,128]{1,0:T(8,128)} %bitcast.12, f32[256,128]{1,0:T(8,128)} %bitcast.13, f32[256,128]{1,0:T(8,128)} %bitcast.14), custom_call_target="tpu_custom_call" | custom-call | tf_op jit(solution)/shard_map/pallas_call | solution.py:822
  27.2 0.7 %shard_map.86 = (f32[256,128]{1,0:T(8,128)}, f32[64,64]{1,0:T(8,128)}, f32[64,256]{1,0:T(8,128)}) custom-call(f32[256,128]{1,0:T(8,128)S(1)} %get-tuple-element.9.refs_0_, f32[64,64]{1,0:T(8,128)S(1)} %get-tuple-element.10.refs_1_, f32[64,256]{1,0:T(8,128)S(1)} %get-tuple-element.11.refs_2_), custom_call_target="tpu_custom_call" | custom-call | tf_op jit(solution)/shard_map/pallas_call | solution.py:836
